TPU v7x, 256 devices: a whole 4x4x8 slice. The times are simulated.
256 devices in a mesh: tm: 32 (over y, z), space: 8 (over x, core).
Axes of the slice: x: 4, y: 4, z: 8, core: 2. Of those that a mesh axis runs over, the one named last changes fastest.
Arguments:
- inverse_factor: bfloat16 [2, 32, 4096, 4096], P(None, 'tm', 'space'), may hold values from -1.5 to 1.5, as said below
- tile_mask: int32 [32, 32], replicated, may hold values 0 or 1
- carry_rate: float32 [32, 4096, 2], P('tm', 'space'), may hold values from 0 to 1
- right_side: float32 [32, 4096, 2, 128], P('tm', 'space'), may hold values from -1.5 to 1.5
- arrow_rows: bfloat16 [32, 4096, 2, 512], P('tm', 'space'), may hold values from -0.0625 to 0.0625
- fixed_rhs: float32 [2, 512, 128], P(None, ('tm', 'space')), may hold values from -6 to 6
- tip_factor: bfloat16 [2, 512, 512], replicated, may hold values from -1 to 1, as said below
Outputs:
- solution: float32 [32, 4096, 2, 128], P('tm', 'space')
- fixed_solution: float32 [2, 512, 128], P(None, ('tm', 'space'))
Inputs may be any that keep to these rules, and one draw needn't show every extreme that they name: `tile_mask`: 1 marks a tile that may be nonzero. `inverse_factor`: only entries on or below the diagonal are read. `tip_factor`: only entries on or below the diagonal are read.
All inputs are finite; a program needn't handle non-finite values.
Results may differ from a plain program's by a relative error of at most 0.022.
Values may be sent and summed in bfloat16 or wider, within the bound.
No kernel may reach another device: no remote copies, remote signals or barrier semaphores. Data moves between devices by JAX's collectives and lax.ppermute only.
A program may use at most 320 MiB of HBM per device.

v0:
```python
import jax
import jax.numpy as jnp
from jax import lax
from jax.sharding import PartitionSpec as P

TILE = 128


def carried_in(shard, axis, join, neutral, backward):
    count = lax.axis_size(axis)
    place = lax.axis_index(axis)
    ahead = count - 1 - place if backward else place
    gathered = jax.tree.map(
        lambda a, kind: lax.all_gather(a.astype(kind), axis), shard, (jnp.bfloat16, jnp.bfloat16)
    )
    state = jax.tree.map(lambda a, e: jnp.zeros_like(a) + jnp.asarray(e, a.dtype), shard, neutral)

    def one(turn, state):
        source = count - 1 - turn if backward else turn
        return join(
            state,
            jax.tree.map(
                lambda a, own: lax.dynamic_index_in_dim(a, source, 0, False).astype(own.dtype),
                gathered,
                shard,
            ),
        )

    return lax.fori_loop(0, ahead, one, state)


def combine(earlier, latter):
    rate_new = latter[0] * earlier[0]
    rest = tuple(
        (value_l + latter[0] * value_e for value_l, value_e in zip(latter[1:], earlier[1:]))
    )
    return (rate_new,) + rest


def tile_keep(tile_table, row_start, row_total, col_total):
    tile_count = tile_table.shape[0]
    tile_ids = jnp.arange(tile_count, dtype=jnp.int32)
    row_index = row_start + jnp.arange(row_total, dtype=jnp.int32)
    col_index = jnp.arange(col_total, dtype=jnp.int32)
    row_onehot = (row_index[:, None] // TILE == tile_ids[None, :]).astype(jnp.float32)
    col_onehot = (col_index[:, None] // TILE == tile_ids[None, :]).astype(jnp.float32)
    marked = jnp.dot(jnp.dot(row_onehot, tile_table.astype(jnp.float32)), col_onehot.T)
    return (marked > 0.5) & (row_index[:, None] >= col_index[None, :])


def on_device(inverse_factor, tile_mask, carry_rate, right_side, arrow_rows, fixed_rhs, tip_factor):
    row_count = right_side.shape[1]
    node_total = inverse_factor.shape[3]
    row_start = lax.axis_index("space") * row_count
    tile_table = jnp.maximum(tile_mask, jnp.eye(tile_mask.shape[0], dtype=jnp.int32))
    weights = inverse_factor[:, 0]
    bf_zero = jnp.zeros((), jnp.bfloat16)
    rate_col = carry_rate[0][:, :, None]
    source = right_side[0]
    unit_rate = jnp.ones_like(rate_col)
    earlier_sum = carried_in(
        (rate_col, source), "tm", combine, (unit_rate, jnp.zeros_like(source)), False
    )
    forward = source + rate_col * earlier_sum[1]
    forward_b = forward.astype(jnp.bfloat16)
    row_keep = tile_keep(tile_table, row_start, row_count, node_total)
    masked_rows = jnp.where(row_keep[None], weights, bf_zero)
    block = masked_rows
    inner_rows = jnp.einsum(
        "hrn,nhk->rhk",
        block,
        lax.all_gather(forward_b, "space", axis=0, tiled=True),
        preferred_element_type=jnp.float32,
    ).astype(jnp.bfloat16)
    block = masked_rows
    scaled = lax.psum_scatter(
        jnp.einsum("hrn,rhk->nhk", block, inner_rows, preferred_element_type=jnp.float32).astype(
            jnp.bfloat16
        ),
        "space",
        scatter_dimension=0,
        tiled=True,
    ).astype(jnp.float32)
    arrow_part = arrow_rows[0]
    coupling = jnp.einsum("rhf,rhk->hfk", arrow_part, forward_b, preferred_element_type=jnp.float32)
    share_rows = fixed_rhs.shape[1]
    share_start = lax.axis_index(("tm", "space")) * share_rows
    contrib = -coupling
    own_part = lax.dynamic_slice_in_dim(contrib, share_start, share_rows, 1) + fixed_rhs
    contrib = lax.dynamic_update_slice_in_dim(contrib, own_part, share_start, 1)
    fixed_forward = lax.psum(contrib, ("tm", "space")).astype(jnp.bfloat16)
    fixed_total = tip_factor.shape[1]
    fixed_index = jnp.arange(fixed_total, dtype=jnp.int32)
    lower_tri = fixed_index[:, None] >= fixed_index[None, :]
    tip_lower = jnp.where(lower_tri[None], tip_factor, bf_zero)
    tip_inner = jnp.einsum(
        "hij,hjk->hik", tip_lower, fixed_forward, preferred_element_type=jnp.float32
    ).astype(jnp.bfloat16)
    fixed_solution = jnp.einsum(
        "hij,hik->hjk", tip_lower, tip_inner, preferred_element_type=jnp.float32
    )
    fixed_own = lax.dynamic_slice_in_dim(fixed_solution, share_start, share_rows, 1)
    fixed_b = fixed_solution.astype(jnp.bfloat16)
    carried = scaled - jnp.einsum(
        "rhf,hfk->rhk", arrow_part, fixed_b, preferred_element_type=jnp.float32
    )
    following = carried_in(
        (rate_col, rate_col * carried), "tm", combine, (unit_rate, jnp.zeros_like(carried)), True
    )
    solution = carried + following[1]
    return (solution[None], fixed_own)


def solution(mesh):
    placed = (
        P(None, "tm", "space", None),
        P(),
        P("tm", "space", None),
        P("tm", "space", None, None),
        P("tm", "space", None, None),
        P(None, ("tm", "space"), None),
        P(),
    )
    return jax.shard_map(
        on_device,
        mesh=mesh,
        in_specs=placed,
        out_specs=(P("tm", "space", None, None), P(None, ("tm", "space"), None)),
        check_vma=False,
    )
```

profile of v0, /device:TPU:32, one launch (start us, length us, event | category | flops | bytes accessed | tf_op | source)
XLA Modules:
  0.0 592.9 jit_solution(12626880782622736189)
XLA Ops:
  7.2 1.9 copy.62
  9.2 1.2 copy.34
  11.1 51.2 %all-gather = bf16[32,512,2]{1,2,0:T(2,128)(2,1)S(1)} all-gather(bf16[1,512,2]{1,2,0:T(2,128)(2,1)S(1)} %convert_element_type.103), channel_id=2, replica_groups=mesh['tm'=32,'space'=8] {'tm'}, dimensions={0}, use_global_device_ids=true | all-gather | bytes 67584 | tf_op jit(solution)/shard_map/all_gather | solution.py:14
  62.3 3.3 copy.37
  65.6 44.9 %all-gather.6.cloned.1.call-done = bf16[32,512,2,128]{3,1,2,0:T(8,128)(2,1)} async-done(((bf16[1,512,2,128]{3,1,2,0:T(8,128)(2,1)}), bf16[32,512,2,128]{3,1,2,0:T(8,128)(2,1)}) %all-gather.6.cloned.1.call-update) | async-done | bytes 8388624 | tf_op jit(solution)/shard_map/all_gather | solution.py:14
  110.7 4.4 while.26
  111.7 1.0 constant_dynamic-slice_fusion.3
  112.6 2.5 convert_add_fusion.4
  116.3 4.2 fusion
  120.5 152.8 %all-gather.8.cloned.1.call-done = bf16[4096,2,128]{0,2,1:T(8,128)(2,1)} async-done(((bf16[512,2,128]{0,2,1:T(8,128)(2,1)}), bf16[4096,2,128]{0,2,1:T(8,128)(2,1)}) %all-gather.8.cloned.1.call-update) | async-done | bytes 2097168 | tf_op jit(solution)/shard_map/all_gather | solution.py:72
  273.3 13.2 %fusion.4 = bf16[4096,2,128]{0,2,1:T(8,128)(2,1)} fusion(bf16[2,1,512,4096]{3,2,1,0:T(8,128)(2,1)} %param.11, pred[512,4096]{1,0:T(8,128)(4,1)} %fusion, bf16[4096,2,128]{0,2,1:T(8,128)(2,1)} %all-gather.8.cloned.1.call-done), kind=kOutput, calls=%fused_computation.12 | convolution fusion | flops 2157051904 | bytes 14680064 | tf_op jit(solution)/shard_map/hrn,rhk->nhk/dot_general | solution.py:77
  287.3 1.1 dynamic_update_slice.3
  288.4 79.5 %all-reduce.1 = bf16[2,512,128]{1,2,0:T(8,128)(2,1)S(1)} all-reduce(f32[2,512,128]{1,2,0:T(8,128)S(1)} %dynamic_update_slice.3), channel_id=1, replica_groups=mesh['tm'=32,'space'=8] {'tm','space'}, use_global_device_ids=true, to_apply=%region_3.4 | all-reduce | flops 131072 | bytes 786432 | tf_op jit(solution)/shard_map/psum | solution.py:91
  367.9 2.3 fusion.9
  370.2 2.1 multiply_convert_fusion
  373.0 101.6 %all-gather.10.cloned.1.call-done = bf16[16384,2,128]{0,2,1:T(8,128)(2,1)} async-done(((bf16[512,2,128]{0,2,1:T(8,128)(2,1)}), bf16[16384,2,128]{0,2,1:T(8,128)(2,1)}) %all-gather.10.cloned.1.call-update) | async-done | bytes 8388624 | tf_op jit(solution)/shard_map/all_gather | solution.py:14
  474.6 21.1 %copy.52 = bf16[16384,2,128]{2,1,0:T(2,128)(2,1)} copy(bf16[16384,2,128]{0,2,1:T(8,128)(2,1)} %all-gather.10.cloned.1.call-done) | data formatting | bytes 16777216 | tf_op jit(solution)/shard_map/while | solution.py:29
  495.8 89.2 %while.27 = (s32[]{:T(128)}, f32[512,2,128]{2,1,0:T(2,128)S(1)}, s32[]{:T(128)}, bf16[32,512,2,128]{3,2,1,0:T(2,128)(2,1)}, bf16[32,512,2,1]{2,1,3,0:T(8,128)(2,...) while((s32[]{:T(128)}, f32[512,2,128]{2,1,0:T(2,128)S(1)}, s32[]{:T(128)}, ...), condition=%wide.region_5.6_spmd, body=%wide.region_4.5_spmd.sunk | while | flops 394246 | bytes 1321107 | solution.py:29
  496.8 2.0 convert_add_fusion.5
  499.8 2.0 convert_add_fusion.5
  501.8 0.9 bitcast_convert_fusion.5
  502.8 2.0 convert_add_fusion.5
  504.8 0.9 bitcast_convert_fusion.5
  505.7 2.0 convert_add_fusion.5
  507.8 0.9 bitcast_convert_fusion.5
  508.7 2.0 convert_add_fusion.5
  510.7 0.9 bitcast_convert_fusion.5
  511.7 2.0 convert_add_fusion.5
  513.7 0.9 bitcast_convert_fusion.5
  514.7 2.0 convert_add_fusion.5
  517.6 2.0 convert_add_fusion.5
  520.6 2.0 convert_add_fusion.5
  522.6 0.9 bitcast_convert_fusion.5
  523.6 2.0 convert_add_fusion.5
  525.6 0.9 bitcast_convert_fusion.5
  526.6 2.0 convert_add_fusion.5
  528.6 0.9 bitcast_convert_fusion.5
  529.5 2.0 convert_add_fusion.5
  531.6 0.9 bitcast_convert_fusion.5
  532.5 2.0 convert_add_fusion.5
  535.5 2.0 convert_add_fusion.5
  538.5 2.0 convert_add_fusion.5
  540.5 0.9 bitcast_convert_fusion.5
  541.4 2.0 convert_add_fusion.5
  543.5 0.9 bitcast_convert_fusion.5
  544.4 2.0 convert_add_fusion.5
  546.4 0.9 bitcast_convert_fusion.5
  547.4 2.0 convert_add_fusion.5
  549.4 0.9 bitcast_convert_fusion.5
  550.4 2.0 convert_add_fusion.5
  553.3 2.0 convert_add_fusion.5
  556.3 2.0 convert_add_fusion.5
  558.3 0.9 bitcast_convert_fusion.5
  559.3 2.0 convert_add_fusion.5
  561.3 0.9 bitcast_convert_fusion.5
  562.2 2.0 convert_add_fusion.5
  565.2 2.0 convert_add_fusion.5
  568.2 2.0 convert_add_fusion.5
  571.2 2.0 convert_add_fusion.5
  574.1 2.0 convert_add_fusion.5
  577.1 2.0 convert_add_fusion.5
  580.1 2.0 convert_add_fusion.5
  583.1 2.0 convert_add_fusion.5
  585.4 1.0 copy.48
  (49 shorter events, 18.7 us)
Async XLA Ops:
  7.2 279.7 %copy-start = (bf16[1,512,2,512]{3,2,1,0:T(2,128)(2,1)S(1)}, bf16[1,512,2,512]{3,2,1,0:T(2,128)(2,1)}, u32[]{:S(2)}) copy-start(bf16[1,512,2,512]{3,2,1,0:T(2,128)(2,1)} %param.15) | copy-start | bytes 3145732
  7.2 103.4 %all-gather.6.cloned.1.call-start = ((), (), s32[]{:S(2)}) async-start(), calls=%async_computation.1 | async-start | bytes 8650752 | tf_op jit(solution)/shard_map/all_gather | solution.py:14
  9.1 264.2 %all-gather.8.cloned.1.call-start = ((), (), s32[]{:S(2)}) async-start(), calls=%async_computation.2 | async-start | bytes 2359296 | tf_op jit(solution)/shard_map/all_gather | solution.py:72
  110.7 4.7 copy-start.2
  110.7 5.6 copy-start.4
  116.2 254.0 %reduce-scatter.2.cloned.1.call-start = ((), (), s32[]{:S(2)}) async-start(), calls=%async_computation.3 | async-start | bytes 2359296 | tf_op jit(solution)/shard_map/reduce_scatter | solution.py:76
  120.5 166.1 %copy-start.3 = (f32[2,2,128]{2,1,0:T(2,128)S(1)}, f32[2,2,128]{2,1,0:T(2,128)}, u32[]{:S(2)}) copy-start(f32[2,2,128]{2,1,0:T(2,128)} %param.16) | copy-start | bytes 6148
  120.5 166.4 %copy-start.1 = (bf16[512,2,128]{0,2,1:T(8,128)(2,1)S(1)}, bf16[512,2,128]{0,2,1:T(8,128)(2,1)}, u32[]{:S(2)}) copy-start(bf16[512,2,128]{0,2,1:T(8,128)(2,1)} %fusion.19) | copy-start | bytes 786436
  286.5 188.1 %all-gather.10.cloned.1.call-start = ((), (), s32[]{:S(2)}) async-start(), calls=%async_computation.4 | async-start | bytes 8650752 | tf_op jit(solution)/shard_map/all_gather | solution.py:14
Sparse Core Ops, SparseCore 0:
  11.2 99.3 all-gather.5
  116.3 156.9 all-gather.7
  286.7 36.9 reduce-scatter.1
  372.5 102.0 all-gather.9
where the time goes:
time: 598 us; the launch traced here: 593 us
  waiting for transfers between devices  299 us (50%)
  blocking collectives  131 us (22%)
  other arithmetic  93.4 us (16%)
  local copies, waits for them, and re-layouts  32 us (5%)
  matrix products  22.2 us (4%)
  between operations  14 us (2%)
    all_gather x1, waiting for transfers between devices, on_device(): lax.all_gather(forward_b, 'space', axis=0, tiled=True)  153 us
    all_gather x2, waiting for transfers between devices, carried_in(): lax.all_gather(a.astype(kind), axis)  147 us
    psum x1, blocking collectives, on_device(): fixed_forward = lax.psum(contrib, ('tm', 'space')).astype(jnp.bfloat16)  79.5 us
    add x31, other arithmetic, combine(): value_l + latter[0] * value_e  62.8 us
    all_gather x1, blocking collectives, carried_in(): lax.all_gather(a.astype(kind), axis)  51.2 us
    convert_element_type x31, other arithmetic, one(): lax.dynamic_index_in_dim(a, source, 0, False).astype(own.dtype)  28.8 us
    while x4, local copies, waits for them, and re-layouts, carried_in(): return lax.fori_loop(0, ahead, one, state)  24.8 us
    dot_general x1, matrix products, on_device(): jnp.einsum('hrn,rhk->nhk', block, inner_rows, preferred_element_type=jnp....  13.2 us
  transfers between devices with their start and end apart: 4, of which 3 were waited for; matrix products, arithmetic and copies ran while one was open for 2% of the time, Pallas kernels for 0%

commit v1 on v0

v1 whole, which is shorter than its diff:
```python
import functools
import jax
import jax.numpy as jnp
from jax import lax
from jax.experimental import pallas as pl
from jax.experimental.pallas import tpu as pltpu
from jax.sharding import PartitionSpec as P

TILE = 128
BF = jnp.bfloat16
F32 = jnp.float32
MIB = 1 << 20
SHIFTS = (0, 1, 3, 2)


def call(kernel, outs, scratch=(), in_specs=None, vmem=32, flops=1 << 20, moved=1 << 20):
    extra = {} if in_specs is None else {"in_specs": in_specs}
    return pl.pallas_call(
        kernel,
        out_shape=outs,
        scratch_shapes=list(scratch),
        compiler_params=pltpu.CompilerParams(vmem_limit_bytes=vmem * MIB),
        cost_estimate=pl.CostEstimate(flops=flops, bytes_accessed=moved, transcendentals=0),
        **extra,
    )


def shape(dims, kind):
    return jax.ShapeDtypeStruct(dims, kind)


def pack_kernel(side_ref, rate_ref, out_ref):
    blocks, _, lanes = out_ref.shape
    count = side_ref.shape[0] // 2
    per = count // blocks
    for h in range(2):
        rows = side_ref[pl.ds(h, count, stride=2), :]
        out_ref[:, h * per : (h + 1) * per, :] = rows.reshape(blocks, per, lanes).astype(BF)
    rate = rate_ref[...]
    high = rate.astype(BF).astype(F32)
    middle = (rate - high).astype(BF).astype(F32)
    low = rate - high - middle
    terms = jnp.concatenate([high, middle, low, jnp.zeros_like(low)], axis=0)
    shared = lanes // per
    for group in range(count // lanes):
        part = terms[:, group * lanes : (group + 1) * lanes].astype(BF)
        out_ref[group * shared : (group + 1) * shared, 2 * per :, :] = jnp.broadcast_to(
            part[None], (shared,) + part.shape
        )


def forward_kernel(got_ref, out_ref, rate_ref, rows_ref, turn_ref):
    times, height, lanes = got_ref.shape
    per = (height - 8) // 2
    rows_ref[...] = got_ref[:, 2 * per :, :].astype(F32).reshape(times * 8, lanes)
    parts = []
    for h in range(2):
        terms = [rows_ref[pl.ds(2 * k + h, times, stride=8), :] for k in range(3)]
        parts.append(terms[0] + terms[1] + terms[2])
    filler = jnp.zeros((lanes - 2 * times, lanes), F32)
    turn_ref[...] = jnp.transpose(jnp.concatenate(parts + [filler], axis=0))
    place = lax.axis_index("tm")
    start = pl.multiple_of(lax.rem(place, lanes // per) * per, per)
    rate = turn_ref[pl.ds(start, per), :]
    rate_ref[...] = rate
    current = got_ref[0, : 2 * per, :].astype(F32)
    out_ref[0] = current.astype(BF)
    for t in range(1, times):
        now = jnp.concatenate(
            [
                jnp.broadcast_to(rate[:, h * times + t : h * times + t + 1], (per, lanes))
                for h in range(2)
            ],
            axis=0,
        )
        current = got_ref[t, : 2 * per, :].astype(F32) + now * current
        out_ref[t] = current.astype(BF)


def backward_kernel(got_ref, rate_ref, out_ref):
    times, height, lanes = got_ref.shape
    per = height // 2
    rate = rate_ref[...]
    following = jnp.zeros((height, lanes), F32)
    out_ref[times - 1] = following.astype(BF)
    for t in range(times - 2, -1, -1):
        now = jnp.concatenate(
            [
                jnp.broadcast_to(rate[:, h * times + t + 1 : h * times + t + 2], (per, lanes))
                for h in range(2)
            ],
            axis=0,
        )
        following = now * (got_ref[t + 1].astype(F32) + following)
        out_ref[t] = following.astype(BF)


def setting_rows(ref, h):
    blocks, height, lanes = ref.shape
    per = height // 2
    return ref[:, h * per : (h + 1) * per, :].reshape(blocks * per, lanes)


def coupling_kernel(arrow_ref, forward_ref, out_ref):
    blocks, height, lanes = out_ref.shape
    per = height // 2
    for h in range(2):
        total = lax.dot_general(
            arrow_ref[h],
            setting_rows(forward_ref, h),
            (((0,), (0,)), ((), ())),
            preferred_element_type=F32,
        )
        out_ref[:, h * per : (h + 1) * per, :] = (-total).astype(BF).reshape(blocks, per, lanes)


def sum_kernel(got_ref, rhs_ref, out_ref):
    times, height, lanes = got_ref.shape
    total = got_ref[0].astype(F32)
    for t in range(1, times):
        total = total + got_ref[t].astype(F32)
    out_ref[...] = total
    own = rhs_ref.shape[1]
    place = lax.axis_index("space") * own
    for h in range(2):
        rows = pl.ds(h * (height // 2) + place, own)
        out_ref[rows, :] = out_ref[rows, :] + rhs_ref[h]


def tip_kernel(fixed_ref, tip_ref, full_ref, own_ref, solved_ref):
    order = tip_ref.shape[1]
    row = lax.broadcasted_iota(jnp.int32, (order, order), 0)
    col = lax.broadcasted_iota(jnp.int32, (order, order), 1)
    own = own_ref.shape[1]
    place = (lax.axis_index("tm") * lax.axis_size("space") + lax.axis_index("space")) * own
    for h in range(2):
        lower = jnp.where(row >= col, tip_ref[h].astype(F32), 0.0).astype(BF)
        inner = jnp.dot(lower, setting_rows(fixed_ref, h), preferred_element_type=F32).astype(BF)
        solved = lax.dot_general(
            lower, inner, (((0,), (0,)), ((), ())), preferred_element_type=F32
        )
        solved_ref[...] = solved
        full_ref[h] = solved.astype(BF)
        own_ref[h] = solved_ref[pl.ds(place, own), :]


def factor_kernel(mask_ref, *refs):
    pieces = refs[:8]
    factor_ref, keep_ref, send_ref, held, total, sems = refs[8:]
    rows = total.shape[1]
    per = pieces[0].shape[1] // 2
    blocks = pieces[0].shape[0]
    tiles = rows // TILE
    place = lax.axis_index("space")
    chip, core = place // 2, lax.rem(place, 2)

    def index_of(e, shift):
        return 2 * lax.rem(chip + shift, 4) + (1 - core if e else core)

    sources = [index_of(e, 4 - shift) for e in range(2) for shift in SHIFTS]

    def copy(j):
        start = pl.multiple_of(sources[j] * rows, rows)
        return pltpu.make_async_copy(
            factor_ref.at[:, :, pl.ds(start, rows)], held.at[j], sems.at[j]
        )

    for j in range(8):

        @pl.when(sources[j] <= place)
        def _(j=j):
            copy(j).start()

    total[...] = jnp.zeros_like(total)
    for j in range(8):

        @pl.when(sources[j] <= place)
        def _(j=j):
            copy(j).wait()

            @pl.loop(0, tiles * tiles)
            def _(at):
                r, c = at // tiles, lax.rem(at, tiles)
                marked = mask_ref[place * tiles + r, sources[j] * tiles + c] > 0
                dead = jnp.logical_not(marked)
                if j == 0:
                    dead = jnp.logical_or(jnp.logical_and(dead, r != c), r < c)

                @pl.when(dead)
                def _():
                    rs = pl.ds(pl.multiple_of(r * TILE, TILE), TILE)
                    cs = pl.ds(pl.multiple_of(c * TILE, TILE), TILE)
                    held[j, :, rs, cs] = jnp.zeros((2, TILE, TILE), BF)

            if j == 0:
                row = lax.broadcasted_iota(jnp.int32, (TILE, TILE), 0)
                col = lax.broadcasted_iota(jnp.int32, (TILE, TILE), 1)
                for h in range(2):
                    for r in range(tiles):
                        sl = slice(r * TILE, (r + 1) * TILE)
                        block = held[0, h, sl, sl].astype(F32)
                        held[0, h, sl, sl] = jnp.where(row >= col, block, 0.0).astype(BF)
            for h in range(2):
                total[h] += jnp.dot(
                    held[j, h], setting_rows(pieces[j], h), preferred_element_type=F32
                )

    for e, out_ref in ((1, send_ref), (0, keep_ref)):
        for d, shift in enumerate(SHIFTS):
            target = index_of(e, shift)
            at = 4 * e + SHIFTS.index((4 - shift) % 4)

            @pl.when(target <= place)
            def _(at=at, d=d, out_ref=out_ref):
                for h in range(2):
                    got = lax.dot_general(
                        held[at, h],
                        total[h].astype(BF),
                        (((0,), (0,)), ((), ())),
                        preferred_element_type=F32,
                    )
                    out_ref[d, :, h * per : (h + 1) * per, :] = got.astype(BF).reshape(
                        blocks, per, TILE
                    )

            @pl.when(target > place)
            def _(d=d, out_ref=out_ref):
                out_ref[d] = jnp.zeros(out_ref.shape[1:], BF)


def add_kernel(keep_ref, got_ref, *outs):
    for d, out_ref in enumerate(outs):
        out_ref[...] = (keep_ref[d].astype(F32) + got_ref[d].astype(F32)).astype(BF)


def carried_kernel(a_ref, b_ref, c_ref, d_ref, arrow_ref, fixed_ref, carried_ref, out_ref):
    blocks, height, lanes = a_ref.shape
    per = height // 2
    for h in range(2):
        total = setting_rows(a_ref, h).astype(F32)
        for ref in (b_ref, c_ref, d_ref):
            total = total + setting_rows(ref, h).astype(F32)
        total = total - jnp.dot(arrow_ref[h], fixed_ref[h], preferred_element_type=F32)
        carried_ref[h] = total
        out_ref[:, h * per : (h + 1) * per, :] = total.astype(BF).reshape(blocks, per, lanes)


def final_kernel(carried_ref, following_ref, out_ref):
    count = carried_ref.shape[1]
    for h in range(2):
        out_ref[pl.ds(h, count, stride=2), :] = carried_ref[h] + setting_rows(
            following_ref, h
        ).astype(F32)


def on_device(inverse_factor, tile_mask, carry_rate, right_side, arrow_rows, fixed_rhs, tip_factor):
    times = lax.axis_size("tm")
    devices = lax.axis_size("space")
    _, count, _, lanes = right_side.shape
    per = count // times
    block = (times, 2 * per, lanes)
    fixed_total = tip_factor.shape[1]
    near = [(i, i + 1 - 2 * (i % 2)) for i in range(devices)]

    def along(shift):
        chips = devices // 2
        return [(i, 2 * ((i // 2 + shift) % chips) + i % 2) for i in range(devices)]

    def turned(array):
        return lax.all_to_all(array, "tm", 0, 0, tiled=True)

    arrow = jnp.transpose(arrow_rows[0], (1, 0, 2))
    packed = call(pack_kernel, shape((times, 2 * per + 8, lanes), BF))(
        right_side.reshape(2 * count, lanes), jnp.transpose(carry_rate[0])
    )
    forward, rate = call(
        forward_kernel,
        (shape(block, BF), shape((per, lanes), F32)),
        [pltpu.VMEM((8 * times, lanes), F32), pltpu.VMEM((lanes, lanes), F32)],
    )(turned(packed))
    forward_b = turned(forward)

    pieces = [forward_b] + [lax.ppermute(forward_b, "space", along(s)) for s in SHIFTS[1:]]
    coupling = call(coupling_kernel, shape((times, 2 * fixed_total // times, lanes), BF))(
        arrow, forward_b
    )
    sums = call(sum_kernel, shape((2 * fixed_total // times, lanes), F32))(
        turned(coupling), fixed_rhs
    )
    pieces = pieces + [lax.ppermute(p, "space", near) for p in pieces]
    keep, send = call(
        factor_kernel,
        (shape((4,) + block, BF), shape((4,) + block, BF)),
        [
            pltpu.VMEM((8, 2, count, count), BF),
            pltpu.VMEM((2, count, lanes), F32),
            pltpu.SemaphoreType.DMA((8,)),
        ],
        in_specs=[pl.BlockSpec(memory_space=pltpu.SMEM)]
        + [pl.BlockSpec(memory_space=pltpu.VMEM)] * 8
        + [pl.BlockSpec(memory_space=pl.ANY)],
        vmem=40,
        flops=1 << 31,
        moved=12 * MIB,
    )(tile_mask, *pieces, inverse_factor[:, 0])
    parts = call(add_kernel, (shape(block, BF),) * 4)(keep, lax.ppermute(send, "space", near))
    scaled = [parts[0]] + [lax.ppermute(p, "space", along(s)) for p, s in zip(parts[1:], SHIFTS[1:])]

    sums = sums + lax.ppermute(sums, "space", near)
    fixed = sums
    for s in SHIFTS[1:]:
        fixed = fixed + lax.ppermute(sums, "space", along(s))
    fixed_forward = turned(
        jnp.broadcast_to(fixed.astype(BF)[None], (times,) + fixed.shape)
    )
    fixed_b, fixed_own = call(
        tip_kernel,
        (shape((2, fixed_total, lanes), BF), shape(fixed_rhs.shape, F32)),
        [pltpu.VMEM((fixed_total, lanes), F32)],
    )(fixed_forward, tip_factor)

    carried, ready = call(carried_kernel, (shape((2, count, lanes), F32), shape(block, BF)))(
        *scaled, arrow, fixed_b
    )
    following = turned(call(backward_kernel, shape(block, BF))(turned(ready), rate))
    solution = call(final_kernel, shape((2 * count, lanes), F32))(carried, following)
    return (solution.reshape(right_side.shape), fixed_own)


def solution(mesh):
    placed = (
        P(None, "tm", "space", None),
        P(),
        P("tm", "space", None),
        P("tm", "space", None, None),
        P("tm", "space", None, None),
        P(None, ("tm", "space"), None),
        P(),
    )
    return jax.shard_map(
        on_device,
        mesh=mesh,
        in_specs=placed,
        out_specs=(P("tm", "space", None, None), P(None, ("tm", "space"), None)),
        check_vma=False,
    )
```

time: 598 us -> 166 us (0.28)
  waiting for transfers between devices: 299 us -> 21.9 us
  other arithmetic: 93.4 us -> 0.01 us
  blocking collectives: 131 us -> 95.6 us
  starting transfers between devices: 0.16 us -> 28.8 us
  local copies, waits for them, and re-layouts: 32 us -> 8.41 us
  matrix products: 22.2 us -> 0 us
  between operations: 14 us -> 0.74 us
  Pallas kernels: 0 us -> 10.3 us
    all_gather x3 -> x0, waiting for transfers between devices: 299 us -> none  [the longest x1 153 us: on_device(): lax.all_gather(forward_b, 'space', axis=0, tiled=True)]
    all_to_all x0 -> x5, blocking collectives: none -> 95.6 us  [turned(): return lax.all_to_all(array, 'tm', 0, 0, tiled=True)]
    psum x1 -> x0, blocking collectives: 79.5 us -> none  [on_device(): fixed_forward = lax.psum(contrib, ('tm', 'space')).astype(jnp.bfloat16)]
    add x32 -> x1, other arithmetic: 62.9 us -> 0.01 us  [on_device(): sums = sums + lax.ppermute(sums, 'space', near)]
    all_gather x1 -> x0, blocking collectives: 51.2 us -> none  [carried_in(): lax.all_gather(a.astype(kind), axis)]
    convert_element_type x33 -> x1, other arithmetic: 30.3 us -> 0.01 us  [on_device(): fixed.astype(BF)[None]]
    while x4 -> x0, local copies, waits for them, and re-layouts: 24.8 us -> none  [carried_in(): return lax.fori_loop(0, ahead, one, state)]
    ppermute x0 -> x15, starting transfers between devices: none -> 24.2 us  [the longest x3 12.3 us: on_device(): fixed = fixed + lax.ppermute(sums, 'space', along(s))]
  transfers between devices with their start and end apart: 4 -> 16, of which waited for: 3 -> 9; matrix products, arithmetic and copies ran while one was open for 2% -> 1% of each run, Pallas kernels for 0% -> 3%
where the time goes in v1:
time: 166 us
  blocking collectives  95.6 us (58%)
  starting transfers between devices  28.8 us (17%)
  waiting for transfers between devices  21.9 us (13%)
  Pallas kernels  10.3 us (6%)
  local copies, waits for them, and re-layouts  8.41 us (5%)
    all_to_all x5, blocking collectives, turned(): return lax.all_to_all(array, 'tm', 0, 0, tiled=True)  95.6 us
    ppermute x3, starting transfers between devices, on_device(): fixed = fixed + lax.ppermute(sums, 'space', along(s))  12.3 us
    ppermute x3, waiting for transfers between devices, on_device(): lax.ppermute(forward_b, 'space', along(s))  7.86 us
    unnamed x19, local copies, waits for them, and re-layouts  7.67 us
    ppermute x3, starting transfers between devices, on_device(): lax.ppermute(forward_b, 'space', along(s))  5.05 us
    ppermute x3, starting transfers between devices, on_device(): lax.ppermute(p, 'space', along(s))  4.62 us
    all_to_all x1, starting transfers between devices, turned(): return lax.all_to_all(array, 'tm', 0, 0, tiled=True)  4.56 us
    pallas_call x1, Pallas kernels, on_device(): call(factor_kernel, (shape((4,) + block, BF), shape((4,) + block, BF)), [...  3.99 us
  transfers between devices with their start and end apart: 16, of which 9 were waited for; matrix products, arithmetic and copies ran while one was open for 1% of the time, Pallas kernels for 3%

profile of v1, /device:TPU:32, one launch (start us, length us, event | category | flops | bytes accessed | tf_op | source)
XLA Modules:
  0.0 165.7 jit_solution(14513120788978727519)
XLA Ops:
  0.6 0.0 copy-start.2
  0.6 1.0 copy-done.2
  1.7 0.0 copy-start.6
  1.7 0.7 copy-done.6
  2.4 0.0 copy-start.7
  2.4 0.1 shard_map.86
  2.4 24.9 %all_to_all.30.got_ref = bf16[32,40,128]{2,1,0:T(8,128)(2,1)S(1)} all-to-all(bf16[32,40,128]{2,1,0:T(8,128)(2,1)S(1)} %shard_map.86), channel_id=1, replica_groups=mesh['tm'=32,'space'=8] {'tm'}, dimensions={0} | all-to-all | bytes 655360 | tf_op jit(solution)/shard_map/all_to_all | solution.py:270
  27.3 0.4 shard_map.87
  27.7 15.9 %all_to_all.31.refs_0_.forward_ref = bf16[32,32,128]{2,1,0:T(8,128)(2,1)S(1)} all-to-all(bf16[32,32,128]{2,1,0:T(8,128)(2,1)S(1)} %get-tuple-element.14), channel_id=1, replica_groups=mesh['tm'=32,'space'=8] {'tm'}, dimensions={0} | all-to-all | bytes 524288 | tf_op jit(solution)/shard_map/all_to_all | solution.py:270
  43.6 1.5 collective-permute-start
  45.1 1.7 %collective-permute-start.1 = (bf16[32,32,128]{2,1,0:T(8,128)(2,1)S(1)}, bf16[32,32,128]{2,1,0:T(8,128)(2,1)S(1)}, u32[]{:S(2)}, u32[]{:S(2)}) collective-permute-start(bf16[32,32,128]{2,1,0:T(8,128)(2,1)S(1)} %all_to_all.31.refs_0_.forward_ref), channel_id=1, source_target_pairs={{0,6},{1,7},{2,0},{3,1},{4,2},{5,3},{6,4},{7,5},{8,14},{9,15},{10,... | collective-permute-start | bytes 786440 | tf_op jit(solution)/shard_map/ppermute | solution.py:283
  46.9 1.8 %collective-permute-start.2 = (bf16[32,32,128]{2,1,0:T(8,128)(2,1)S(1)}, bf16[32,32,128]{2,1,0:T(8,128)(2,1)S(1)}, u32[]{:S(2)}, u32[]{:S(2)}) collective-permute-start(bf16[32,32,128]{2,1,0:T(8,128)(2,1)S(1)} %all_to_all.31.refs_0_.forward_ref), channel_id=1, source_target_pairs={{0,4},{1,5},{2,6},{3,7},{4,0},{5,1},{6,2},{7,3},{8,12},{9,13},{10,... | collective-permute-start | bytes 786440 | tf_op jit(solution)/shard_map/ppermute | solution.py:283
  48.7 0.0 collective-permute-start.3
  48.7 5.3 %collective-permute-done.refs_1_ = bf16[32,32,128]{2,1,0:T(8,128)(2,1)S(1)} collective-permute-done((bf16[32,32,128]{2,1,0:T(8,128)(2,1)S(1)}, bf16[32,32,128]{2,1,0:T(8,128)(2,1)S(1)}, u32[]{:S(2)}, u32[]{:S(2)}) %collective-permute-start) | collective-permute-done | bytes 262176 | tf_op jit(solution)/shard_map/ppermute | solution.py:283
  54.0 0.0 collective-permute-start.4
  54.0 0.0 collective-permute-done.1.refs_2_
  54.0 0.5 collective-permute-start.5
  54.5 2.5 %collective-permute-done.2.refs_3_ = bf16[32,32,128]{2,1,0:T(8,128)(2,1)S(1)} collective-permute-done((bf16[32,32,128]{2,1,0:T(8,128)(2,1)S(1)}, bf16[32,32,128]{2,1,0:T(8,128)(2,1)S(1)}, u32[]{:S(2)}, u32[]{:S(2)}) %collective-permute-start.2) | collective-permute-done | bytes 262176 | tf_op jit(solution)/shard_map/ppermute | solution.py:283
  57.1 0.0 collective-permute-start.6
  57.1 0.0 collective-permute-done.3.refs_4_
  57.1 0.0 collective-permute-done.4.refs_5_
  57.1 0.0 collective-permute-done.5.refs_6_
  57.1 1.5 collective-permute-done.6.refs_7_
  58.6 0.0 copy-start
  58.6 3.4 %copy-done = bf16[2,1,512,4096]{3,2,1,0:T(8,128)(2,1)S(1)} copy-done((bf16[2,1,512,4096]{3,2,1,0:T(8,128)(2,1)S(1)}, bf16[2,1,512,4096]{3,2,1,0:T(8,128)(2,1)}, u32[]{:S(2)}) %copy-start) | copy-done | bytes 8388632
  62.0 0.0 copy-start.5
  62.0 0.7 copy-done.5
  62.7 0.0 copy-start.1
  62.7 4.0 %shard_map.88 = (bf16[4,32,32,128]{3,2,1,0:T(8,128)(2,1)S(1)}, bf16[4,32,32,128]{3,2,1,0:T(8,128)(2,1)}) custom-call(s32[32,32]{1,0:T(8,128)S(1)} %copy-done.5, bf16[32,32,128]{2,1,0:T(8,128)(2,1)S(1)} %all_to_all.31.refs_0_.forward_ref, bf16[32,32,128]{2,1,0:T(8,128)(2,1)S(1)} %collective-permute-done.refs_1_, ...), custom_call_target="tpu_custom_call" | custom-call | flops 2147483648 | bytes 12582912 | tf_op jit(solution)/shard_map/pallas_call | solution.py:291
  66.7 1.7 %collective-permute-start.7 = (bf16[4,32,32,128]{3,2,1,0:T(8,128)(2,1)}, bf16[4,32,32,128]{3,2,1,0:T(8,128)(2,1)}, u32[]{:S(2)}, u32[]{:S(2)}) collective-permute-start(bf16[4,32,32,128]{3,2,1,0:T(8,128)(2,1)} %get-tuple-element.16), channel_id=1, source_target_pairs={{0,1},{1,0},{2,3},{3,2},{4,5},{5,4},{6,7},{7,6},{8,9},{9,8},{10,11... | collective-permute-start | bytes 3145736 | tf_op jit(solution)/shard_map/ppermute | solution.py:306
  68.4 0.0 copy-done.8
  68.4 0.2 copy.11
  68.5 0.5 shard_map.90
  69.0 17.8 %all_to_all.32.got_ref = bf16[32,32,128]{2,1,0:T(8,128)(2,1)S(1)} all-to-all(bf16[32,32,128]{2,1,0:T(8,128)(2,1)S(1)} %shard_map.90), channel_id=1, replica_groups=mesh['tm'=32,'space'=8] {'tm'}, dimensions={0} | all-to-all | bytes 524288 | tf_op jit(solution)/shard_map/all_to_all | solution.py:270
  86.8 0.0 copy-done.7
  86.9 0.1 collective-permute-start.11
  87.0 1.2 collective-permute-done.11
  88.2 4.0 %collective-permute-start.12 = (f32[32,128]{1,0:T(8,128)S(1)}, f32[32,128]{1,0:T(8,128)S(1)}, u32[]{:S(2)}, u32[]{:S(2)}) collective-permute-start(f32[32,128]{1,0:T(8,128)S(1)} %add.12), channel_id=1, source_target_pairs={{0,2},{1,3},{2,4},{3,5},{4,6},{5,7},{6,0},{7,1},{8,10},{9,11},{10,... | collective-permute-start | bytes 49160 | tf_op jit(solution)/shard_map/ppermute | solution.py:312
  92.1 6.9 %collective-permute-start.13 = (f32[32,128]{1,0:T(8,128)S(1)}, f32[32,128]{1,0:T(8,128)S(1)}, u32[]{:S(2)}, u32[]{:S(2)}) collective-permute-start(f32[32,128]{1,0:T(8,128)S(1)} %add.12), channel_id=1, source_target_pairs={{0,6},{1,7},{2,0},{3,1},{4,2},{5,3},{6,4},{7,5},{8,14},{9,15},{10,... | collective-permute-start | bytes 49160 | tf_op jit(solution)/shard_map/ppermute | solution.py:312
  99.1 1.4 collective-permute-start.14
  100.4 0.2 collective-permute-done.12
  100.7 0.0 collective-permute-done.13
  100.7 3.6 %collective-permute-done.14 = f32[32,128]{1,0:T(8,128)S(1)} collective-permute-done((f32[32,128]{1,0:T(8,128)S(1)}, f32[32,128]{1,0:T(8,128)S(1)}, u32[]{:S(2)}, u32[]{:S(2)}) %collective-permute-start.14) | collective-permute-done | bytes 16416 | tf_op jit(solution)/shard_map/ppermute | solution.py:312
  104.3 0.7 broadcast_in_dim.2
  105.1 4.6 %all-to-all-start.3 = ((bf16[32,32,128]{2,1,0:T(8,128)(2,1)}), bf16[32,32,128]{2,1,0:T(8,128)(2,1)S(1)}, u32[]{:S(2)}, u32[]{:S(2)}) async-start(bf16[32,32,128]{2,1,0:T(8,128)(2,1)} %broadcast_in_dim.2), calls=%async_computation.3 | async-start | bytes 524288 | tf_op jit(solution)/shard_map/all_to_all | solution.py:270
  109.6 0.0 collective-permute-done.7.got_ref
  109.6 2.2 %shard_map.89 = (bf16[32,32,128]{2,1,0:T(8,128)(2,1)S(1)}, bf16[32,32,128]{2,1,0:T(8,128)(2,1)}, bf16[32,32,128]{2,1,0:T(8,128)(2,1)}, bf16[32,32,128]{2,1,0:T(8,128)(2,1)}) custom-call(bf16[4,32,32,128]{3,2,1,0:T(8,128)(2,1)S(1)} %get-tuple-element.15.keep_ref, bf16[4,32,32,128]{3,2,1,0:T(8,128)(2,1)} %collective-permute-done.7.got_ref), custom_call_target="tpu_custom_call" | custom-call | flops 1048576 | bytes 1048576 | tf_op jit(solution)/shard_map/pallas_call | solution.py:306
  111.8 0.0 copy-start.3
  111.8 0.7 copy-done.3
  112.6 1.4 collective-permute-start.10
  113.9 1.4 collective-permute-start.8
  115.4 1.8 %collective-permute-start.9 = (bf16[32,32,128]{2,1,0:T(8,128)(2,1)}, bf16[32,32,128]{2,1,0:T(8,128)(2,1)S(1)}, u32[]{:S(2)}, u32[]{:S(2)}) collective-permute-start(bf16[32,32,128]{2,1,0:T(8,128)(2,1)} %get-tuple-element.19), channel_id=1, source_target_pairs={{0,6},{1,7},{2,0},{3,1},{4,2},{5,3},{6,4},{7,5},{8,14},{9,15},{10,... | collective-permute-start | bytes 786440 | tf_op jit(solution)/shard_map/ppermute | solution.py:307
  117.2 3.6 %all-to-all-done.3.fixed_ref = bf16[32,32,128]{2,1,0:T(8,128)(2,1)S(1)} async-done(((bf16[32,32,128]{2,1,0:T(8,128)(2,1)}), bf16[32,32,128]{2,1,0:T(8,128)(2,1)S(1)}, u32[]{:S(2)}, u32[]{:S(2)}) %all-to-all-start.3) | async-done | bytes 262176 | tf_op jit(solution)/shard_map/all_to_all | solution.py:270
  120.8 0.0 copy-done.1
  120.8 1.6 shard_map.92
  122.4 1.1 collective-permute-done.10.d_ref
  123.5 2.8 %collective-permute-done.8.b_ref = bf16[32,32,128]{2,1,0:T(8,128)(2,1)S(1)} collective-permute-done((bf16[32,32,128]{2,1,0:T(8,128)(2,1)}, bf16[32,32,128]{2,1,0:T(8,128)(2,1)S(1)}, u32[]{:S(2)}, u32[]{:S(2)}) %collective-permute-start.8) | collective-permute-done | bytes 262176 | tf_op jit(solution)/shard_map/ppermute | solution.py:307
  126.2 0.0 collective-permute-done.9.c_ref
  126.2 0.9 copy-done.4
  127.2 0.4 shard_map.93
  127.6 21.5 %all_to_all.33.got_ref = bf16[32,32,128]{2,1,0:T(8,128)(2,1)S(1)} all-to-all(bf16[32,32,128]{2,1,0:T(8,128)(2,1)S(1)} %get-tuple-element.23), channel_id=1, replica_groups=mesh['tm'=32,'space'=8] {'tm'}, dimensions={0} | all-to-all | bytes 524288 | tf_op jit(solution)/shard_map/all_to_all | solution.py:270
  149.1 0.3 shard_map.94
  149.4 15.5 %all_to_all.34.following_ref = bf16[32,32,128]{2,1,0:T(8,128)(2,1)S(1)} all-to-all(bf16[32,32,128]{2,1,0:T(8,128)(2,1)S(1)} %shard_map.94), channel_id=1, replica_groups=mesh['tm'=32,'space'=8] {'tm'}, dimensions={0} | all-to-all | bytes 524288 | tf_op jit(solution)/shard_map/all_to_all | solution.py:270
  164.9 0.8 shard_map.95
  (5 shorter events, 0.1 us)
Async XLA Ops:
  0.6 1.0 copy-start.2
  1.7 0.7 copy-start.6
  2.4 66.0 %copy-start.8 = (bf16[1,512,2,512]{3,2,1,0:T(2,128)(2,1)S(1)}, bf16[1,512,2,512]{3,2,1,0:T(2,128)(2,1)}, u32[]{:S(2)}) copy-start(bf16[1,512,2,512]{3,2,1,0:T(2,128)(2,1)} %param.11) | copy-start | bytes 3145732
  2.4 84.5 %copy-start.7 = (f32[2,2,128]{2,1,0:T(2,128)S(1)}, f32[2,2,128]{2,1,0:T(2,128)}, u32[]{:S(2)}) copy-start(f32[2,2,128]{2,1,0:T(2,128)} %rhs_ref.1) | copy-start | bytes 6148
  43.6 10.4 %collective-permute-start = (bf16[32,32,128]{2,1,0:T(8,128)(2,1)S(1)}, bf16[32,32,128]{2,1,0:T(8,128)(2,1)S(1)}, u32[]{:S(2)}, u32[]{:S(2)}) collective-permute-start(bf16[32,32,128]{2,1,0:T(8,128)(2,1)S(1)} %all_to_all.31.refs_0_.forward_ref), channel_id=1, source_target_pairs={{0,2},{1,3},{2,4},{3,5},{4,6},{5,7},{6,0},{7,1},{8,10},{9,11},{10,... | collective-permute-start | bytes 786440 | tf_op jit(solution)/shard_map/ppermute | solution.py:283
  45.1 8.9 %collective-permute-start.1 = (bf16[32,32,128]{2,1,0:T(8,128)(2,1)S(1)}, bf16[32,32,128]{2,1,0:T(8,128)(2,1)S(1)}, u32[]{:S(2)}, u32[]{:S(2)}) collective-permute-start(bf16[32,32,128]{2,1,0:T(8,128)(2,1)S(1)} %all_to_all.31.refs_0_.forward_ref), channel_id=1, source_target_pairs={{0,6},{1,7},{2,0},{3,1},{4,2},{5,3},{6,4},{7,5},{8,14},{9,15},{10,... | collective-permute-start | bytes 786440 | tf_op jit(solution)/shard_map/ppermute | solution.py:283
  46.9 10.2 %collective-permute-start.2 = (bf16[32,32,128]{2,1,0:T(8,128)(2,1)S(1)}, bf16[32,32,128]{2,1,0:T(8,128)(2,1)S(1)}, u32[]{:S(2)}, u32[]{:S(2)}) collective-permute-start(bf16[32,32,128]{2,1,0:T(8,128)(2,1)S(1)} %all_to_all.31.refs_0_.forward_ref), channel_id=1, source_target_pairs={{0,4},{1,5},{2,6},{3,7},{4,0},{5,1},{6,2},{7,3},{8,12},{9,13},{10,... | collective-permute-start | bytes 786440 | tf_op jit(solution)/shard_map/ppermute | solution.py:283
  48.7 8.4 %collective-permute-start.3 = (bf16[32,32,128]{2,1,0:T(8,128)(2,1)S(1)}, bf16[32,32,128]{2,1,0:T(8,128)(2,1)S(1)}, u32[]{:S(2)}, u32[]{:S(2)}) collective-permute-start(bf16[32,32,128]{2,1,0:T(8,128)(2,1)S(1)} %all_to_all.31.refs_0_.forward_ref), channel_id=1, source_target_pairs={{0,1},{1,0},{2,3},{3,2},{4,5},{5,4},{6,7},{7,6},{8,9},{9,8},{10,11... | collective-permute-start | bytes 786440 | tf_op jit(solution)/shard_map/ppermute | solution.py:290
  54.0 3.0 %collective-permute-start.4 = (bf16[32,32,128]{2,1,0:T(8,128)(2,1)S(1)}, bf16[32,32,128]{2,1,0:T(8,128)(2,1)S(1)}, u32[]{:S(2)}, u32[]{:S(2)}) collective-permute-start(bf16[32,32,128]{2,1,0:T(8,128)(2,1)S(1)} %collective-permute-done.refs_1_), channel_id=1, source_target_pairs={{0,1},{1,0},{2,3},{3,2},{4,5},{5,4},{6,7},{7,6},{8,9},{9,8},{10,11... | collective-permute-start | bytes 786440 | tf_op jit(solution)/shard_map/ppermute | solution.py:290
  54.0 3.0 %collective-permute-start.5 = (bf16[32,32,128]{2,1,0:T(8,128)(2,1)S(1)}, bf16[32,32,128]{2,1,0:T(8,128)(2,1)S(1)}, u32[]{:S(2)}, u32[]{:S(2)}) collective-permute-start(bf16[32,32,128]{2,1,0:T(8,128)(2,1)S(1)} %collective-permute-done.1.refs_2_), channel_id=1, source_target_pairs={{0,1},{1,0},{2,3},{3,2},{4,5},{5,4},{6,7},{7,6},{8,9},{9,8},{10,11... | collective-permute-start | bytes 786440 | tf_op jit(solution)/shard_map/ppermute | solution.py:290
  57.1 1.5 collective-permute-start.6
  58.6 3.4 %copy-start = (bf16[2,1,512,4096]{3,2,1,0:T(8,128)(2,1)S(1)}, bf16[2,1,512,4096]{3,2,1,0:T(8,128)(2,1)}, u32[]{:S(2)}) copy-start(bf16[2,1,512,4096]{3,2,1,0:T(8,128)(2,1)} %param.7) | copy-start | bytes 25165828
  62.0 0.7 copy-start.5
  62.7 58.1 %copy-start.1 = (bf16[2,512,512]{2,1,0:T(8,128)(2,1)S(1)}, bf16[2,512,512]{2,1,0:T(8,128)(2,1)}, u32[]{:S(2)}) copy-start(bf16[2,512,512]{2,1,0:T(8,128)(2,1)} %tip_ref.1) | copy-start | bytes 3145732
  66.7 42.9 %collective-permute-start.7 = (bf16[4,32,32,128]{3,2,1,0:T(8,128)(2,1)}, bf16[4,32,32,128]{3,2,1,0:T(8,128)(2,1)}, u32[]{:S(2)}, u32[]{:S(2)}) collective-permute-start(bf16[4,32,32,128]{3,2,1,0:T(8,128)(2,1)} %get-tuple-element.16), channel_id=1, source_target_pairs={{0,1},{1,0},{2,3},{3,2},{4,5},{5,4},{6,7},{7,6},{8,9},{9,8},{10,11... | collective-permute-start | bytes 3145736 | tf_op jit(solution)/shard_map/ppermute | solution.py:306
  86.9 1.3 collective-permute-start.11
  88.2 12.5 %collective-permute-start.12 = (f32[32,128]{1,0:T(8,128)S(1)}, f32[32,128]{1,0:T(8,128)S(1)}, u32[]{:S(2)}, u32[]{:S(2)}) collective-permute-start(f32[32,128]{1,0:T(8,128)S(1)} %add.12), channel_id=1, source_target_pairs={{0,2},{1,3},{2,4},{3,5},{4,6},{5,7},{6,0},{7,1},{8,10},{9,11},{10,... | collective-permute-start | bytes 49160 | tf_op jit(solution)/shard_map/ppermute | solution.py:312
  92.1 8.6 %collective-permute-start.13 = (f32[32,128]{1,0:T(8,128)S(1)}, f32[32,128]{1,0:T(8,128)S(1)}, u32[]{:S(2)}, u32[]{:S(2)}) collective-permute-start(f32[32,128]{1,0:T(8,128)S(1)} %add.12), channel_id=1, source_target_pairs={{0,6},{1,7},{2,0},{3,1},{4,2},{5,3},{6,4},{7,5},{8,14},{9,15},{10,... | collective-permute-start | bytes 49160 | tf_op jit(solution)/shard_map/ppermute | solution.py:312
  99.1 5.2 %collective-permute-start.14 = (f32[32,128]{1,0:T(8,128)S(1)}, f32[32,128]{1,0:T(8,128)S(1)}, u32[]{:S(2)}, u32[]{:S(2)}) collective-permute-start(f32[32,128]{1,0:T(8,128)S(1)} %add.12), channel_id=1, source_target_pairs={{0,4},{1,5},{2,6},{3,7},{4,0},{5,1},{6,2},{7,3},{8,12},{9,13},{10,... | collective-permute-start | bytes 49160 | tf_op jit(solution)/shard_map/ppermute | solution.py:312
  105.1 15.7 %all-to-all-start.3 = ((bf16[32,32,128]{2,1,0:T(8,128)(2,1)}), bf16[32,32,128]{2,1,0:T(8,128)(2,1)S(1)}, u32[]{:S(2)}, u32[]{:S(2)}) async-start(bf16[32,32,128]{2,1,0:T(8,128)(2,1)} %broadcast_in_dim.2), calls=%async_computation.3 | async-start | bytes 524288 | tf_op jit(solution)/shard_map/all_to_all | solution.py:270
  111.8 0.7 copy-start.3
  112.6 10.9 %collective-permute-start.10 = (bf16[32,32,128]{2,1,0:T(8,128)(2,1)}, bf16[32,32,128]{2,1,0:T(8,128)(2,1)S(1)}, u32[]{:S(2)}, u32[]{:S(2)}) collective-permute-start(bf16[32,32,128]{2,1,0:T(8,128)(2,1)} %get-tuple-element.20), channel_id=1, source_target_pairs={{0,4},{1,5},{2,6},{3,7},{4,0},{5,1},{6,2},{7,3},{8,12},{9,13},{10,... | collective-permute-start | bytes 786440 | tf_op jit(solution)/shard_map/ppermute | solution.py:307
  113.9 12.3 %collective-permute-start.8 = (bf16[32,32,128]{2,1,0:T(8,128)(2,1)}, bf16[32,32,128]{2,1,0:T(8,128)(2,1)S(1)}, u32[]{:S(2)}, u32[]{:S(2)}) collective-permute-start(bf16[32,32,128]{2,1,0:T(8,128)(2,1)} %get-tuple-element.18), channel_id=1, source_target_pairs={{0,2},{1,3},{2,4},{3,5},{4,6},{5,7},{6,0},{7,1},{8,10},{9,11},{10,... | collective-permute-start | bytes 786440 | tf_op jit(solution)/shard_map/ppermute | solution.py:307
  115.4 10.9 %collective-permute-start.9 = (bf16[32,32,128]{2,1,0:T(8,128)(2,1)}, bf16[32,32,128]{2,1,0:T(8,128)(2,1)S(1)}, u32[]{:S(2)}, u32[]{:S(2)}) collective-permute-start(bf16[32,32,128]{2,1,0:T(8,128)(2,1)} %get-tuple-element.19), channel_id=1, source_target_pairs={{0,6},{1,7},{2,0},{3,1},{4,2},{5,3},{6,4},{7,5},{8,14},{9,15},{10,... | collective-permute-start | bytes 786440 | tf_op jit(solution)/shard_map/ppermute | solution.py:307
  126.2 1.0 copy-start.4

commit v2 on v1

--- a/solution.py
+++ b/solution.py
@@ -13,8 +13,10 @@
 SHIFTS = (0, 1, 3, 2)
 
 
-def call(kernel, outs, scratch=(), in_specs=None, vmem=32, flops=1 << 20, moved=1 << 20):
+def call(kernel, outs, scratch=(), in_specs=None, out_specs=None, vmem=6, flops=1 << 20, moved=1 << 20):
     extra = {} if in_specs is None else {"in_specs": in_specs}
+    if out_specs is not None:
+        extra["out_specs"] = out_specs
     return pl.pallas_call(
         kernel,
         out_shape=outs,
@@ -144,39 +146,47 @@
         own_ref[h] = solved_ref[pl.ds(place, own), :]
 
 
+def index_of(e, shift):
+    place = lax.axis_index("space")
+    chip, core = place // 2, lax.rem(place, 2)
+    return 2 * lax.rem(chip + shift, 4) + (1 - core if e else core)
+
+
 def factor_kernel(mask_ref, *refs):
     pieces = refs[:8]
-    factor_ref, keep_ref, send_ref, held, total, sems = refs[8:]
-    rows = total.shape[1]
-    per = pieces[0].shape[1] // 2
-    blocks = pieces[0].shape[0]
+    factor_ref, keep_ref, send_ref, held, values, total, parts, sems = refs[8:]
+    rows = held.shape[2]
     tiles = rows // TILE
     place = lax.axis_index("space")
-    chip, core = place // 2, lax.rem(place, 2)
-
-    def index_of(e, shift):
-        return 2 * lax.rem(chip + shift, 4) + (1 - core if e else core)
-
     sources = [index_of(e, 4 - shift) for e in range(2) for shift in SHIFTS]
 
-    def copy(j):
+    def copies(j):
         start = pl.multiple_of(sources[j] * rows, rows)
-        return pltpu.make_async_copy(
-            factor_ref.at[:, :, pl.ds(start, rows)], held.at[j], sems.at[j]
-        )
+        return (
+            pltpu.make_async_copy(pieces[j], values.at[j], sems.at[0, j]),
+            pltpu.make_async_copy(
+                factor_ref.at[:, :, pl.ds(start, rows)], held.at[j], sems.at[1, j]
+            ),
+        )
+
+    def copy_out(e, d):
+        out_ref = send_ref if e else keep_ref
+        return pltpu.make_async_copy(parts.at[4 * e + d], out_ref.at[d], sems.at[2, 4 * e + d])
 
     for j in range(8):
 
         @pl.when(sources[j] <= place)
         def _(j=j):
-            copy(j).start()
+            for copy in copies(j):
+                copy.start()
 
     total[...] = jnp.zeros_like(total)
     for j in range(8):
 
         @pl.when(sources[j] <= place)
         def _(j=j):
-            copy(j).wait()
+            for copy in copies(j):
+                copy.wait()
 
             @pl.loop(0, tiles * tiles)
             def _(at):
@@ -202,44 +212,64 @@
                         held[0, h, sl, sl] = jnp.where(row >= col, block, 0.0).astype(BF)
             for h in range(2):
                 total[h] += jnp.dot(
-                    held[j, h], setting_rows(pieces[j], h), preferred_element_type=F32
+                    held[j, h], setting_rows(values.at[j], h), preferred_element_type=F32
                 )
 
-    for e, out_ref in ((1, send_ref), (0, keep_ref)):
+    inner = [jnp.transpose(total[h]).astype(BF) for h in range(2)]
+    for e in (1, 0):
         for d, shift in enumerate(SHIFTS):
             target = index_of(e, shift)
             at = 4 * e + SHIFTS.index((4 - shift) % 4)
 
             @pl.when(target <= place)
-            def _(at=at, d=d, out_ref=out_ref):
+            def _(at=at, to=4 * e + d):
                 for h in range(2):
-                    got = lax.dot_general(
-                        held[at, h],
-                        total[h].astype(BF),
-                        (((0,), (0,)), ((), ())),
-                        preferred_element_type=F32,
-                    )
-                    out_ref[d, :, h * per : (h + 1) * per, :] = got.astype(BF).reshape(
-                        blocks, per, TILE
-                    )
+                    parts[to, h] = jnp.dot(
+                        inner[h], held[at, h], preferred_element_type=F32
+                    ).astype(BF)
 
             @pl.when(target > place)
-            def _(d=d, out_ref=out_ref):
-                out_ref[d] = jnp.zeros(out_ref.shape[1:], BF)
-
-
-def add_kernel(keep_ref, got_ref, *outs):
-    for d, out_ref in enumerate(outs):
-        out_ref[...] = (keep_ref[d].astype(F32) + got_ref[d].astype(F32)).astype(BF)
+            def _(to=4 * e + d):
+                parts[to] = jnp.zeros(parts.shape[1:], BF)
+
+            copy_out(e, d).start()
+    for e in (1, 0):
+        for d in range(4):
+            copy_out(e, d).wait()
+
+
+def add_kernel(keep_ref, got_ref, *refs):
+    outs = refs[:4]
+    kept, other, sems = refs[4:]
+    ins = [
+        (
+            pltpu.make_async_copy(keep_ref.at[d], kept.at[d], sems.at[0, d]),
+            pltpu.make_async_copy(got_ref.at[d], other.at[d], sems.at[1, d]),
+        )
+        for d in range(4)
+    ]
+    back = [pltpu.make_async_copy(kept.at[d], outs[d], sems.at[2, d]) for d in range(4)]
+    order = (3, 1, 2, 0)
+    for d in order:
+        for copy in ins[d]:
+            copy.start()
+    for d in order:
+        for copy in ins[d]:
+            copy.wait()
+        kept[d] = (kept[d].astype(F32) + other[d].astype(F32)).astype(BF)
+        back[d].start()
+    for d in order:
+        back[d].wait()
 
 
 def carried_kernel(a_ref, b_ref, c_ref, d_ref, arrow_ref, fixed_ref, carried_ref, out_ref):
-    blocks, height, lanes = a_ref.shape
+    blocks, height, lanes = out_ref.shape
     per = height // 2
     for h in range(2):
-        total = setting_rows(a_ref, h).astype(F32)
+        total = a_ref[h].astype(F32)
         for ref in (b_ref, c_ref, d_ref):
-            total = total + setting_rows(ref, h).astype(F32)
+            total = total + ref[h].astype(F32)
+        total = jnp.transpose(total)
         total = total - jnp.dot(arrow_ref[h], fixed_ref[h], preferred_element_type=F32)
         carried_ref[h] = total
         out_ref[:, h * per : (h + 1) * per, :] = total.astype(BF).reshape(blocks, per, lanes)
@@ -269,6 +299,9 @@
     def turned(array):
         return lax.all_to_all(array, "tm", 0, 0, tiled=True)
 
+    def distant(array):
+        return pltpu.with_memory_space_constraint(array, pltpu.HBM)
+
     arrow = jnp.transpose(arrow_rows[0], (1, 0, 2))
     packed = call(pack_kernel, shape((times, 2 * per + 8, lanes), BF))(
         right_side.reshape(2 * count, lanes), jnp.transpose(carry_rate[0])
@@ -280,6 +313,7 @@
     )(turned(packed))
     forward_b = turned(forward)
 
+    far = pl.BlockSpec(memory_space=pltpu.HBM)
     pieces = [forward_b] + [lax.ppermute(forward_b, "space", along(s)) for s in SHIFTS[1:]]
     coupling = call(coupling_kernel, shape((times, 2 * fixed_total // times, lanes), BF))(
         arrow, forward_b
@@ -288,31 +322,42 @@
         turned(coupling), fixed_rhs
     )
     pieces = pieces + [lax.ppermute(p, "space", near) for p in pieces]
+    pieces, sums = lax.optimization_barrier((pieces, sums))
+    part = (2, lanes, count)
     keep, send = call(
         factor_kernel,
-        (shape((4,) + block, BF), shape((4,) + block, BF)),
+        (shape((4,) + part, BF), shape((4,) + part, BF)),
         [
             pltpu.VMEM((8, 2, count, count), BF),
+            pltpu.VMEM((8,) + block, BF),
             pltpu.VMEM((2, count, lanes), F32),
-            pltpu.SemaphoreType.DMA((8,)),
+            pltpu.VMEM((8,) + part, BF),
+            pltpu.SemaphoreType.DMA((3, 8)),
         ],
-        in_specs=[pl.BlockSpec(memory_space=pltpu.SMEM)]
-        + [pl.BlockSpec(memory_space=pltpu.VMEM)] * 8
-        + [pl.BlockSpec(memory_space=pl.ANY)],
-        vmem=40,
+        in_specs=[pl.BlockSpec(memory_space=pltpu.SMEM)] + [far] * 9,
+        out_specs=(far, far),
+        vmem=24,
         flops=1 << 31,
         moved=12 * MIB,
-    )(tile_mask, *pieces, inverse_factor[:, 0])
-    parts = call(add_kernel, (shape(block, BF),) * 4)(keep, lax.ppermute(send, "space", near))
+    )(tile_mask, *[distant(p) for p in pieces], distant(inverse_factor[:, 0]))
+    parts = call(
+        add_kernel,
+        (shape(part, BF),) * 4,
+        [
+            pltpu.VMEM((4,) + part, BF),
+            pltpu.VMEM((4,) + part, BF),
+            pltpu.SemaphoreType.DMA((3, 4)),
+        ],
+        in_specs=[far, far],
+        out_specs=(far,) * 4,
+    )(distant(keep), distant(lax.ppermute(send, "space", near)))
     scaled = [parts[0]] + [lax.ppermute(p, "space", along(s)) for p, s in zip(parts[1:], SHIFTS[1:])]
 
     sums = sums + lax.ppermute(sums, "space", near)
     fixed = sums
     for s in SHIFTS[1:]:
         fixed = fixed + lax.ppermute(sums, "space", along(s))
-    fixed_forward = turned(
-        jnp.broadcast_to(fixed.astype(BF)[None], (times,) + fixed.shape)
-    )
+    fixed_forward = turned(jnp.broadcast_to(fixed.astype(BF)[None], (times,) + fixed.shape))
     fixed_b, fixed_own = call(
         tip_kernel,
         (shape((2, fixed_total, lanes), BF), shape(fixed_rhs.shape, F32)),

time: 166 us -> 149 us (0.90)
  blocking collectives: 95.6 us -> 76.6 us
  waiting for transfers between devices: 21.9 us -> 24.6 us
  local copies, waits for them, and re-layouts: 8.41 us -> 6.25 us
    all_to_all x5 -> x4, blocking collectives: 95.6 us -> 76.6 us  [turned(): return lax.all_to_all(array, 'tm', 0, 0, tiled=True)]
    all_to_all x1 -> x2, waiting for transfers between devices: 3.6 us -> 15.3 us  [turned(): return lax.all_to_all(array, 'tm', 0, 0, tiled=True)]
    ppermute x3, waiting for transfers between devices: 7.86 us -> 0.43 us  [on_device(): lax.ppermute(forward_b, 'space', along(s))]
    all_to_all x1 -> x2, starting transfers between devices: 4.56 us -> 8.97 us  [turned(): return lax.all_to_all(array, 'tm', 0, 0, tiled=True)]
    ppermute x3, starting transfers between devices: 12.3 us -> 10 us  [on_device(): fixed = fixed + lax.ppermute(sums, 'space', along(s))]
    unnamed x19, local copies, waits for them, and re-layouts: 7.67 us -> 5.49 us
  transfers between devices with their start and end apart: 16 -> 17, of which waited for: 9 -> 7; matrix products, arithmetic and copies ran while one was open for 1% -> 1% of each run, Pallas kernels for 3% -> 3%
where the time goes in v2:
time: 149 us; the launch traced here: 148 us
  blocking collectives  76.6 us (51%)
  starting transfers between devices  29.1 us (20%)
  waiting for transfers between devices  24.6 us (17%)
  Pallas kernels  11.1 us (7%)
  local copies, waits for them, and re-layouts  6.25 us (4%)
    all_to_all x4, blocking collectives, turned(): return lax.all_to_all(array, 'tm', 0, 0, tiled=True)  76.6 us
    all_to_all x2, waiting for transfers between devices, turned(): return lax.all_to_all(array, 'tm', 0, 0, tiled=True)  15.3 us
    ppermute x3, starting transfers between devices, on_device(): fixed = fixed + lax.ppermute(sums, 'space', along(s))  10 us
    all_to_all x2, starting transfers between devices, turned(): return lax.all_to_all(array, 'tm', 0, 0, tiled=True)  8.97 us
    unnamed x19, local copies, waits for them, and re-layouts  5.49 us
    ppermute x3, starting transfers between devices, on_device(): lax.ppermute(forward_b, 'space', along(s))  5.05 us
    ppermute x3, waiting for transfers between devices, on_device(): fixed = fixed + lax.ppermute(sums, 'space', along(s))  4.08 us
    pallas_call x1, Pallas kernels, on_device(): call(factor_kernel, (shape((4,) + part, BF), shape((4,) + part, BF)), [pl...  3.97 us
  transfers between devices with their start and end apart: 17, of which 7 were waited for; matrix products, arithmetic and copies ran while one was open for 1% of the time, Pallas kernels for 3%

profile of v2, /device:TPU:32, one launch (start us, length us, event | category | flops | bytes accessed | tf_op | source)
XLA Modules:
  0.0 148.4 jit_solution(3949317142307209043)
XLA Ops:
  0.6 0.0 copy-start.3
  0.6 1.0 copy-done.3
  1.7 0.0 copy-start.5
  1.7 0.7 copy-done.5
  2.4 0.1 shard_map.86
  2.4 24.7 %all_to_all.30.got_ref = bf16[32,40,128]{2,1,0:T(8,128)(2,1)S(1)} all-to-all(bf16[32,40,128]{2,1,0:T(8,128)(2,1)S(1)} %shard_map.86), channel_id=1, replica_groups=mesh['tm'=32,'space'=8] {'tm'}, dimensions={0} | all-to-all | bytes 655360 | tf_op jit(solution)/shard_map/all_to_all | solution.py:300
  27.2 0.4 shard_map.87
  27.6 15.9 %all_to_all.31.forward_ref.refs_0_ = bf16[32,32,128]{2,1,0:T(8,128)(2,1)S(1)} all-to-all(bf16[32,32,128]{2,1,0:T(8,128)(2,1)S(1)} %get-tuple-element.23), channel_id=1, replica_groups=mesh['tm'=32,'space'=8] {'tm'}, dimensions={0} | all-to-all | bytes 524288 | tf_op jit(solution)/shard_map/all_to_all | solution.py:300
  43.5 3.0 %collective-permute-start.2 = (bf16[32,32,128]{2,1,0:T(8,128)(2,1)S(1)}, bf16[32,32,128]{2,1,0:T(8,128)(2,1)S(1)}, u32[]{:S(2)}, u32[]{:S(2)}) collective-permute-start(bf16[32,32,128]{2,1,0:T(8,128)(2,1)S(1)} %all_to_all.31.forward_ref.refs_0_), channel_id=1, source_target_pairs={{0,4},{1,5},{2,6},{3,7},{4,0},{5,1},{6,2},{7,3},{8,12},{9,13},{10,... | collective-permute-start | bytes 786440 | tf_op jit(solution)/shard_map/ppermute | solution.py:317
  46.5 1.1 collective-permute-start.1
  47.7 0.9 collective-permute-start
  48.6 1.4 copy.11
  49.9 0.0 copy-start.1
  50.0 1.2 shard_map.88
  51.2 4.6 %all-to-all-start.2 = ((bf16[32,32,128]{2,1,0:T(8,128)(2,1)}), bf16[32,32,128]{2,1,0:T(8,128)(2,1)S(1)}, u32[]{:S(2)}, u32[]{:S(2)}) async-start(bf16[32,32,128]{2,1,0:T(8,128)(2,1)} %shard_map.88), calls=%async_computation.2 | async-start | bytes 524288 | tf_op jit(solution)/shard_map/all_to_all | solution.py:300
  55.7 0.1 collective-permute-start.3
  55.8 0.0 collective-permute-done.2.refs_3_
  55.8 0.0 copy-start.7
  55.9 0.5 collective-permute-start.6
  56.3 0.0 collective-permute-done.1.refs_2_
  56.4 0.1 collective-permute-start.5
  56.5 0.4 collective-permute-done.refs_1_
  56.8 0.0 collective-permute-start.4
  56.9 9.9 %all-to-all-done.2.got_ref = bf16[32,32,128]{2,1,0:T(8,128)(2,1)S(1)} async-done(((bf16[32,32,128]{2,1,0:T(8,128)(2,1)}), bf16[32,32,128]{2,1,0:T(8,128)(2,1)S(1)}, u32[]{:S(2)}, u32[]{:S(2)}) %all-to-all-start.2) | async-done | bytes 262176 | tf_op jit(solution)/shard_map/all_to_all | solution.py:300
  66.8 0.7 copy-done.6
  67.5 0.0 collective-permute-done.3.refs_4_
  67.5 0.0 collective-permute-done.6.refs_7_
  67.5 0.0 collective-permute-done.5.refs_6_
  67.5 0.0 collective-permute-done.4.refs_5_
  67.5 0.0 copy-done.7
  67.6 0.0 copy-done.8
  67.6 0.0 copy-done
  67.6 0.0 copy-start.4
  67.6 0.7 copy-done.4
  68.3 4.0 %shard_map.90 = (bf16[4,2,128,512]{3,2,1,0:T(8,128)(2,1)S(1)}, bf16[4,2,128,512]{3,2,1,0:T(8,128)(2,1)S(1)}) custom-call(s32[32,32]{1,0:T(8,128)S(1)} %copy-done.4, bf16[32,32,128]{2,1,0:T(8,128)(2,1)} %copy-done, bf16[32,32,128]{2,1,0:T(8,128)(2,1)} %collective-permute-done.refs_1_, bf16[32,32,128]{2,1,0:T(8,128)(2,1)} %copy-done.8, ...), custom_call_target="tpu_custom_call" | custom-call | flops 2147483648 | bytes 12582912 | tf_op jit(solution)/shard_map/pallas_call | solution.py:327
  72.3 0.0 copy-start.2
  72.3 1.0 copy-done.2
  73.3 0.0 collective-permute-start.7
  73.3 0.5 collective-permute-start.11
  73.8 1.8 %collective-permute-done.11 = f32[32,128]{1,0:T(8,128)S(1)} collective-permute-done((f32[32,128]{1,0:T(8,128)S(1)}, f32[32,128]{1,0:T(8,128)S(1)}, u32[]{:S(2)}, u32[]{:S(2)}) %collective-permute-start.11) | collective-permute-done | bytes 16416 | tf_op jit(solution)/shard_map/ppermute | solution.py:356
  75.6 5.2 %collective-permute-start.14 = (f32[32,128]{1,0:T(8,128)S(1)}, f32[32,128]{1,0:T(8,128)S(1)}, u32[]{:S(2)}, u32[]{:S(2)}) collective-permute-start(f32[32,128]{1,0:T(8,128)S(1)} %add.12), channel_id=1, source_target_pairs={{0,4},{1,5},{2,6},{3,7},{4,0},{5,1},{6,2},{7,3},{8,12},{9,13},{10,... | collective-permute-start | bytes 49160 | tf_op jit(solution)/shard_map/ppermute | solution.py:359
  80.8 4.0 %collective-permute-start.13 = (f32[32,128]{1,0:T(8,128)S(1)}, f32[32,128]{1,0:T(8,128)S(1)}, u32[]{:S(2)}, u32[]{:S(2)}) collective-permute-start(f32[32,128]{1,0:T(8,128)S(1)} %add.12), channel_id=1, source_target_pairs={{0,6},{1,7},{2,0},{3,1},{4,2},{5,3},{6,4},{7,5},{8,14},{9,15},{10,... | collective-permute-start | bytes 49160 | tf_op jit(solution)/shard_map/ppermute | solution.py:359
  84.7 0.9 collective-permute-start.12
  85.6 0.0 collective-permute-done.14
  85.6 1.9 %collective-permute-done.13 = f32[32,128]{1,0:T(8,128)S(1)} collective-permute-done((f32[32,128]{1,0:T(8,128)S(1)}, f32[32,128]{1,0:T(8,128)S(1)}, u32[]{:S(2)}, u32[]{:S(2)}) %collective-permute-start.13) | collective-permute-done | bytes 16416 | tf_op jit(solution)/shard_map/ppermute | solution.py:359
  87.5 2.2 %collective-permute-done.12 = f32[32,128]{1,0:T(8,128)S(1)} collective-permute-done((f32[32,128]{1,0:T(8,128)S(1)}, f32[32,128]{1,0:T(8,128)S(1)}, u32[]{:S(2)}, u32[]{:S(2)}) %collective-permute-start.12) | collective-permute-done | bytes 16416 | tf_op jit(solution)/shard_map/ppermute | solution.py:359
  89.7 0.8 broadcast_in_dim.2
  90.5 4.4 %all-to-all-start.3 = ((bf16[32,32,128]{2,1,0:T(8,128)(2,1)}), bf16[32,32,128]{2,1,0:T(8,128)(2,1)S(1)}, u32[]{:S(2)}, u32[]{:S(2)}) async-start(bf16[32,32,128]{2,1,0:T(8,128)(2,1)} %broadcast_in_dim.2), calls=%async_computation.3 | async-start | bytes 524288 | tf_op jit(solution)/shard_map/all_to_all | solution.py:300
  94.9 0.0 collective-permute-done.7.got_ref
  94.9 2.2 %shard_map.91 = (bf16[2,128,512]{2,1,0:T(8,128)(2,1)S(1)}, bf16[2,128,512]{2,1,0:T(8,128)(2,1)}, bf16[2,128,512]{2,1,0:T(8,128)(2,1)}, bf16[2,128,512]{2,1,0:T(8,128)(2,1)}) custom-call(bf16[4,2,128,512]{3,2,1,0:T(8,128)(2,1)} %copy-done.2, bf16[4,2,128,512]{3,2,1,0:T(8,128)(2,1)} %collective-permute-done.7.got_ref), custom_call_target="tpu_custom_call" | custom-call | flops 1048576 | bytes 1048576 | tf_op jit(solution)/shard_map/pallas_call | solution.py:343
  97.1 0.1 collective-permute-start.8
  97.2 3.2 %collective-permute-start.9 = (bf16[2,128,512]{2,1,0:T(8,128)(2,1)}, bf16[2,128,512]{2,1,0:T(8,128)(2,1)S(1)}, u32[]{:S(2)}, u32[]{:S(2)}) collective-permute-start(bf16[2,128,512]{2,1,0:T(8,128)(2,1)} %get-tuple-element.36), channel_id=1, source_target_pairs={{0,6},{1,7},{2,0},{3,1},{4,2},{5,3},{6,4},{7,5},{8,14},{9,15},{10,... | collective-permute-start | bytes 786440 | tf_op jit(solution)/shard_map/ppermute | solution.py:354
  100.4 0.5 collective-permute-start.10
  100.9 5.4 %all-to-all-done.3.fixed_ref = bf16[32,32,128]{2,1,0:T(8,128)(2,1)S(1)} async-done(((bf16[32,32,128]{2,1,0:T(8,128)(2,1)}), bf16[32,32,128]{2,1,0:T(8,128)(2,1)S(1)}, u32[]{:S(2)}, u32[]{:S(2)}) %all-to-all-start.3) | async-done | bytes 262176 | tf_op jit(solution)/shard_map/all_to_all | solution.py:300
  106.3 0.0 copy-done.1
  106.4 1.6 %shard_map.92 = (bf16[2,512,128]{2,1,0:T(8,128)(2,1)S(1)}, f32[2,2,128]{2,1,0:T(2,128)}) custom-call(bf16[32,32,128]{2,1,0:T(8,128)(2,1)S(1)} %all-to-all-done.3.fixed_ref, bf16[2,512,512]{2,1,0:T(8,128)(2,1)S(1)} %copy-done.1), custom_call_target="tpu_custom_call" | custom-call | flops 1048576 | bytes 1048576 | tf_op jit(solution)/shard_map/pallas_call | solution.py:361
  107.9 3.0 %collective-permute-done.8.b_ref = bf16[2,128,512]{2,1,0:T(8,128)(2,1)S(1)} collective-permute-done((bf16[2,128,512]{2,1,0:T(8,128)(2,1)}, bf16[2,128,512]{2,1,0:T(8,128)(2,1)S(1)}, u32[]{:S(2)}, u32[]{:S(2)}) %collective-permute-start.8) | collective-permute-done | bytes 262176 | tf_op jit(solution)/shard_map/ppermute | solution.py:354
  110.9 0.0 collective-permute-done.9.c_ref
  110.9 0.0 collective-permute-done.10.d_ref
  110.9 0.4 shard_map.93
  111.4 20.6 %all_to_all.32.got_ref = bf16[32,32,128]{2,1,0:T(8,128)(2,1)S(1)} all-to-all(bf16[32,32,128]{2,1,0:T(8,128)(2,1)S(1)} %get-tuple-element.41), channel_id=1, replica_groups=mesh['tm'=32,'space'=8] {'tm'}, dimensions={0} | all-to-all | bytes 524288 | tf_op jit(solution)/shard_map/all_to_all | solution.py:300
  132.0 0.3 shard_map.94
  132.3 15.3 %all_to_all.33.following_ref = bf16[32,32,128]{2,1,0:T(8,128)(2,1)S(1)} all-to-all(bf16[32,32,128]{2,1,0:T(8,128)(2,1)S(1)} %shard_map.94), channel_id=1, replica_groups=mesh['tm'=32,'space'=8] {'tm'}, dimensions={0} | all-to-all | bytes 524288 | tf_op jit(solution)/shard_map/all_to_all | solution.py:300
  147.5 0.8 shard_map.95
  (6 shorter events, 0.1 us)
Async XLA Ops:
  0.6 1.0 copy-start.3
  1.7 0.7 copy-start.5
  43.5 24.1 %copy-start = (bf16[32,32,128]{2,1,0:T(8,128)(2,1)}, bf16[32,32,128]{2,1,0:T(8,128)(2,1)S(1)}, u32[]{:S(2)}) copy-start(bf16[32,32,128]{2,1,0:T(8,128)(2,1)S(1)} %all_to_all.31.forward_ref.refs_0_) | copy-start | bytes 786436
  43.5 12.3 %collective-permute-start.2 = (bf16[32,32,128]{2,1,0:T(8,128)(2,1)S(1)}, bf16[32,32,128]{2,1,0:T(8,128)(2,1)S(1)}, u32[]{:S(2)}, u32[]{:S(2)}) collective-permute-start(bf16[32,32,128]{2,1,0:T(8,128)(2,1)S(1)} %all_to_all.31.forward_ref.refs_0_), channel_id=1, source_target_pairs={{0,4},{1,5},{2,6},{3,7},{4,0},{5,1},{6,2},{7,3},{8,12},{9,13},{10,... | collective-permute-start | bytes 786440 | tf_op jit(solution)/shard_map/ppermute | solution.py:317
  46.5 9.8 %collective-permute-start.1 = (bf16[32,32,128]{2,1,0:T(8,128)(2,1)S(1)}, bf16[32,32,128]{2,1,0:T(8,128)(2,1)S(1)}, u32[]{:S(2)}, u32[]{:S(2)}) collective-permute-start(bf16[32,32,128]{2,1,0:T(8,128)(2,1)S(1)} %all_to_all.31.forward_ref.refs_0_), channel_id=1, source_target_pairs={{0,6},{1,7},{2,0},{3,1},{4,2},{5,3},{6,4},{7,5},{8,14},{9,15},{10,... | collective-permute-start | bytes 786440 | tf_op jit(solution)/shard_map/ppermute | solution.py:317
  47.7 9.2 %collective-permute-start = (bf16[32,32,128]{2,1,0:T(8,128)(2,1)S(1)}, bf16[32,32,128]{2,1,0:T(8,128)(2,1)}, u32[]{:S(2)}, u32[]{:S(2)}) collective-permute-start(bf16[32,32,128]{2,1,0:T(8,128)(2,1)S(1)} %all_to_all.31.forward_ref.refs_0_), channel_id=1, source_target_pairs={{0,2},{1,3},{2,4},{3,5},{4,6},{5,7},{6,0},{7,1},{8,10},{9,11},{10,... | collective-permute-start | bytes 786440 | tf_op jit(solution)/shard_map/ppermute | solution.py:317
  49.9 56.4 %copy-start.1 = (bf16[2,512,512]{2,1,0:T(8,128)(2,1)S(1)}, bf16[2,512,512]{2,1,0:T(8,128)(2,1)}, u32[]{:S(2)}) copy-start(bf16[2,512,512]{2,1,0:T(8,128)(2,1)} %tip_ref.1) | copy-start | bytes 3145732
  51.2 15.6 %all-to-all-start.2 = ((bf16[32,32,128]{2,1,0:T(8,128)(2,1)}), bf16[32,32,128]{2,1,0:T(8,128)(2,1)S(1)}, u32[]{:S(2)}, u32[]{:S(2)}) async-start(bf16[32,32,128]{2,1,0:T(8,128)(2,1)} %shard_map.88), calls=%async_computation.2 | async-start | bytes 524288 | tf_op jit(solution)/shard_map/all_to_all | solution.py:300
  55.7 11.8 %collective-permute-start.3 = (bf16[32,32,128]{2,1,0:T(8,128)(2,1)S(1)}, bf16[32,32,128]{2,1,0:T(8,128)(2,1)}, u32[]{:S(2)}, u32[]{:S(2)}) collective-permute-start(bf16[32,32,128]{2,1,0:T(8,128)(2,1)S(1)} %all_to_all.31.forward_ref.refs_0_), channel_id=1, source_target_pairs={{0,1},{1,0},{2,3},{3,2},{4,5},{5,4},{6,7},{7,6},{8,9},{9,8},{10,11... | collective-permute-start | bytes 786440 | tf_op jit(solution)/shard_map/ppermute | solution.py:324
  55.8 11.7 %copy-start.7 = (bf16[32,32,128]{2,1,0:T(8,128)(2,1)}, bf16[32,32,128]{2,1,0:T(8,128)(2,1)S(1)}, u32[]{:S(2)}) copy-start(bf16[32,32,128]{2,1,0:T(8,128)(2,1)S(1)} %collective-permute-done.2.refs_3_) | copy-start | bytes 786436
  55.9 11.7 %collective-permute-start.6 = (bf16[32,32,128]{2,1,0:T(8,128)(2,1)S(1)}, bf16[32,32,128]{2,1,0:T(8,128)(2,1)}, u32[]{:S(2)}, u32[]{:S(2)}) collective-permute-start(bf16[32,32,128]{2,1,0:T(8,128)(2,1)S(1)} %collective-permute-done.2.refs_3_), channel_id=1, source_target_pairs={{0,1},{1,0},{2,3},{3,2},{4,5},{5,4},{6,7},{7,6},{8,9},{9,8},{10,11... | collective-permute-start | bytes 786440 | tf_op jit(solution)/shard_map/ppermute | solution.py:324
  56.4 11.2 %copy-start.8 = (bf16[32,32,128]{2,1,0:T(8,128)(2,1)}, bf16[32,32,128]{2,1,0:T(8,128)(2,1)S(1)}, u32[]{:S(2)}) copy-start(bf16[32,32,128]{2,1,0:T(8,128)(2,1)S(1)} %collective-permute-done.1.refs_2_) | copy-start | bytes 786436
  56.4 11.2 %collective-permute-start.5 = (bf16[32,32,128]{2,1,0:T(8,128)(2,1)S(1)}, bf16[32,32,128]{2,1,0:T(8,128)(2,1)}, u32[]{:S(2)}, u32[]{:S(2)}) collective-permute-start(bf16[32,32,128]{2,1,0:T(8,128)(2,1)S(1)} %collective-permute-done.1.refs_2_), channel_id=1, source_target_pairs={{0,1},{1,0},{2,3},{3,2},{4,5},{5,4},{6,7},{7,6},{8,9},{9,8},{10,11... | collective-permute-start | bytes 786440 | tf_op jit(solution)/shard_map/ppermute | solution.py:324
  56.8 10.7 %collective-permute-start.4 = (bf16[32,32,128]{2,1,0:T(8,128)(2,1)}, bf16[32,32,128]{2,1,0:T(8,128)(2,1)}, u32[]{:S(2)}, u32[]{:S(2)}) collective-permute-start(bf16[32,32,128]{2,1,0:T(8,128)(2,1)} %collective-permute-done.refs_1_), channel_id=1, source_target_pairs={{0,1},{1,0},{2,3},{3,2},{4,5},{5,4},{6,7},{7,6},{8,9},{9,8},{10,11... | collective-permute-start | bytes 786440 | tf_op jit(solution)/shard_map/ppermute | solution.py:324
  66.8 0.7 copy-start.6
  67.6 0.7 copy-start.4
  72.3 1.0 copy-start.2
  73.3 21.6 %collective-permute-start.7 = (bf16[4,2,128,512]{3,2,1,0:T(8,128)(2,1)S(1)}, bf16[4,2,128,512]{3,2,1,0:T(8,128)(2,1)}, u32[]{:S(2)}, u32[]{:S(2)}) collective-permute-start(bf16[4,2,128,512]{3,2,1,0:T(8,128)(2,1)S(1)} %get-tuple-element.33), channel_id=1, source_target_pairs={{0,1},{1,0},{2,3},{3,2},{4,5},{5,4},{6,7},{7,6},{8,9},{9,8},{10,11... | collective-permute-start | bytes 3145736 | tf_op jit(solution)/shard_map/ppermute | solution.py:353
  73.3 2.3 %collective-permute-start.11 = (f32[32,128]{1,0:T(8,128)S(1)}, f32[32,128]{1,0:T(8,128)S(1)}, u32[]{:S(2)}, u32[]{:S(2)}) collective-permute-start(f32[32,128]{1,0:T(8,128)S(1)} %shard_map.89), channel_id=1, source_target_pairs={{0,1},{1,0},{2,3},{3,2},{4,5},{5,4},{6,7},{7,6},{8,9},{9,8},{10,11... | collective-permute-start | bytes 49160 | tf_op jit(solution)/shard_map/ppermute | solution.py:356
  75.6 10.0 %collective-permute-start.14 = (f32[32,128]{1,0:T(8,128)S(1)}, f32[32,128]{1,0:T(8,128)S(1)}, u32[]{:S(2)}, u32[]{:S(2)}) collective-permute-start(f32[32,128]{1,0:T(8,128)S(1)} %add.12), channel_id=1, source_target_pairs={{0,4},{1,5},{2,6},{3,7},{4,0},{5,1},{6,2},{7,3},{8,12},{9,13},{10,... | collective-permute-start | bytes 49160 | tf_op jit(solution)/shard_map/ppermute | solution.py:359
  80.8 6.7 %collective-permute-start.13 = (f32[32,128]{1,0:T(8,128)S(1)}, f32[32,128]{1,0:T(8,128)S(1)}, u32[]{:S(2)}, u32[]{:S(2)}) collective-permute-start(f32[32,128]{1,0:T(8,128)S(1)} %add.12), channel_id=1, source_target_pairs={{0,6},{1,7},{2,0},{3,1},{4,2},{5,3},{6,4},{7,5},{8,14},{9,15},{10,... | collective-permute-start | bytes 49160 | tf_op jit(solution)/shard_map/ppermute | solution.py:359
  84.7 4.9 %collective-permute-start.12 = (f32[32,128]{1,0:T(8,128)S(1)}, f32[32,128]{1,0:T(8,128)S(1)}, u32[]{:S(2)}, u32[]{:S(2)}) collective-permute-start(f32[32,128]{1,0:T(8,128)S(1)} %add.12), channel_id=1, source_target_pairs={{0,2},{1,3},{2,4},{3,5},{4,6},{5,7},{6,0},{7,1},{8,10},{9,11},{10,... | collective-permute-start | bytes 49160 | tf_op jit(solution)/shard_map/ppermute | solution.py:359
  90.5 15.9 %all-to-all-start.3 = ((bf16[32,32,128]{2,1,0:T(8,128)(2,1)}), bf16[32,32,128]{2,1,0:T(8,128)(2,1)S(1)}, u32[]{:S(2)}, u32[]{:S(2)}) async-start(bf16[32,32,128]{2,1,0:T(8,128)(2,1)} %broadcast_in_dim.2), calls=%async_computation.3 | async-start | bytes 524288 | tf_op jit(solution)/shard_map/all_to_all | solution.py:300
  97.1 13.8 %collective-permute-start.8 = (bf16[2,128,512]{2,1,0:T(8,128)(2,1)}, bf16[2,128,512]{2,1,0:T(8,128)(2,1)S(1)}, u32[]{:S(2)}, u32[]{:S(2)}) collective-permute-start(bf16[2,128,512]{2,1,0:T(8,128)(2,1)} %get-tuple-element.35), channel_id=1, source_target_pairs={{0,2},{1,3},{2,4},{3,5},{4,6},{5,7},{6,0},{7,1},{8,10},{9,11},{10,... | collective-permute-start | bytes 786440 | tf_op jit(solution)/shard_map/ppermute | solution.py:354
  97.2 13.7 %collective-permute-start.9 = (bf16[2,128,512]{2,1,0:T(8,128)(2,1)}, bf16[2,128,512]{2,1,0:T(8,128)(2,1)S(1)}, u32[]{:S(2)}, u32[]{:S(2)}) collective-permute-start(bf16[2,128,512]{2,1,0:T(8,128)(2,1)} %get-tuple-element.36), channel_id=1, source_target_pairs={{0,6},{1,7},{2,0},{3,1},{4,2},{5,3},{6,4},{7,5},{8,14},{9,15},{10,... | collective-permute-start | bytes 786440 | tf_op jit(solution)/shard_map/ppermute | solution.py:354
  100.4 10.5 %collective-permute-start.10 = (bf16[2,128,512]{2,1,0:T(8,128)(2,1)}, bf16[2,128,512]{2,1,0:T(8,128)(2,1)S(1)}, u32[]{:S(2)}, u32[]{:S(2)}) collective-permute-start(bf16[2,128,512]{2,1,0:T(8,128)(2,1)} %get-tuple-element.37), channel_id=1, source_target_pairs={{0,4},{1,5},{2,6},{3,7},{4,0},{5,1},{6,2},{7,3},{8,12},{9,13},{10,... | collective-permute-start | bytes 786440 | tf_op jit(solution)/shard_map/ppermute | solution.py:354

commit v3 on v2

--- a/solution.py
+++ b/solution.py
@@ -31,13 +31,26 @@
     return jax.ShapeDtypeStruct(dims, kind)
 
 
-def pack_kernel(side_ref, rate_ref, out_ref):
+def pack_kernel(side_hbm, rate_hbm, out_ref, side_ref, rate_ref, sems):
     blocks, _, lanes = out_ref.shape
     count = side_ref.shape[0] // 2
     per = count // blocks
-    for h in range(2):
-        rows = side_ref[pl.ds(h, count, stride=2), :]
-        out_ref[:, h * per : (h + 1) * per, :] = rows.reshape(blocks, per, lanes).astype(BF)
+    groups = 4
+    copies = [pltpu.make_async_copy(rate_hbm, rate_ref, sems.at[groups])]
+    for g in range(groups):
+        rows = pl.ds(g * (2 * count // groups), 2 * count // groups)
+        copies.append(pltpu.make_async_copy(side_hbm.at[rows], side_ref.at[rows], sems.at[g]))
+    for copy in copies:
+        copy.start()
+    copies[0].wait()
+    for g in range(groups):
+        copies[1 + g].wait()
+        first, some = g * (blocks // groups), blocks // groups
+        for h in range(2):
+            rows = side_ref[pl.ds(2 * first * per + h, some * per, stride=2), :]
+            out_ref[first : first + some, h * per : (h + 1) * per, :] = rows.reshape(
+                some, per, lanes
+            ).astype(BF)
     rate = rate_ref[...]
     high = rate.astype(BF).astype(F32)
     middle = (rate - high).astype(BF).astype(F32)
@@ -129,6 +142,11 @@
         out_ref[rows, :] = out_ref[rows, :] + rhs_ref[h]
 
 
+def spread_kernel(a_ref, b_ref, c_ref, d_ref, out_ref):
+    total = (a_ref[...] + b_ref[...]) + (c_ref[...] + d_ref[...])
+    out_ref[...] = jnp.broadcast_to(total.astype(BF)[None], out_ref.shape)
+
+
 def tip_kernel(fixed_ref, tip_ref, full_ref, own_ref, solved_ref):
     order = tip_ref.shape[1]
     row = lax.broadcasted_iota(jnp.int32, (order, order), 0)
@@ -152,41 +170,32 @@
     return 2 * lax.rem(chip + shift, 4) + (1 - core if e else core)
 
 
-def factor_kernel(mask_ref, *refs):
-    pieces = refs[:8]
-    factor_ref, keep_ref, send_ref, held, values, total, parts, sems = refs[8:]
+def keep_kernel(mask_ref, factor_ref, out_ref, held, sems):
     rows = held.shape[2]
     tiles = rows // TILE
     place = lax.axis_index("space")
     sources = [index_of(e, 4 - shift) for e in range(2) for shift in SHIFTS]
 
-    def copies(j):
+    def copy_in(j):
         start = pl.multiple_of(sources[j] * rows, rows)
-        return (
-            pltpu.make_async_copy(pieces[j], values.at[j], sems.at[0, j]),
-            pltpu.make_async_copy(
-                factor_ref.at[:, :, pl.ds(start, rows)], held.at[j], sems.at[1, j]
-            ),
-        )
-
-    def copy_out(e, d):
-        out_ref = send_ref if e else keep_ref
-        return pltpu.make_async_copy(parts.at[4 * e + d], out_ref.at[d], sems.at[2, 4 * e + d])
+        return pltpu.make_async_copy(
+            factor_ref.at[:, :, pl.ds(start, rows)], held.at[j], sems.at[0, j]
+        )
+
+    def copy_out(j):
+        return pltpu.make_async_copy(held.at[j], out_ref.at[j], sems.at[1, j])
 
     for j in range(8):
 
         @pl.when(sources[j] <= place)
         def _(j=j):
-            for copy in copies(j):
-                copy.start()
-
-    total[...] = jnp.zeros_like(total)
+            copy_in(j).start()
+
     for j in range(8):
 
         @pl.when(sources[j] <= place)
         def _(j=j):
-            for copy in copies(j):
-                copy.wait()
+            copy_in(j).wait()
 
             @pl.loop(0, tiles * tiles)
             def _(at):
@@ -210,10 +219,49 @@
                         sl = slice(r * TILE, (r + 1) * TILE)
                         block = held[0, h, sl, sl].astype(F32)
                         held[0, h, sl, sl] = jnp.where(row >= col, block, 0.0).astype(BF)
+            copy_out(j).start()
+
+    for j in range(8):
+
+        @pl.when(sources[j] <= place)
+        def _(j=j):
+            copy_out(j).wait()
+
+
+def factor_kernel(*refs):
+    pieces = refs[:8]
+    factor_ref, keep_ref, send_ref, held, values, total, parts, sems = refs[8:]
+    place = lax.axis_index("space")
+    sources = [index_of(e, 4 - shift) for e in range(2) for shift in SHIFTS]
+
+    def copies(j):
+        return (
+            pltpu.make_async_copy(pieces[j], values.at[j], sems.at[0, j]),
+            pltpu.make_async_copy(factor_ref.at[j], held.at[j], sems.at[1, j]),
+        )
+
+    def copy_out(e, d):
+        out_ref = send_ref if e else keep_ref
+        return pltpu.make_async_copy(parts.at[4 * e + d], out_ref.at[d], sems.at[2, 4 * e + d])
+
+    for j in range(8):
+
+        @pl.when(sources[j] <= place)
+        def _(j=j):
+            for copy in copies(j):
+                copy.start()
+
+    for j in range(8):
+
+        @pl.when(sources[j] <= place)
+        def _(j=j):
+            for copy in copies(j):
+                copy.wait()
             for h in range(2):
-                total[h] += jnp.dot(
+                got = jnp.dot(
                     held[j, h], setting_rows(values.at[j], h), preferred_element_type=F32
                 )
+                total[h] = total[h] + got if j else got
 
     inner = [jnp.transpose(total[h]).astype(BF) for h in range(2)]
     for e in (1, 0):
@@ -256,20 +304,24 @@
     for d in order:
         for copy in ins[d]:
             copy.wait()
-        kept[d] = (kept[d].astype(F32) + other[d].astype(F32)).astype(BF)
+        kept[d] = kept[d] + other[d]
         back[d].start()
     for d in order:
         back[d].wait()
 
 
-def carried_kernel(a_ref, b_ref, c_ref, d_ref, arrow_ref, fixed_ref, carried_ref, out_ref):
+def carried_kernel(
+    a_hbm, b_ref, c_ref, d_ref, arrow_ref, fixed_ref, carried_ref, out_ref, a_ref, sem
+):
     blocks, height, lanes = out_ref.shape
     per = height // 2
-    for h in range(2):
-        total = a_ref[h].astype(F32)
-        for ref in (b_ref, c_ref, d_ref):
-            total = total + ref[h].astype(F32)
-        total = jnp.transpose(total)
+    copy = pltpu.make_async_copy(a_hbm, a_ref, sem)
+    copy.start()
+    for h in range(2):
+        total = b_ref[h].astype(F32) + c_ref[h].astype(F32) + d_ref[h].astype(F32)
+        if h == 0:
+            copy.wait()
+        total = jnp.transpose(total + a_ref[h].astype(F32))
         total = total - jnp.dot(arrow_ref[h], fixed_ref[h], preferred_element_type=F32)
         carried_ref[h] = total
         out_ref[:, h * per : (h + 1) * per, :] = total.astype(BF).reshape(blocks, per, lanes)
@@ -302,31 +354,55 @@
     def distant(array):
         return pltpu.with_memory_space_constraint(array, pltpu.HBM)
 
-    arrow = jnp.transpose(arrow_rows[0], (1, 0, 2))
-    packed = call(pack_kernel, shape((times, 2 * per + 8, lanes), BF))(
-        right_side.reshape(2 * count, lanes), jnp.transpose(carry_rate[0])
-    )
+    far = pl.BlockSpec(memory_space=pltpu.HBM)
+    packed = call(
+        pack_kernel,
+        shape((times, 2 * per + 8, lanes), BF),
+        [
+            pltpu.VMEM((2 * count, lanes), F32),
+            pltpu.VMEM((2, count), F32),
+            pltpu.SemaphoreType.DMA((5,)),
+        ],
+        in_specs=[far, far],
+    )(distant(right_side.reshape(2 * count, lanes)), distant(jnp.transpose(carry_rate[0])))
+    packed, tile_mask = lax.optimization_barrier((packed, tile_mask))
+    held = call(
+        keep_kernel,
+        pltpu.HBM((8, 2, count, count), BF),
+        [pltpu.VMEM((8, 2, count, count), BF), pltpu.SemaphoreType.DMA((2, 8))],
+        in_specs=[pl.BlockSpec(memory_space=pltpu.SMEM), far],
+        out_specs=far,
+        vmem=12,
+        moved=16 * MIB,
+    )(tile_mask, distant(inverse_factor[:, 0]))
+    packed, held = lax.optimization_barrier((turned(packed), held))
     forward, rate = call(
         forward_kernel,
         (shape(block, BF), shape((per, lanes), F32)),
         [pltpu.VMEM((8 * times, lanes), F32), pltpu.VMEM((lanes, lanes), F32)],
-    )(turned(packed))
+    )(packed)
     forward_b = turned(forward)
 
-    far = pl.BlockSpec(memory_space=pltpu.HBM)
     pieces = [forward_b] + [lax.ppermute(forward_b, "space", along(s)) for s in SHIFTS[1:]]
-    coupling = call(coupling_kernel, shape((times, 2 * fixed_total // times, lanes), BF))(
-        arrow, forward_b
-    )
+    arrow_rows, forward_b = lax.optimization_barrier((arrow_rows, forward_b))
+    arrow = jnp.transpose(arrow_rows[0], (1, 0, 2))
+    coupling = call(
+        coupling_kernel,
+        shape((times, 2 * fixed_total // times, lanes), BF),
+        flops=1 << 32,
+        moved=8 * MIB,
+    )(arrow, forward_b)
     sums = call(sum_kernel, shape((2 * fixed_total // times, lanes), F32))(
         turned(coupling), fixed_rhs
     )
     pieces = pieces + [lax.ppermute(p, "space", near) for p in pieces]
+    sums = sums + lax.ppermute(sums, "space", near)
     pieces, sums = lax.optimization_barrier((pieces, sums))
+    fixed = [sums] + [lax.ppermute(sums, "space", along(s)) for s in SHIFTS[1:]]
     part = (2, lanes, count)
     keep, send = call(
         factor_kernel,
-        (shape((4,) + part, BF), shape((4,) + part, BF)),
+        (pltpu.HBM((4,) + part, BF), pltpu.HBM((4,) + part, BF)),
         [
             pltpu.VMEM((8, 2, count, count), BF),
             pltpu.VMEM((8,) + block, BF),
@@ -334,15 +410,17 @@
             pltpu.VMEM((8,) + part, BF),
             pltpu.SemaphoreType.DMA((3, 8)),
         ],
-        in_specs=[pl.BlockSpec(memory_space=pltpu.SMEM)] + [far] * 9,
+        in_specs=[far] * 9,
         out_specs=(far, far),
         vmem=24,
         flops=1 << 31,
         moved=12 * MIB,
-    )(tile_mask, *[distant(p) for p in pieces], distant(inverse_factor[:, 0]))
+    )(*[distant(p) for p in pieces], distant(held))
+    spread = call(spread_kernel, shape((times,) + sums.shape, BF))(*fixed)
+    send, spread = lax.optimization_barrier((send, spread))
     parts = call(
         add_kernel,
-        (shape(part, BF),) * 4,
+        (pltpu.HBM(part, BF),) * 4,
         [
             pltpu.VMEM((4,) + part, BF),
             pltpu.VMEM((4,) + part, BF),
@@ -353,20 +431,18 @@
     )(distant(keep), distant(lax.ppermute(send, "space", near)))
     scaled = [parts[0]] + [lax.ppermute(p, "space", along(s)) for p, s in zip(parts[1:], SHIFTS[1:])]
 
-    sums = sums + lax.ppermute(sums, "space", near)
-    fixed = sums
-    for s in SHIFTS[1:]:
-        fixed = fixed + lax.ppermute(sums, "space", along(s))
-    fixed_forward = turned(jnp.broadcast_to(fixed.astype(BF)[None], (times,) + fixed.shape))
     fixed_b, fixed_own = call(
         tip_kernel,
         (shape((2, fixed_total, lanes), BF), shape(fixed_rhs.shape, F32)),
         [pltpu.VMEM((fixed_total, lanes), F32)],
-    )(fixed_forward, tip_factor)
-
-    carried, ready = call(carried_kernel, (shape((2, count, lanes), F32), shape(block, BF)))(
-        *scaled, arrow, fixed_b
-    )
+    )(turned(spread), tip_factor)
+
+    carried, ready = call(
+        carried_kernel,
+        (shape((2, count, lanes), F32), shape(block, BF)),
+        [pltpu.VMEM(part, BF), pltpu.SemaphoreType.DMA],
+        in_specs=[far] + [pl.BlockSpec(memory_space=pltpu.VMEM)] * 5,
+    )(distant(scaled[0]), *scaled[1:], arrow, fixed_b)
     following = turned(call(backward_kernel, shape(block, BF))(turned(ready), rate))
     solution = call(final_kernel, shape((2 * count, lanes), F32))(carried, following)
     return (solution.reshape(right_side.shape), fixed_own)

time: 149 us -> 147 us (0.987)
  blocking collectives: 76.6 us -> 52.6 us
  starting transfers between devices: 29.1 us -> 43.3 us
  Pallas kernels: 11.1 us -> 18 us
  waiting for transfers between devices: 24.6 us -> 30.7 us
  local copies, waits for them, and re-layouts: 6.25 us -> 0.9 us
    all_to_all x4 -> x3, blocking collectives: 76.6 us -> 52.6 us  [turned(): return lax.all_to_all(array, 'tm', 0, 0, tiled=True)]
    all_to_all x2 -> x3, starting transfers between devices: 8.97 us -> 25.8 us  [turned(): return lax.all_to_all(array, 'tm', 0, 0, tiled=True)]
    ppermute x3, waiting for transfers between devices: 0.43 us -> 9 us  [on_device(): lax.ppermute(forward_b, 'space', along(s))]
    pallas_call x5 -> x7, Pallas kernels: 7.91 us -> 14.9 us  [the longest x1 3.71 us: on_device(): call(factor_kernel, (pltpu.HBM((4,) + part, BF), pltpu.HBM((4,) + part, B...]
    ppermute x3, starting transfers between devices: 10 us -> 3.85 us  [on_device(): fixed = [sums] + [lax.ppermute(sums, 'space', along(s)) for s in SHIFTS[1:]]]
    unnamed x19 -> x14, local copies, waits for them, and re-layouts: 5.49 us -> 0.74 us
    ppermute x3, waiting for transfers between devices: 2.97 us -> 7.51 us  [on_device(): lax.ppermute(p, 'space', along(s))]
    ppermute x3, starting transfers between devices: 3.82 us -> 7.74 us  [on_device(): lax.ppermute(p, 'space', along(s))]
  transfers between devices with their start and end apart: 17 -> 18, of which waited for: 7 -> 10; matrix products, arithmetic and copies ran while one was open for 1% -> 0% of each run, Pallas kernels for 3% -> 8%
where the time goes in v3:
time: 147 us; the launch traced here: 146 us
  blocking collectives  52.6 us (36%)
  starting transfers between devices  43.3 us (29%)
  waiting for transfers between devices  30.7 us (21%)
  Pallas kernels  18 us (12%)
    all_to_all x3, blocking collectives, turned(): return lax.all_to_all(array, 'tm', 0, 0, tiled=True)  52.6 us
    all_to_all x3, starting transfers between devices, turned(): return lax.all_to_all(array, 'tm', 0, 0, tiled=True)  25.8 us
    all_to_all x3, waiting for transfers between devices, turned(): return lax.all_to_all(array, 'tm', 0, 0, tiled=True)  12.1 us
    ppermute x3, waiting for transfers between devices, on_device(): lax.ppermute(forward_b, 'space', along(s))  9 us
    ppermute x3, starting transfers between devices, on_device(): lax.ppermute(p, 'space', along(s))  7.74 us
    ppermute x3, waiting for transfers between devices, on_device(): lax.ppermute(p, 'space', along(s))  7.51 us
    ppermute x3, starting transfers between devices, on_device(): lax.ppermute(forward_b, 'space', along(s))  5.14 us
    ppermute x3, starting transfers between devices, on_device(): fixed = [sums] + [lax.ppermute(sums, 'space', along(s)) for s in SHIFTS[1:]]  3.85 us
  transfers between devices with their start and end apart: 18, of which 10 were waited for; matrix products, arithmetic and copies ran while one was open for 0% of the time, Pallas kernels for 8%

profile of v3, /device:TPU:32, one launch (start us, length us, event | category | flops | bytes accessed | tf_op | source)
XLA Modules:
  0.0 146.3 jit_solution(15688376576238050588)
XLA Ops:
  0.6 1.9 %shard_map.86 = bf16[32,40,128]{2,1,0:T(8,128)(2,1)} custom-call(f32[1024,128]{1,0:T(8,128)} %bitcast.14, f32[2,512]{1,0:T(2,128)} %bitcast.16), custom_call_target="tpu_custom_call" | custom-call | flops 1048576 | bytes 1048576 | tf_op jit(solution)/shard_map/pallas_call | solution.py:358
  2.5 11.4 %all-to-all-start = ((bf16[32,40,128]{2,1,0:T(8,128)(2,1)}), bf16[32,40,128]{2,1,0:T(8,128)(2,1)S(1)}, u32[]{:S(2)}, u32[]{:S(2)}) async-start(bf16[32,40,128]{2,1,0:T(8,128)(2,1)} %shard_map.86), calls=%async_computation | async-start | bytes 655360 | tf_op jit(solution)/shard_map/all_to_all | solution.py:352
  13.9 0.0 copy-start.2
  13.9 0.7 copy-done.2
  14.6 0.0 copy-start.4
  14.6 3.6 %shard_map.87.refs_8_ = bf16[8,2,512,512]{3,2,1,0:T(8,128)(2,1)} custom-call(s32[32,32]{1,0:T(8,128)S(1)} %copy-done.2, bf16[2,512,4096]{2,1,0:T(8,128)(2,1)} %bitcast.13), custom_call_target="tpu_custom_call" | custom-call | flops 1048576 | bytes 16777216 | tf_op jit(solution)/shard_map/pallas_call | solution.py:369
  18.2 9.3 %all-to-all-done.got_ref = bf16[32,40,128]{2,1,0:T(8,128)(2,1)S(1)} async-done(((bf16[32,40,128]{2,1,0:T(8,128)(2,1)}), bf16[32,40,128]{2,1,0:T(8,128)(2,1)S(1)}, u32[]{:S(2)}, u32[]{:S(2)}) %all-to-all-start) | async-done | bytes 327712 | tf_op jit(solution)/shard_map/all_to_all | solution.py:352
  27.5 0.4 shard_map.88
  27.9 15.9 %all_to_all.30.forward_ref.refs_0_ = bf16[32,32,128]{2,1,0:T(8,128)(2,1)S(1)} all-to-all(bf16[32,32,128]{2,1,0:T(8,128)(2,1)S(1)} %get-tuple-element.34), channel_id=1, replica_groups=mesh['tm'=32,'space'=8] {'tm'}, dimensions={0} | all-to-all | bytes 524288 | tf_op jit(solution)/shard_map/all_to_all | solution.py:352
  43.8 0.0 copy-done.4
  43.8 0.0 copy-start.1
  43.8 0.2 copy.11
  44.0 0.0 copy-start.3
  44.0 1.2 shard_map.89
  45.2 0.0 copy-start
  45.2 4.7 %all-to-all-start.2 = ((bf16[32,32,128]{2,1,0:T(8,128)(2,1)}), bf16[32,32,128]{2,1,0:T(8,128)(2,1)S(1)}, u32[]{:S(2)}, u32[]{:S(2)}) async-start(bf16[32,32,128]{2,1,0:T(8,128)(2,1)} %shard_map.89), calls=%async_computation.2 | async-start | bytes 524288 | tf_op jit(solution)/shard_map/all_to_all | solution.py:352
  49.9 3.1 %collective-permute-start.2 = (bf16[32,32,128]{2,1,0:T(8,128)(2,1)S(1)}, bf16[32,32,128]{2,1,0:T(8,128)(2,1)S(1)}, u32[]{:S(2)}, u32[]{:S(2)}) collective-permute-start(bf16[32,32,128]{2,1,0:T(8,128)(2,1)S(1)} %all_to_all.30.forward_ref.refs_0_), channel_id=1, source_target_pairs={{0,4},{1,5},{2,6},{3,7},{4,0},{5,1},{6,2},{7,3},{8,12},{9,13},{10,... | collective-permute-start | bytes 786440 | tf_op jit(solution)/shard_map/ppermute | solution.py:386
  53.0 1.1 collective-permute-start.1
  54.2 0.9 collective-permute-start
  55.1 0.0 copy-done.1
  55.1 0.0 collective-permute-start.3
  55.1 5.4 %collective-permute-done.2.refs_3_ = bf16[32,32,128]{2,1,0:T(8,128)(2,1)S(1)} collective-permute-done((bf16[32,32,128]{2,1,0:T(8,128)(2,1)S(1)}, bf16[32,32,128]{2,1,0:T(8,128)(2,1)S(1)}, u32[]{:S(2)}, u32[]{:S(2)}) %collective-permute-start.2) | collective-permute-done | bytes 262176 | tf_op jit(solution)/shard_map/ppermute | solution.py:386
  60.5 0.0 copy-start.5
  60.5 0.0 collective-permute-start.6
  60.5 3.6 %collective-permute-done.1.refs_2_ = bf16[32,32,128]{2,1,0:T(8,128)(2,1)S(1)} collective-permute-done((bf16[32,32,128]{2,1,0:T(8,128)(2,1)S(1)}, bf16[32,32,128]{2,1,0:T(8,128)(2,1)S(1)}, u32[]{:S(2)}, u32[]{:S(2)}) %collective-permute-start.1) | collective-permute-done | bytes 262176 | tf_op jit(solution)/shard_map/ppermute | solution.py:386
  64.1 0.0 collective-permute-start.5
  64.1 0.0 collective-permute-done.refs_1_
  64.1 0.5 collective-permute-start.4
  64.6 0.0 all-to-all-done.2.got_ref
  64.6 0.0 copy-done.3
  64.6 0.2 collective-permute-start.7
  64.8 1.2 collective-permute-done.7
  66.0 0.0 collective-permute-done.3.refs_4_
  66.0 0.0 collective-permute-done.6.refs_7_
  66.0 0.0 collective-permute-done.5.refs_6_
  66.1 0.3 collective-permute-done.4.refs_5_
  66.3 1.8 %collective-permute-start.10 = (f32[32,128]{1,0:T(8,128)S(1)}, f32[32,128]{1,0:T(8,128)S(1)}, u32[]{:S(2)}, u32[]{:S(2)}) collective-permute-start(f32[32,128]{1,0:T(8,128)S(1)} %add.3.a_ref), channel_id=1, source_target_pairs={{0,4},{1,5},{2,6},{3,7},{4,0},{5,1},{6,2},{7,3},{8,12},{9,13},{10,... | collective-permute-start | bytes 49160 | tf_op jit(solution)/shard_map/ppermute | solution.py:401
  68.2 1.4 collective-permute-start.9
  69.6 0.6 collective-permute-start.8
  70.2 0.0 copy-done.5
  70.2 0.0 copy-done.6
  70.2 3.7 %shard_map.91 = (bf16[4,2,128,512]{3,2,1,0:T(8,128)(2,1)}, bf16[4,2,128,512]{3,2,1,0:T(8,128)(2,1)}) custom-call(bf16[32,32,128]{2,1,0:T(8,128)(2,1)} %copy-done.1, bf16[32,32,128]{2,1,0:T(8,128)(2,1)} %collective-permute-done.refs_1_, bf16[32,32,128]{2,1,0:T(8,128)(2,1)} %copy-done.6, bf16[32,32,128]{2,1,0:T(8,128)(2,1)} %copy-done.5, ...), custom_call_target="tpu_custom_call" | custom-call | flops 2147483648 | bytes 12582912 | tf_op jit(solution)/shard_map/pallas_call | solution.py:403
  73.9 0.0 collective-permute-done.10.d_ref
  73.9 0.0 collective-permute-done.9.c_ref
  73.9 0.6 collective-permute-done.8.b_ref
  74.5 0.7 shard_map.92
  75.3 0.0 collective-permute-start.11
  75.3 9.8 %all-to-all-start.3 = ((bf16[32,32,128]{2,1,0:T(8,128)(2,1)}), bf16[32,32,128]{2,1,0:T(8,128)(2,1)S(1)}, u32[]{:S(2)}, u32[]{:S(2)}) async-start(bf16[32,32,128]{2,1,0:T(8,128)(2,1)} %shard_map.92), calls=%async_computation.3 | async-start | bytes 524288 | tf_op jit(solution)/shard_map/all_to_all | solution.py:352
  85.1 0.0 collective-permute-done.11.got_ref
  85.1 2.3 %shard_map.93 = (bf16[2,128,512]{2,1,0:T(8,128)(2,1)}, bf16[2,128,512]{2,1,0:T(8,128)(2,1)}, bf16[2,128,512]{2,1,0:T(8,128)(2,1)}, bf16[2,128,512]{2,1,0:T(8,128)(2,1)}) custom-call(bf16[4,2,128,512]{3,2,1,0:T(8,128)(2,1)} %get-tuple-element.46.keep_ref, bf16[4,2,128,512]{3,2,1,0:T(8,128)(2,1)} %collective-permute-done.11.got_ref), custom_call_target="tpu_custom_call" | custom-call | flops 1048576 | bytes 1048576 | tf_op jit(solution)/shard_map/pallas_call | solution.py:421
  87.4 2.4 %collective-permute-start.12 = (bf16[2,128,512]{2,1,0:T(8,128)(2,1)}, bf16[2,128,512]{2,1,0:T(8,128)(2,1)S(1)}, u32[]{:S(2)}, u32[]{:S(2)}) collective-permute-start(bf16[2,128,512]{2,1,0:T(8,128)(2,1)} %get-tuple-element.51), channel_id=1, source_target_pairs={{0,2},{1,3},{2,4},{3,5},{4,6},{5,7},{6,0},{7,1},{8,10},{9,11},{10,... | collective-permute-start | bytes 786440 | tf_op jit(solution)/shard_map/ppermute | solution.py:432
  89.8 3.9 %collective-permute-start.13 = (bf16[2,128,512]{2,1,0:T(8,128)(2,1)}, bf16[2,128,512]{2,1,0:T(8,128)(2,1)S(1)}, u32[]{:S(2)}, u32[]{:S(2)}) collective-permute-start(bf16[2,128,512]{2,1,0:T(8,128)(2,1)} %get-tuple-element.52), channel_id=1, source_target_pairs={{0,6},{1,7},{2,0},{3,1},{4,2},{5,3},{6,4},{7,5},{8,14},{9,15},{10,... | collective-permute-start | bytes 786440 | tf_op jit(solution)/shard_map/ppermute | solution.py:432
  93.8 1.4 collective-permute-start.14
  95.1 2.8 %all-to-all-done.3.fixed_ref = bf16[32,32,128]{2,1,0:T(8,128)(2,1)S(1)} async-done(((bf16[32,32,128]{2,1,0:T(8,128)(2,1)}), bf16[32,32,128]{2,1,0:T(8,128)(2,1)S(1)}, u32[]{:S(2)}, u32[]{:S(2)}) %all-to-all-start.3) | async-done | bytes 262176 | tf_op jit(solution)/shard_map/all_to_all | solution.py:352
  98.0 0.0 copy-done
  98.0 1.6 %shard_map.94 = (bf16[2,512,128]{2,1,0:T(8,128)(2,1)S(1)}, f32[2,2,128]{2,1,0:T(2,128)}) custom-call(bf16[32,32,128]{2,1,0:T(8,128)(2,1)S(1)} %all-to-all-done.3.fixed_ref, bf16[2,512,512]{2,1,0:T(8,128)(2,1)S(1)} %copy-done), custom_call_target="tpu_custom_call" | custom-call | flops 1048576 | bytes 1048576 | tf_op jit(solution)/shard_map/pallas_call | solution.py:434
  99.6 0.7 collective-permute-done.12.b_ref
  100.3 5.1 %collective-permute-done.13.c_ref = bf16[2,128,512]{2,1,0:T(8,128)(2,1)S(1)} collective-permute-done((bf16[2,128,512]{2,1,0:T(8,128)(2,1)}, bf16[2,128,512]{2,1,0:T(8,128)(2,1)S(1)}, u32[]{:S(2)}, u32[]{:S(2)}) %collective-permute-start.13) | collective-permute-done | bytes 262176 | tf_op jit(solution)/shard_map/ppermute | solution.py:432
  105.3 1.7 %collective-permute-done.14.d_ref = bf16[2,128,512]{2,1,0:T(8,128)(2,1)S(1)} collective-permute-done((bf16[2,128,512]{2,1,0:T(8,128)(2,1)}, bf16[2,128,512]{2,1,0:T(8,128)(2,1)S(1)}, u32[]{:S(2)}, u32[]{:S(2)}) %collective-permute-start.14) | collective-permute-done | bytes 262176 | tf_op jit(solution)/shard_map/ppermute | solution.py:432
  107.1 1.4 shard_map.95
  108.5 21.1 %all_to_all.31.got_ref = bf16[32,32,128]{2,1,0:T(8,128)(2,1)S(1)} all-to-all(bf16[32,32,128]{2,1,0:T(8,128)(2,1)S(1)} %get-tuple-element.57), channel_id=1, replica_groups=mesh['tm'=32,'space'=8] {'tm'}, dimensions={0} | all-to-all | bytes 524288 | tf_op jit(solution)/shard_map/all_to_all | solution.py:352
  129.6 0.3 shard_map.96
  129.8 15.6 %all_to_all.32.following_ref = bf16[32,32,128]{2,1,0:T(8,128)(2,1)S(1)} all-to-all(bf16[32,32,128]{2,1,0:T(8,128)(2,1)S(1)} %shard_map.96), channel_id=1, replica_groups=mesh['tm'=32,'space'=8] {'tm'}, dimensions={0} | all-to-all | bytes 524288 | tf_op jit(solution)/shard_map/all_to_all | solution.py:352
  145.4 0.8 shard_map.97
  (3 shorter events, 0.0 us)
Async XLA Ops:
  2.5 25.0 %all-to-all-start = ((bf16[32,40,128]{2,1,0:T(8,128)(2,1)}), bf16[32,40,128]{2,1,0:T(8,128)(2,1)S(1)}, u32[]{:S(2)}, u32[]{:S(2)}) async-start(bf16[32,40,128]{2,1,0:T(8,128)(2,1)} %shard_map.86), calls=%async_computation | async-start | bytes 655360 | tf_op jit(solution)/shard_map/all_to_all | solution.py:352
  13.9 0.7 copy-start.2
  14.6 29.2 %copy-start.4 = (bf16[1,512,2,512]{3,2,1,0:T(2,128)(2,1)S(1)}, bf16[1,512,2,512]{3,2,1,0:T(2,128)(2,1)}, u32[]{:S(2)}) copy-start(bf16[1,512,2,512]{3,2,1,0:T(2,128)(2,1)} %param.11) | copy-start | bytes 3145732
  43.8 11.2 %copy-start.1 = (bf16[32,32,128]{2,1,0:T(8,128)(2,1)}, bf16[32,32,128]{2,1,0:T(8,128)(2,1)S(1)}, u32[]{:S(2)}) copy-start(bf16[32,32,128]{2,1,0:T(8,128)(2,1)S(1)} %all_to_all.30.forward_ref.refs_0_) | copy-start | bytes 786436
  44.0 20.6 %copy-start.3 = (f32[2,2,128]{2,1,0:T(2,128)S(1)}, f32[2,2,128]{2,1,0:T(2,128)}, u32[]{:S(2)}) copy-start(f32[2,2,128]{2,1,0:T(2,128)} %rhs_ref.1) | copy-start | bytes 6148
  45.2 52.7 %copy-start = (bf16[2,512,512]{2,1,0:T(8,128)(2,1)S(1)}, bf16[2,512,512]{2,1,0:T(8,128)(2,1)}, u32[]{:S(2)}) copy-start(bf16[2,512,512]{2,1,0:T(8,128)(2,1)} %tip_ref.1) | copy-start | bytes 3145732
  45.2 19.4 %all-to-all-start.2 = ((bf16[32,32,128]{2,1,0:T(8,128)(2,1)}), bf16[32,32,128]{2,1,0:T(8,128)(2,1)S(1)}, u32[]{:S(2)}, u32[]{:S(2)}) async-start(bf16[32,32,128]{2,1,0:T(8,128)(2,1)} %shard_map.89), calls=%async_computation.2 | async-start | bytes 524288 | tf_op jit(solution)/shard_map/all_to_all | solution.py:352
  49.9 10.5 %collective-permute-start.2 = (bf16[32,32,128]{2,1,0:T(8,128)(2,1)S(1)}, bf16[32,32,128]{2,1,0:T(8,128)(2,1)S(1)}, u32[]{:S(2)}, u32[]{:S(2)}) collective-permute-start(bf16[32,32,128]{2,1,0:T(8,128)(2,1)S(1)} %all_to_all.30.forward_ref.refs_0_), channel_id=1, source_target_pairs={{0,4},{1,5},{2,6},{3,7},{4,0},{5,1},{6,2},{7,3},{8,12},{9,13},{10,... | collective-permute-start | bytes 786440 | tf_op jit(solution)/shard_map/ppermute | solution.py:386
  53.0 11.0 %collective-permute-start.1 = (bf16[32,32,128]{2,1,0:T(8,128)(2,1)S(1)}, bf16[32,32,128]{2,1,0:T(8,128)(2,1)S(1)}, u32[]{:S(2)}, u32[]{:S(2)}) collective-permute-start(bf16[32,32,128]{2,1,0:T(8,128)(2,1)S(1)} %all_to_all.30.forward_ref.refs_0_), channel_id=1, source_target_pairs={{0,6},{1,7},{2,0},{3,1},{4,2},{5,3},{6,4},{7,5},{8,14},{9,15},{10,... | collective-permute-start | bytes 786440 | tf_op jit(solution)/shard_map/ppermute | solution.py:386
  54.2 9.9 %collective-permute-start = (bf16[32,32,128]{2,1,0:T(8,128)(2,1)S(1)}, bf16[32,32,128]{2,1,0:T(8,128)(2,1)}, u32[]{:S(2)}, u32[]{:S(2)}) collective-permute-start(bf16[32,32,128]{2,1,0:T(8,128)(2,1)S(1)} %all_to_all.30.forward_ref.refs_0_), channel_id=1, source_target_pairs={{0,2},{1,3},{2,4},{3,5},{4,6},{5,7},{6,0},{7,1},{8,10},{9,11},{10,... | collective-permute-start | bytes 786440 | tf_op jit(solution)/shard_map/ppermute | solution.py:386
  55.1 11.0 %collective-permute-start.3 = (bf16[32,32,128]{2,1,0:T(8,128)(2,1)S(1)}, bf16[32,32,128]{2,1,0:T(8,128)(2,1)}, u32[]{:S(2)}, u32[]{:S(2)}) collective-permute-start(bf16[32,32,128]{2,1,0:T(8,128)(2,1)S(1)} %all_to_all.30.forward_ref.refs_0_), channel_id=1, source_target_pairs={{0,1},{1,0},{2,3},{3,2},{4,5},{5,4},{6,7},{7,6},{8,9},{9,8},{10,11... | collective-permute-start | bytes 786440 | tf_op jit(solution)/shard_map/ppermute | solution.py:398
  60.5 9.7 %copy-start.5 = (bf16[32,32,128]{2,1,0:T(8,128)(2,1)}, bf16[32,32,128]{2,1,0:T(8,128)(2,1)S(1)}, u32[]{:S(2)}) copy-start(bf16[32,32,128]{2,1,0:T(8,128)(2,1)S(1)} %collective-permute-done.2.refs_3_) | copy-start | bytes 786436
  60.5 5.6 %collective-permute-start.6 = (bf16[32,32,128]{2,1,0:T(8,128)(2,1)S(1)}, bf16[32,32,128]{2,1,0:T(8,128)(2,1)}, u32[]{:S(2)}, u32[]{:S(2)}) collective-permute-start(bf16[32,32,128]{2,1,0:T(8,128)(2,1)S(1)} %collective-permute-done.2.refs_3_), channel_id=1, source_target_pairs={{0,1},{1,0},{2,3},{3,2},{4,5},{5,4},{6,7},{7,6},{8,9},{9,8},{10,11... | collective-permute-start | bytes 786440 | tf_op jit(solution)/shard_map/ppermute | solution.py:398
  64.1 6.1 %copy-start.6 = (bf16[32,32,128]{2,1,0:T(8,128)(2,1)}, bf16[32,32,128]{2,1,0:T(8,128)(2,1)S(1)}, u32[]{:S(2)}) copy-start(bf16[32,32,128]{2,1,0:T(8,128)(2,1)S(1)} %collective-permute-done.1.refs_2_) | copy-start | bytes 786436
  64.1 2.0 %collective-permute-start.5 = (bf16[32,32,128]{2,1,0:T(8,128)(2,1)S(1)}, bf16[32,32,128]{2,1,0:T(8,128)(2,1)}, u32[]{:S(2)}, u32[]{:S(2)}) collective-permute-start(bf16[32,32,128]{2,1,0:T(8,128)(2,1)S(1)} %collective-permute-done.1.refs_2_), channel_id=1, source_target_pairs={{0,1},{1,0},{2,3},{3,2},{4,5},{5,4},{6,7},{7,6},{8,9},{9,8},{10,11... | collective-permute-start | bytes 786440 | tf_op jit(solution)/shard_map/ppermute | solution.py:398
  64.1 2.2 %collective-permute-start.4 = (bf16[32,32,128]{2,1,0:T(8,128)(2,1)}, bf16[32,32,128]{2,1,0:T(8,128)(2,1)}, u32[]{:S(2)}, u32[]{:S(2)}) collective-permute-start(bf16[32,32,128]{2,1,0:T(8,128)(2,1)} %collective-permute-done.refs_1_), channel_id=1, source_target_pairs={{0,1},{1,0},{2,3},{3,2},{4,5},{5,4},{6,7},{7,6},{8,9},{9,8},{10,11... | collective-permute-start | bytes 786440 | tf_op jit(solution)/shard_map/ppermute | solution.py:398
  64.6 1.4 collective-permute-start.7
  66.3 7.6 %collective-permute-start.10 = (f32[32,128]{1,0:T(8,128)S(1)}, f32[32,128]{1,0:T(8,128)S(1)}, u32[]{:S(2)}, u32[]{:S(2)}) collective-permute-start(f32[32,128]{1,0:T(8,128)S(1)} %add.3.a_ref), channel_id=1, source_target_pairs={{0,4},{1,5},{2,6},{3,7},{4,0},{5,1},{6,2},{7,3},{8,12},{9,13},{10,... | collective-permute-start | bytes 49160 | tf_op jit(solution)/shard_map/ppermute | solution.py:401
  68.2 5.8 %collective-permute-start.9 = (f32[32,128]{1,0:T(8,128)S(1)}, f32[32,128]{1,0:T(8,128)S(1)}, u32[]{:S(2)}, u32[]{:S(2)}) collective-permute-start(f32[32,128]{1,0:T(8,128)S(1)} %add.3.a_ref), channel_id=1, source_target_pairs={{0,6},{1,7},{2,0},{3,1},{4,2},{5,3},{6,4},{7,5},{8,14},{9,15},{10,... | collective-permute-start | bytes 49160 | tf_op jit(solution)/shard_map/ppermute | solution.py:401
  69.6 4.9 %collective-permute-start.8 = (f32[32,128]{1,0:T(8,128)S(1)}, f32[32,128]{1,0:T(8,128)S(1)}, u32[]{:S(2)}, u32[]{:S(2)}) collective-permute-start(f32[32,128]{1,0:T(8,128)S(1)} %add.3.a_ref), channel_id=1, source_target_pairs={{0,2},{1,3},{2,4},{3,5},{4,6},{5,7},{6,0},{7,1},{8,10},{9,11},{10,... | collective-permute-start | bytes 49160 | tf_op jit(solution)/shard_map/ppermute | solution.py:401
  75.3 9.8 %collective-permute-start.11 = (bf16[4,2,128,512]{3,2,1,0:T(8,128)(2,1)}, bf16[4,2,128,512]{3,2,1,0:T(8,128)(2,1)}, u32[]{:S(2)}, u32[]{:S(2)}) collective-permute-start(bf16[4,2,128,512]{3,2,1,0:T(8,128)(2,1)} %get-tuple-element.49), channel_id=1, source_target_pairs={{0,1},{1,0},{2,3},{3,2},{4,5},{5,4},{6,7},{7,6},{8,9},{9,8},{10,11... | collective-permute-start | bytes 3145736 | tf_op jit(solution)/shard_map/ppermute | solution.py:431
  75.3 22.7 %all-to-all-start.3 = ((bf16[32,32,128]{2,1,0:T(8,128)(2,1)}), bf16[32,32,128]{2,1,0:T(8,128)(2,1)S(1)}, u32[]{:S(2)}, u32[]{:S(2)}) async-start(bf16[32,32,128]{2,1,0:T(8,128)(2,1)} %shard_map.92), calls=%async_computation.3 | async-start | bytes 524288 | tf_op jit(solution)/shard_map/all_to_all | solution.py:352
  87.4 12.9 %collective-permute-start.12 = (bf16[2,128,512]{2,1,0:T(8,128)(2,1)}, bf16[2,128,512]{2,1,0:T(8,128)(2,1)S(1)}, u32[]{:S(2)}, u32[]{:S(2)}) collective-permute-start(bf16[2,128,512]{2,1,0:T(8,128)(2,1)} %get-tuple-element.51), channel_id=1, source_target_pairs={{0,2},{1,3},{2,4},{3,5},{4,6},{5,7},{6,0},{7,1},{8,10},{9,11},{10,... | collective-permute-start | bytes 786440 | tf_op jit(solution)/shard_map/ppermute | solution.py:432
  89.8 15.5 %collective-permute-start.13 = (bf16[2,128,512]{2,1,0:T(8,128)(2,1)}, bf16[2,128,512]{2,1,0:T(8,128)(2,1)S(1)}, u32[]{:S(2)}, u32[]{:S(2)}) collective-permute-start(bf16[2,128,512]{2,1,0:T(8,128)(2,1)} %get-tuple-element.52), channel_id=1, source_target_pairs={{0,6},{1,7},{2,0},{3,1},{4,2},{5,3},{6,4},{7,5},{8,14},{9,15},{10,... | collective-permute-start | bytes 786440 | tf_op jit(solution)/shard_map/ppermute | solution.py:432
  93.8 13.3 %collective-permute-start.14 = (bf16[2,128,512]{2,1,0:T(8,128)(2,1)}, bf16[2,128,512]{2,1,0:T(8,128)(2,1)S(1)}, u32[]{:S(2)}, u32[]{:S(2)}) collective-permute-start(bf16[2,128,512]{2,1,0:T(8,128)(2,1)} %get-tuple-element.53), channel_id=1, source_target_pairs={{0,4},{1,5},{2,6},{3,7},{4,0},{5,1},{6,2},{7,3},{8,12},{9,13},{10,... | collective-permute-start | bytes 786440 | tf_op jit(solution)/shard_map/ppermute | solution.py:432

commit v4 on v3

--- a/solution.py
+++ b/solution.py
@@ -142,26 +142,41 @@
         out_ref[rows, :] = out_ref[rows, :] + rhs_ref[h]
 
 
-def spread_kernel(a_ref, b_ref, c_ref, d_ref, out_ref):
+def settle_kernel(a_ref, b_ref, c_ref, d_ref, out_ref):
+    rows = out_ref.shape[0]
     total = (a_ref[...] + b_ref[...]) + (c_ref[...] + d_ref[...])
-    out_ref[...] = jnp.broadcast_to(total.astype(BF)[None], out_ref.shape)
-
-
-def tip_kernel(fixed_ref, tip_ref, full_ref, own_ref, solved_ref):
+    first = lax.rem(lax.axis_index("space"), 2) == 0
+    out_ref[...] = jnp.where(first, total[:rows], total[rows:]).astype(BF)
+
+
+def spread_kernel(*refs):
+    out_ref = refs[-1]
+    line = jnp.concatenate([ref[...] for ref in refs[:-1]], axis=0)
+    out_ref[...] = jnp.broadcast_to(line[None], out_ref.shape)
+
+
+def tip_kernel(got_ref, tip_ref, mine_ref, own_ref, other_ref, solved_ref, fixed_ref):
     order = tip_ref.shape[1]
+    line, high, lanes = got_ref.shape
+    rows = order // (line * (lax.axis_size("tm") // line))
+    lines = high // rows
+    outer = lax.axis_index("tm") // line
+    for d in range(lines):
+        start = lax.rem(outer + lines - d, lines) * line
+        fixed_ref[pl.ds(start, line)] = got_ref[:, d * rows : (d + 1) * rows, :]
+    core = lax.rem(lax.axis_index("space"), 2)
     row = lax.broadcasted_iota(jnp.int32, (order, order), 0)
     col = lax.broadcasted_iota(jnp.int32, (order, order), 1)
-    own = own_ref.shape[1]
-    place = (lax.axis_index("tm") * lax.axis_size("space") + lax.axis_index("space")) * own
-    for h in range(2):
-        lower = jnp.where(row >= col, tip_ref[h].astype(F32), 0.0).astype(BF)
-        inner = jnp.dot(lower, setting_rows(fixed_ref, h), preferred_element_type=F32).astype(BF)
-        solved = lax.dot_general(
-            lower, inner, (((0,), (0,)), ((), ())), preferred_element_type=F32
-        )
-        solved_ref[...] = solved
-        full_ref[h] = solved.astype(BF)
-        own_ref[h] = solved_ref[pl.ds(place, own), :]
+    lower = jnp.where(row >= col, tip_ref[core].astype(F32), 0.0).astype(BF)
+    fixed = fixed_ref[...].reshape(order, lanes)
+    inner = jnp.dot(lower, fixed, preferred_element_type=F32).astype(BF)
+    solved = lax.dot_general(lower, inner, (((0,), (0,)), ((), ())), preferred_element_type=F32)
+    solved_ref[...] = solved
+    mine_ref[...] = solved.astype(BF)
+    own = own_ref.shape[0]
+    place = lax.axis_index("tm") * lax.axis_size("space") + lax.axis_index("space")
+    own_ref[...] = solved_ref[pl.ds(place * own, own), :]
+    other_ref[...] = solved_ref[pl.ds((place + 1 - 2 * core) * own, own), :]
 
 
 def index_of(e, shift):
@@ -286,42 +301,27 @@
             copy_out(e, d).wait()
 
 
-def add_kernel(keep_ref, got_ref, *refs):
-    outs = refs[:4]
-    kept, other, sems = refs[4:]
-    ins = [
-        (
-            pltpu.make_async_copy(keep_ref.at[d], kept.at[d], sems.at[0, d]),
-            pltpu.make_async_copy(got_ref.at[d], other.at[d], sems.at[1, d]),
-        )
-        for d in range(4)
-    ]
-    back = [pltpu.make_async_copy(kept.at[d], outs[d], sems.at[2, d]) for d in range(4)]
-    order = (3, 1, 2, 0)
-    for d in order:
-        for copy in ins[d]:
-            copy.start()
-    for d in order:
-        for copy in ins[d]:
-            copy.wait()
-        kept[d] = kept[d] + other[d]
-        back[d].start()
-    for d in order:
-        back[d].wait()
+def add_kernel(keep_ref, got_ref, *outs):
+    for d, out_ref in enumerate(outs):
+        out_ref[...] = keep_ref[d] + got_ref[d]
 
 
 def carried_kernel(
-    a_hbm, b_ref, c_ref, d_ref, arrow_ref, fixed_ref, carried_ref, out_ref, a_ref, sem
+    a_ref, b_ref, c_ref, d_ref, arrow_ref, mine_ref, other_ref, own_ref, got_ref,
+    carried_ref, out_ref, both_ref, fixed_ref
 ):
     blocks, height, lanes = out_ref.shape
     per = height // 2
-    copy = pltpu.make_async_copy(a_hbm, a_ref, sem)
-    copy.start()
+    core = lax.rem(lax.axis_index("space"), 2)
+    fixed_ref[pl.ds(core, 1)] = mine_ref[...][None]
+    fixed_ref[pl.ds(1 - core, 1)] = other_ref[...][None]
+    both_ref[pl.ds(core, 1)] = own_ref[...][None]
+    both_ref[pl.ds(1 - core, 1)] = got_ref[...][None]
     for h in range(2):
-        total = b_ref[h].astype(F32) + c_ref[h].astype(F32) + d_ref[h].astype(F32)
-        if h == 0:
-            copy.wait()
-        total = jnp.transpose(total + a_ref[h].astype(F32))
+        total = (a_ref[h].astype(F32) + b_ref[h].astype(F32)) + (
+            c_ref[h].astype(F32) + d_ref[h].astype(F32)
+        )
+        total = jnp.transpose(total)
         total = total - jnp.dot(arrow_ref[h], fixed_ref[h], preferred_element_type=F32)
         carried_ref[h] = total
         out_ref[:, h * per : (h + 1) * per, :] = total.astype(BF).reshape(blocks, per, lanes)
@@ -402,7 +402,7 @@
     part = (2, lanes, count)
     keep, send = call(
         factor_kernel,
-        (pltpu.HBM((4,) + part, BF), pltpu.HBM((4,) + part, BF)),
+        (shape((4,) + part, BF), shape((4,) + part, BF)),
         [
             pltpu.VMEM((8, 2, count, count), BF),
             pltpu.VMEM((8,) + block, BF),
@@ -416,33 +416,40 @@
         flops=1 << 31,
         moved=12 * MIB,
     )(*[distant(p) for p in pieces], distant(held))
-    spread = call(spread_kernel, shape((times,) + sums.shape, BF))(*fixed)
-    send, spread = lax.optimization_barrier((send, spread))
-    parts = call(
-        add_kernel,
-        (pltpu.HBM(part, BF),) * 4,
-        [
-            pltpu.VMEM((4,) + part, BF),
-            pltpu.VMEM((4,) + part, BF),
-            pltpu.SemaphoreType.DMA((3, 4)),
-        ],
-        in_specs=[far, far],
-        out_specs=(far,) * 4,
-    )(distant(keep), distant(lax.ppermute(send, "space", near)))
+    chunk = (sums.shape[0] // 2, lanes)
+    settled = call(settle_kernel, shape(chunk, BF))(*fixed)
+    send, settled = lax.optimization_barrier((send, settled))
+    parts = call(add_kernel, (shape(part, BF),) * 4, vmem=8)(keep, lax.ppermute(send, "space", near))
+
+    line = 8
+    lines = times // line
+    inner = [[y * line + z for z in range(line)] for y in range(lines)]
+    chunks = [settled]
+    for d in range(1, lines):
+        pairs = [(i, (i + d * line) % times) for i in range(times)]
+        chunks.append(lax.ppermute(settled, "tm", pairs))
+    chunks, parts = lax.optimization_barrier((chunks, parts))
     scaled = [parts[0]] + [lax.ppermute(p, "space", along(s)) for p, s in zip(parts[1:], SHIFTS[1:])]
-
-    fixed_b, fixed_own = call(
+    spread = call(spread_kernel, shape((line, lines * chunk[0], lanes), BF))(*chunks)
+    got = lax.all_to_all(spread, "tm", 0, 0, axis_index_groups=inner, tiled=True)
+    own = (fixed_rhs.shape[1], lanes)
+    mine, own_rows, other_rows = call(
         tip_kernel,
-        (shape((2, fixed_total, lanes), BF), shape(fixed_rhs.shape, F32)),
-        [pltpu.VMEM((fixed_total, lanes), F32)],
-    )(turned(spread), tip_factor)
-
-    carried, ready = call(
+        (shape((fixed_total, lanes), BF), shape(own, F32), shape(own, F32)),
+        [pltpu.VMEM((fixed_total, lanes), F32), pltpu.VMEM((times,) + chunk, BF)],
+    )(got, tip_factor)
+    carried, ready, fixed_own = call(
         carried_kernel,
-        (shape((2, count, lanes), F32), shape(block, BF)),
-        [pltpu.VMEM(part, BF), pltpu.SemaphoreType.DMA],
-        in_specs=[far] + [pl.BlockSpec(memory_space=pltpu.VMEM)] * 5,
-    )(distant(scaled[0]), *scaled[1:], arrow, fixed_b)
+        (shape((2, count, lanes), F32), shape(block, BF), shape(fixed_rhs.shape, F32)),
+        [pltpu.VMEM((2, fixed_total, lanes), BF)],
+    )(
+        *scaled,
+        arrow,
+        mine,
+        lax.ppermute(mine, "space", near),
+        own_rows,
+        lax.ppermute(other_rows, "space", near),
+    )
     following = turned(call(backward_kernel, shape(block, BF))(turned(ready), rate))
     solution = call(final_kernel, shape((2 * count, lanes), F32))(carried, following)
     return (solution.reshape(right_side.shape), fixed_own)

time: 147 us -> 145 us (0.986)
  starting transfers between devices: 43.3 us -> 47.1 us
  Pallas kernels: 18 us -> 14.5 us
  blocking collectives: 52.6 us -> 51.1 us
    all_to_all x3 -> x2, starting transfers between devices: 25.8 us -> 16.1 us  [turned(): return lax.all_to_all(array, 'tm', 0, 0, tiled=True)]
    all_to_all x0 -> x1, starting transfers between devices: none -> 7.22 us  [on_device(): lax.all_to_all(spread, 'tm', 0, 0, axis_index_groups=inner, tiled=True)]
    ppermute x0 -> x5, starting transfers between devices: none -> 6.2 us  [the longest x3 5.62 us: on_device(): chunks.append(lax.ppermute(settled, 'tm', pairs))]
    pallas_call x5 -> x6, Pallas kernels: 9.77 us -> 6.25 us  [the longest x1 2.94 us: on_device(): call(factor_kernel, (shape((4,) + part, BF), shape((4,) + part, BF)), [pl...]
    all_to_all x3 -> x2, waiting for transfers between devices: 12.1 us -> 9.26 us  [turned(): return lax.all_to_all(array, 'tm', 0, 0, tiled=True)]
    ppermute x0 -> x5, waiting for transfers between devices: none -> 2.13 us  [the longest x3 1.29 us: on_device(): chunks.append(lax.ppermute(settled, 'tm', pairs))]
    all_to_all x3, blocking collectives: 52.6 us -> 51.1 us  [turned(): return lax.all_to_all(array, 'tm', 0, 0, tiled=True)]
  transfers between devices with their start and end apart: 18 -> 23, of which waited for: 10 -> 12; matrix products, arithmetic and copies ran while one was open for 0% -> 0% of each run, Pallas kernels for 8% -> 6%
where the time goes in v4:
time: 145 us
  blocking collectives  51.1 us (35%)
  starting transfers between devices  47.1 us (32%)
  waiting for transfers between devices  30.2 us (21%)
  Pallas kernels  14.5 us (10%)
    all_to_all x3, blocking collectives, turned(): return lax.all_to_all(array, 'tm', 0, 0, tiled=True)  51.1 us
    all_to_all x2, starting transfers between devices, turned(): return lax.all_to_all(array, 'tm', 0, 0, tiled=True)  16.1 us
    ppermute x3, waiting for transfers between devices, on_device(): lax.ppermute(forward_b, 'space', along(s))  9.63 us
    all_to_all x2, waiting for transfers between devices, turned(): return lax.all_to_all(array, 'tm', 0, 0, tiled=True)  9.26 us
    ppermute x3, waiting for transfers between devices, on_device(): lax.ppermute(p, 'space', along(s))  8.09 us
    ppermute x3, starting transfers between devices, on_device(): lax.ppermute(p, 'space', along(s))  7.58 us
    all_to_all x1, starting transfers between devices, on_device(): lax.all_to_all(spread, 'tm', 0, 0, axis_index_groups=inner, tiled=True)  7.22 us
    ppermute x3, starting transfers between devices, on_device(): chunks.append(lax.ppermute(settled, 'tm', pairs))  5.62 us
  transfers between devices with their start and end apart: 23, of which 12 were waited for; matrix products, arithmetic and copies ran while one was open for 0% of the time, Pallas kernels for 6%

profile of v4, /device:TPU:32, one launch (start us, length us, event | category | flops | bytes accessed | tf_op | source)
XLA Modules:
  0.0 144.6 jit_solution(6783268497774850891)
XLA Ops:
  0.6 1.9 %shard_map.86 = bf16[32,40,128]{2,1,0:T(8,128)(2,1)} custom-call(f32[1024,128]{1,0:T(8,128)} %bitcast.14, f32[2,512]{1,0:T(2,128)} %bitcast.16), custom_call_target="tpu_custom_call" | custom-call | flops 1048576 | bytes 1048576 | tf_op jit(solution)/shard_map/pallas_call | solution.py:358
  2.5 11.4 %all-to-all-start = ((bf16[32,40,128]{2,1,0:T(8,128)(2,1)}), bf16[32,40,128]{2,1,0:T(8,128)(2,1)S(1)}, u32[]{:S(2)}, u32[]{:S(2)}) async-start(bf16[32,40,128]{2,1,0:T(8,128)(2,1)} %shard_map.86), calls=%async_computation | async-start | bytes 655360 | tf_op jit(solution)/shard_map/all_to_all | solution.py:352
  13.9 0.0 copy-start.2
  13.9 0.7 copy-done.2
  14.6 3.6 %shard_map.87.refs_8_ = bf16[8,2,512,512]{3,2,1,0:T(8,128)(2,1)} custom-call(s32[32,32]{1,0:T(8,128)S(1)} %copy-done.2, bf16[2,512,4096]{2,1,0:T(8,128)(2,1)} %bitcast.13), custom_call_target="tpu_custom_call" | custom-call | flops 1048576 | bytes 16777216 | tf_op jit(solution)/shard_map/pallas_call | solution.py:369
  18.3 9.3 %all-to-all-done.got_ref = bf16[32,40,128]{2,1,0:T(8,128)(2,1)S(1)} async-done(((bf16[32,40,128]{2,1,0:T(8,128)(2,1)}), bf16[32,40,128]{2,1,0:T(8,128)(2,1)S(1)}, u32[]{:S(2)}, u32[]{:S(2)}) %all-to-all-start) | async-done | bytes 327712 | tf_op jit(solution)/shard_map/all_to_all | solution.py:352
  27.5 0.4 shard_map.88
  27.9 15.9 %all_to_all.30.forward_ref.refs_0_ = bf16[32,32,128]{2,1,0:T(8,128)(2,1)S(1)} all-to-all(bf16[32,32,128]{2,1,0:T(8,128)(2,1)S(1)} %get-tuple-element.44), channel_id=1, replica_groups=mesh['tm'=32,'space'=8] {'tm'}, dimensions={0} | all-to-all | bytes 524288 | tf_op jit(solution)/shard_map/all_to_all | solution.py:352
  43.8 0.2 copy.11
  44.0 0.0 copy-start.3
  44.0 1.2 shard_map.89
  45.2 4.7 %all-to-all-start.2 = ((bf16[32,32,128]{2,1,0:T(8,128)(2,1)}), bf16[32,32,128]{2,1,0:T(8,128)(2,1)S(1)}, u32[]{:S(2)}, u32[]{:S(2)}) async-start(bf16[32,32,128]{2,1,0:T(8,128)(2,1)} %shard_map.89), calls=%async_computation.2 | async-start | bytes 524288 | tf_op jit(solution)/shard_map/all_to_all | solution.py:352
  49.9 1.6 %collective-permute-start = (bf16[32,32,128]{2,1,0:T(8,128)(2,1)S(1)}, bf16[32,32,128]{2,1,0:T(8,128)(2,1)S(1)}, u32[]{:S(2)}, u32[]{:S(2)}) collective-permute-start(bf16[32,32,128]{2,1,0:T(8,128)(2,1)S(1)} %all_to_all.30.forward_ref.refs_0_), channel_id=1, source_target_pairs={{0,2},{1,3},{2,4},{3,5},{4,6},{5,7},{6,0},{7,1},{8,10},{9,11},{10,... | collective-permute-start | bytes 786440 | tf_op jit(solution)/shard_map/ppermute | solution.py:386
  51.5 1.9 %collective-permute-start.1 = (bf16[32,32,128]{2,1,0:T(8,128)(2,1)S(1)}, bf16[32,32,128]{2,1,0:T(8,128)(2,1)S(1)}, u32[]{:S(2)}, u32[]{:S(2)}) collective-permute-start(bf16[32,32,128]{2,1,0:T(8,128)(2,1)S(1)} %all_to_all.30.forward_ref.refs_0_), channel_id=1, source_target_pairs={{0,6},{1,7},{2,0},{3,1},{4,2},{5,3},{6,4},{7,5},{8,14},{9,15},{10,... | collective-permute-start | bytes 786440 | tf_op jit(solution)/shard_map/ppermute | solution.py:386
  53.4 1.7 %collective-permute-start.2 = (bf16[32,32,128]{2,1,0:T(8,128)(2,1)S(1)}, bf16[32,32,128]{2,1,0:T(8,128)(2,1)S(1)}, u32[]{:S(2)}, u32[]{:S(2)}) collective-permute-start(bf16[32,32,128]{2,1,0:T(8,128)(2,1)S(1)} %all_to_all.30.forward_ref.refs_0_), channel_id=1, source_target_pairs={{0,4},{1,5},{2,6},{3,7},{4,0},{5,1},{6,2},{7,3},{8,12},{9,13},{10,... | collective-permute-start | bytes 786440 | tf_op jit(solution)/shard_map/ppermute | solution.py:386
  55.1 0.0 collective-permute-start.3
  55.1 4.6 %collective-permute-done.refs_1_ = bf16[32,32,128]{2,1,0:T(8,128)(2,1)S(1)} collective-permute-done((bf16[32,32,128]{2,1,0:T(8,128)(2,1)S(1)}, bf16[32,32,128]{2,1,0:T(8,128)(2,1)S(1)}, u32[]{:S(2)}, u32[]{:S(2)}) %collective-permute-start) | collective-permute-done | bytes 262176 | tf_op jit(solution)/shard_map/ppermute | solution.py:386
  59.6 0.0 collective-permute-start.4
  59.6 3.3 %collective-permute-done.1.refs_2_ = bf16[32,32,128]{2,1,0:T(8,128)(2,1)S(1)} collective-permute-done((bf16[32,32,128]{2,1,0:T(8,128)(2,1)S(1)}, bf16[32,32,128]{2,1,0:T(8,128)(2,1)S(1)}, u32[]{:S(2)}, u32[]{:S(2)}) %collective-permute-start.1) | collective-permute-done | bytes 262176 | tf_op jit(solution)/shard_map/ppermute | solution.py:386
  62.9 0.0 collective-permute-start.5
  62.9 1.8 %collective-permute-done.2.refs_3_ = bf16[32,32,128]{2,1,0:T(8,128)(2,1)S(1)} collective-permute-done((bf16[32,32,128]{2,1,0:T(8,128)(2,1)S(1)}, bf16[32,32,128]{2,1,0:T(8,128)(2,1)S(1)}, u32[]{:S(2)}, u32[]{:S(2)}) %collective-permute-start.2) | collective-permute-done | bytes 262176 | tf_op jit(solution)/shard_map/ppermute | solution.py:386
  64.7 0.0 collective-permute-start.6
  64.7 0.0 all-to-all-done.2.got_ref
  64.8 0.6 collective-permute-start.7
  65.3 0.9 collective-permute-done.7
  66.3 0.0 collective-permute-done.3.refs_4_
  66.3 0.0 collective-permute-done.4.refs_5_
  66.3 0.0 collective-permute-done.5.refs_6_
  66.3 0.1 collective-permute-done.6.refs_7_
  66.4 0.3 collective-permute-start.10
  66.7 2.8 %collective-permute-start.8 = (f32[32,128]{1,0:T(8,128)S(1)}, f32[32,128]{1,0:T(8,128)S(1)}, u32[]{:S(2)}, u32[]{:S(2)}) collective-permute-start(f32[32,128]{1,0:T(8,128)S(1)} %add.3.a_ref), channel_id=1, source_target_pairs={{0,2},{1,3},{2,4},{3,5},{4,6},{5,7},{6,0},{7,1},{8,10},{9,11},{10,... | collective-permute-start | bytes 49160 | tf_op jit(solution)/shard_map/ppermute | solution.py:401
  69.5 0.7 collective-permute-start.9
  70.2 2.9 %shard_map.91 = (bf16[4,2,128,512]{3,2,1,0:T(8,128)(2,1)S(1)}, bf16[4,2,128,512]{3,2,1,0:T(8,128)(2,1)S(1)}) custom-call(bf16[32,32,128]{2,1,0:T(8,128)(2,1)} %copy-done, bf16[32,32,128]{2,1,0:T(8,128)(2,1)} %copy-done.5, bf16[32,32,128]{2,1,0:T(8,128)(2,1)} %copy-done.6, bf16[32,32,128]{2,1,0:T(8,128)(2,1)} %copy-done.7, ...), custom_call_target="tpu_custom_call" | custom-call | flops 2147483648 | bytes 12582912 | tf_op jit(solution)/shard_map/pallas_call | solution.py:403
  73.2 0.0 collective-permute-done.10.d_ref
  73.2 0.0 collective-permute-done.8.b_ref
  73.2 0.0 collective-permute-done.9.c_ref
  73.2 0.5 collective-permute-start.14
  73.7 1.5 %collective-permute-start.11 = (bf16[16,128]{1,0:T(8,128)(2,1)S(1)}, bf16[16,128]{1,0:T(8,128)(2,1)S(1)}, u32[]{:S(2)}, u32[]{:S(2)}) collective-permute-start(bf16[16,128]{1,0:T(8,128)(2,1)S(1)} %shard_map.92.refs_0_), channel_id=1, source_target_pairs={{0,64},{8,72},{16,80},{24,88},{32,96},{40,104},{48,112},{56,120},{... | collective-permute-start | bytes 12296 | tf_op jit(solution)/shard_map/ppermute | solution.py:430
  75.2 2.7 %collective-permute-start.12 = (bf16[16,128]{1,0:T(8,128)(2,1)S(1)}, bf16[16,128]{1,0:T(8,128)(2,1)S(1)}, u32[]{:S(2)}, u32[]{:S(2)}) collective-permute-start(bf16[16,128]{1,0:T(8,128)(2,1)S(1)} %shard_map.92.refs_0_), channel_id=1, source_target_pairs={{0,128},{8,136},{16,144},{24,152},{32,160},{40,168},{48,176},{56,1... | collective-permute-start | bytes 12296 | tf_op jit(solution)/shard_map/ppermute | solution.py:430
  77.9 1.4 collective-permute-start.13
  79.4 0.0 collective-permute-done.14.got_ref
  79.4 0.9 shard_map.93
  80.3 0.0 collective-permute-done.11.refs_1_
  80.3 0.1 collective-permute-done.12.refs_2_
  80.3 1.2 collective-permute-done.13.refs_3_
  81.5 0.7 shard_map.94
  82.2 7.2 %all-to-all-start.3 = ((bf16[8,64,128]{2,1,0:T(8,128)(2,1)}), bf16[8,64,128]{2,1,0:T(8,128)(2,1)S(1)}, u32[]{:S(2)}, u32[]{:S(2)}) async-start(bf16[8,64,128]{2,1,0:T(8,128)(2,1)} %shard_map.94), calls=%async_computation.3 | async-start | bytes 262144 | tf_op jit(solution)/shard_map/all_to_all | solution.py:434
  89.4 2.4 %collective-permute-start.15 = (bf16[2,128,512]{2,1,0:T(8,128)(2,1)}, bf16[2,128,512]{2,1,0:T(8,128)(2,1)S(1)}, u32[]{:S(2)}, u32[]{:S(2)}) collective-permute-start(bf16[2,128,512]{2,1,0:T(8,128)(2,1)} %get-tuple-element.66), channel_id=1, source_target_pairs={{0,2},{1,3},{2,4},{3,5},{4,6},{5,7},{6,0},{7,1},{8,10},{9,11},{10,... | collective-permute-start | bytes 786440 | tf_op jit(solution)/shard_map/ppermute | solution.py:432
  91.8 3.7 %collective-permute-start.16 = (bf16[2,128,512]{2,1,0:T(8,128)(2,1)}, bf16[2,128,512]{2,1,0:T(8,128)(2,1)S(1)}, u32[]{:S(2)}, u32[]{:S(2)}) collective-permute-start(bf16[2,128,512]{2,1,0:T(8,128)(2,1)} %get-tuple-element.67), channel_id=1, source_target_pairs={{0,6},{1,7},{2,0},{3,1},{4,2},{5,3},{6,4},{7,5},{8,14},{9,15},{10,... | collective-permute-start | bytes 786440 | tf_op jit(solution)/shard_map/ppermute | solution.py:432
  95.6 1.5 %collective-permute-start.17 = (bf16[2,128,512]{2,1,0:T(8,128)(2,1)S(1)}, bf16[2,128,512]{2,1,0:T(8,128)(2,1)S(1)}, u32[]{:S(2)}, u32[]{:S(2)}) collective-permute-start(bf16[2,128,512]{2,1,0:T(8,128)(2,1)S(1)} %get-tuple-element.68), channel_id=1, source_target_pairs={{0,4},{1,5},{2,6},{3,7},{4,0},{5,1},{6,2},{7,3},{8,12},{9,13},{10,... | collective-permute-start | bytes 786440 | tf_op jit(solution)/shard_map/ppermute | solution.py:432
  97.0 0.0 all-to-all-done.3.got_ref
  97.1 0.8 shard_map.95
  97.8 0.1 collective-permute-start.18
  97.9 0.5 collective-permute-start.19
  98.4 0.8 collective-permute-done.19.got_ref
  99.3 2.8 %collective-permute-done.15.b_ref = bf16[2,128,512]{2,1,0:T(8,128)(2,1)S(1)} collective-permute-done((bf16[2,128,512]{2,1,0:T(8,128)(2,1)}, bf16[2,128,512]{2,1,0:T(8,128)(2,1)S(1)}, u32[]{:S(2)}, u32[]{:S(2)}) %collective-permute-start.15) | collective-permute-done | bytes 262176 | tf_op jit(solution)/shard_map/ppermute | solution.py:432
  102.1 3.5 %collective-permute-done.16.c_ref = bf16[2,128,512]{2,1,0:T(8,128)(2,1)S(1)} collective-permute-done((bf16[2,128,512]{2,1,0:T(8,128)(2,1)}, bf16[2,128,512]{2,1,0:T(8,128)(2,1)S(1)}, u32[]{:S(2)}, u32[]{:S(2)}) %collective-permute-start.16) | collective-permute-done | bytes 262176 | tf_op jit(solution)/shard_map/ppermute | solution.py:432
  105.5 1.8 %collective-permute-done.17.d_ref = bf16[2,128,512]{2,1,0:T(8,128)(2,1)S(1)} collective-permute-done((bf16[2,128,512]{2,1,0:T(8,128)(2,1)S(1)}, bf16[2,128,512]{2,1,0:T(8,128)(2,1)S(1)}, u32[]{:S(2)}, u32[]{:S(2)}) %collective-permute-start.17) | collective-permute-done | bytes 262176 | tf_op jit(solution)/shard_map/ppermute | solution.py:432
  107.4 0.0 collective-permute-done.18.other_ref
  107.4 1.0 shard_map.96
  108.3 20.0 %all_to_all.31.got_ref = bf16[32,32,128]{2,1,0:T(8,128)(2,1)S(1)} all-to-all(bf16[32,32,128]{2,1,0:T(8,128)(2,1)S(1)} %get-tuple-element.77), channel_id=1, replica_groups=mesh['tm'=32,'space'=8] {'tm'}, dimensions={0} | all-to-all | bytes 524288 | tf_op jit(solution)/shard_map/all_to_all | solution.py:352
  128.3 0.3 shard_map.97
  128.6 15.2 %all_to_all.32.following_ref = bf16[32,32,128]{2,1,0:T(8,128)(2,1)S(1)} all-to-all(bf16[32,32,128]{2,1,0:T(8,128)(2,1)S(1)} %shard_map.97), channel_id=1, replica_groups=mesh['tm'=32,'space'=8] {'tm'}, dimensions={0} | all-to-all | bytes 524288 | tf_op jit(solution)/shard_map/all_to_all | solution.py:352
  143.8 0.8 shard_map.98
  (16 shorter events, 0.1 us)
Async XLA Ops:
  2.5 25.0 %all-to-all-start = ((bf16[32,40,128]{2,1,0:T(8,128)(2,1)}), bf16[32,40,128]{2,1,0:T(8,128)(2,1)S(1)}, u32[]{:S(2)}, u32[]{:S(2)}) async-start(bf16[32,40,128]{2,1,0:T(8,128)(2,1)} %shard_map.86), calls=%async_computation | async-start | bytes 655360 | tf_op jit(solution)/shard_map/all_to_all | solution.py:352
  13.9 0.7 copy-start.2
  14.6 29.2 %copy-start.4 = (bf16[1,512,2,512]{3,2,1,0:T(2,128)(2,1)S(1)}, bf16[1,512,2,512]{3,2,1,0:T(2,128)(2,1)}, u32[]{:S(2)}) copy-start(bf16[1,512,2,512]{3,2,1,0:T(2,128)(2,1)} %param.11) | copy-start | bytes 3145732
  43.8 11.2 %copy-start = (bf16[32,32,128]{2,1,0:T(8,128)(2,1)}, bf16[32,32,128]{2,1,0:T(8,128)(2,1)S(1)}, u32[]{:S(2)}) copy-start(bf16[32,32,128]{2,1,0:T(8,128)(2,1)S(1)} %all_to_all.30.forward_ref.refs_0_) | copy-start | bytes 786436
  44.0 20.7 %copy-start.3 = (f32[2,2,128]{2,1,0:T(2,128)S(1)}, f32[2,2,128]{2,1,0:T(2,128)}, u32[]{:S(2)}) copy-start(f32[2,2,128]{2,1,0:T(2,128)} %rhs_ref.1) | copy-start | bytes 6148
  45.2 51.8 %copy-start.1 = (bf16[2,512,512]{2,1,0:T(8,128)(2,1)S(1)}, bf16[2,512,512]{2,1,0:T(8,128)(2,1)}, u32[]{:S(2)}) copy-start(bf16[2,512,512]{2,1,0:T(8,128)(2,1)} %tip_ref.1) | copy-start | bytes 3145732
  45.2 19.5 %all-to-all-start.2 = ((bf16[32,32,128]{2,1,0:T(8,128)(2,1)}), bf16[32,32,128]{2,1,0:T(8,128)(2,1)S(1)}, u32[]{:S(2)}, u32[]{:S(2)}) async-start(bf16[32,32,128]{2,1,0:T(8,128)(2,1)} %shard_map.89), calls=%async_computation.2 | async-start | bytes 524288 | tf_op jit(solution)/shard_map/all_to_all | solution.py:352
  49.9 9.7 %collective-permute-start = (bf16[32,32,128]{2,1,0:T(8,128)(2,1)S(1)}, bf16[32,32,128]{2,1,0:T(8,128)(2,1)S(1)}, u32[]{:S(2)}, u32[]{:S(2)}) collective-permute-start(bf16[32,32,128]{2,1,0:T(8,128)(2,1)S(1)} %all_to_all.30.forward_ref.refs_0_), channel_id=1, source_target_pairs={{0,2},{1,3},{2,4},{3,5},{4,6},{5,7},{6,0},{7,1},{8,10},{9,11},{10,... | collective-permute-start | bytes 786440 | tf_op jit(solution)/shard_map/ppermute | solution.py:386
  51.5 11.4 %collective-permute-start.1 = (bf16[32,32,128]{2,1,0:T(8,128)(2,1)S(1)}, bf16[32,32,128]{2,1,0:T(8,128)(2,1)S(1)}, u32[]{:S(2)}, u32[]{:S(2)}) collective-permute-start(bf16[32,32,128]{2,1,0:T(8,128)(2,1)S(1)} %all_to_all.30.forward_ref.refs_0_), channel_id=1, source_target_pairs={{0,6},{1,7},{2,0},{3,1},{4,2},{5,3},{6,4},{7,5},{8,14},{9,15},{10,... | collective-permute-start | bytes 786440 | tf_op jit(solution)/shard_map/ppermute | solution.py:386
  53.4 11.3 %collective-permute-start.2 = (bf16[32,32,128]{2,1,0:T(8,128)(2,1)S(1)}, bf16[32,32,128]{2,1,0:T(8,128)(2,1)S(1)}, u32[]{:S(2)}, u32[]{:S(2)}) collective-permute-start(bf16[32,32,128]{2,1,0:T(8,128)(2,1)S(1)} %all_to_all.30.forward_ref.refs_0_), channel_id=1, source_target_pairs={{0,4},{1,5},{2,6},{3,7},{4,0},{5,1},{6,2},{7,3},{8,12},{9,13},{10,... | collective-permute-start | bytes 786440 | tf_op jit(solution)/shard_map/ppermute | solution.py:386
  55.1 11.2 %collective-permute-start.3 = (bf16[32,32,128]{2,1,0:T(8,128)(2,1)S(1)}, bf16[32,32,128]{2,1,0:T(8,128)(2,1)}, u32[]{:S(2)}, u32[]{:S(2)}) collective-permute-start(bf16[32,32,128]{2,1,0:T(8,128)(2,1)S(1)} %all_to_all.30.forward_ref.refs_0_), channel_id=1, source_target_pairs={{0,1},{1,0},{2,3},{3,2},{4,5},{5,4},{6,7},{7,6},{8,9},{9,8},{10,11... | collective-permute-start | bytes 786440 | tf_op jit(solution)/shard_map/ppermute | solution.py:398
  59.6 10.6 %copy-start.5 = (bf16[32,32,128]{2,1,0:T(8,128)(2,1)}, bf16[32,32,128]{2,1,0:T(8,128)(2,1)S(1)}, u32[]{:S(2)}) copy-start(bf16[32,32,128]{2,1,0:T(8,128)(2,1)S(1)} %collective-permute-done.refs_1_) | copy-start | bytes 786436
  59.6 6.7 %collective-permute-start.4 = (bf16[32,32,128]{2,1,0:T(8,128)(2,1)S(1)}, bf16[32,32,128]{2,1,0:T(8,128)(2,1)}, u32[]{:S(2)}, u32[]{:S(2)}) collective-permute-start(bf16[32,32,128]{2,1,0:T(8,128)(2,1)S(1)} %collective-permute-done.refs_1_), channel_id=1, source_target_pairs={{0,1},{1,0},{2,3},{3,2},{4,5},{5,4},{6,7},{7,6},{8,9},{9,8},{10,11... | collective-permute-start | bytes 786440 | tf_op jit(solution)/shard_map/ppermute | solution.py:398
  62.9 7.3 %copy-start.6 = (bf16[32,32,128]{2,1,0:T(8,128)(2,1)}, bf16[32,32,128]{2,1,0:T(8,128)(2,1)S(1)}, u32[]{:S(2)}) copy-start(bf16[32,32,128]{2,1,0:T(8,128)(2,1)S(1)} %collective-permute-done.1.refs_2_) | copy-start | bytes 786436
  62.9 3.4 %collective-permute-start.5 = (bf16[32,32,128]{2,1,0:T(8,128)(2,1)S(1)}, bf16[32,32,128]{2,1,0:T(8,128)(2,1)}, u32[]{:S(2)}, u32[]{:S(2)}) collective-permute-start(bf16[32,32,128]{2,1,0:T(8,128)(2,1)S(1)} %collective-permute-done.1.refs_2_), channel_id=1, source_target_pairs={{0,1},{1,0},{2,3},{3,2},{4,5},{5,4},{6,7},{7,6},{8,9},{9,8},{10,11... | collective-permute-start | bytes 786440 | tf_op jit(solution)/shard_map/ppermute | solution.py:398
  64.7 5.5 %copy-start.7 = (bf16[32,32,128]{2,1,0:T(8,128)(2,1)}, bf16[32,32,128]{2,1,0:T(8,128)(2,1)S(1)}, u32[]{:S(2)}) copy-start(bf16[32,32,128]{2,1,0:T(8,128)(2,1)S(1)} %collective-permute-done.2.refs_3_) | copy-start | bytes 786436
  64.7 1.7 %collective-permute-start.6 = (bf16[32,32,128]{2,1,0:T(8,128)(2,1)S(1)}, bf16[32,32,128]{2,1,0:T(8,128)(2,1)}, u32[]{:S(2)}, u32[]{:S(2)}) collective-permute-start(bf16[32,32,128]{2,1,0:T(8,128)(2,1)S(1)} %collective-permute-done.2.refs_3_), channel_id=1, source_target_pairs={{0,1},{1,0},{2,3},{3,2},{4,5},{5,4},{6,7},{7,6},{8,9},{9,8},{10,11... | collective-permute-start | bytes 786440 | tf_op jit(solution)/shard_map/ppermute | solution.py:398
  64.8 1.5 %collective-permute-start.7 = (f32[32,128]{1,0:T(8,128)S(1)}, f32[32,128]{1,0:T(8,128)S(1)}, u32[]{:S(2)}, u32[]{:S(2)}) collective-permute-start(f32[32,128]{1,0:T(8,128)S(1)} %shard_map.90), channel_id=1, source_target_pairs={{0,1},{1,0},{2,3},{3,2},{4,5},{5,4},{6,7},{7,6},{8,9},{9,8},{10,11... | collective-permute-start | bytes 49160 | tf_op jit(solution)/shard_map/ppermute | solution.py:399
  66.4 6.8 %collective-permute-start.10 = (f32[32,128]{1,0:T(8,128)S(1)}, f32[32,128]{1,0:T(8,128)S(1)}, u32[]{:S(2)}, u32[]{:S(2)}) collective-permute-start(f32[32,128]{1,0:T(8,128)S(1)} %add.3.a_ref), channel_id=1, source_target_pairs={{0,4},{1,5},{2,6},{3,7},{4,0},{5,1},{6,2},{7,3},{8,12},{9,13},{10,... | collective-permute-start | bytes 49160 | tf_op jit(solution)/shard_map/ppermute | solution.py:401
  66.7 6.5 %collective-permute-start.8 = (f32[32,128]{1,0:T(8,128)S(1)}, f32[32,128]{1,0:T(8,128)S(1)}, u32[]{:S(2)}, u32[]{:S(2)}) collective-permute-start(f32[32,128]{1,0:T(8,128)S(1)} %add.3.a_ref), channel_id=1, source_target_pairs={{0,2},{1,3},{2,4},{3,5},{4,6},{5,7},{6,0},{7,1},{8,10},{9,11},{10,... | collective-permute-start | bytes 49160 | tf_op jit(solution)/shard_map/ppermute | solution.py:401
  69.5 3.7 %collective-permute-start.9 = (f32[32,128]{1,0:T(8,128)S(1)}, f32[32,128]{1,0:T(8,128)S(1)}, u32[]{:S(2)}, u32[]{:S(2)}) collective-permute-start(f32[32,128]{1,0:T(8,128)S(1)} %add.3.a_ref), channel_id=1, source_target_pairs={{0,6},{1,7},{2,0},{3,1},{4,2},{5,3},{6,4},{7,5},{8,14},{9,15},{10,... | collective-permute-start | bytes 49160 | tf_op jit(solution)/shard_map/ppermute | solution.py:401
  73.2 6.1 %collective-permute-start.14 = (bf16[4,2,128,512]{3,2,1,0:T(8,128)(2,1)S(1)}, bf16[4,2,128,512]{3,2,1,0:T(8,128)(2,1)S(1)}, u32[]{:S(2)}, u32[]{:S(2)}) collective-permute-start(bf16[4,2,128,512]{3,2,1,0:T(8,128)(2,1)S(1)} %get-tuple-element.60), channel_id=1, source_target_pairs={{0,1},{1,0},{2,3},{3,2},{4,5},{5,4},{6,7},{7,6},{8,9},{9,8},{10,11... | collective-permute-start | bytes 3145736 | tf_op jit(solution)/shard_map/ppermute | solution.py:422
  73.7 6.5 %collective-permute-start.11 = (bf16[16,128]{1,0:T(8,128)(2,1)S(1)}, bf16[16,128]{1,0:T(8,128)(2,1)S(1)}, u32[]{:S(2)}, u32[]{:S(2)}) collective-permute-start(bf16[16,128]{1,0:T(8,128)(2,1)S(1)} %shard_map.92.refs_0_), channel_id=1, source_target_pairs={{0,64},{8,72},{16,80},{24,88},{32,96},{40,104},{48,112},{56,120},{... | collective-permute-start | bytes 12296 | tf_op jit(solution)/shard_map/ppermute | solution.py:430
  75.2 5.1 %collective-permute-start.12 = (bf16[16,128]{1,0:T(8,128)(2,1)S(1)}, bf16[16,128]{1,0:T(8,128)(2,1)S(1)}, u32[]{:S(2)}, u32[]{:S(2)}) collective-permute-start(bf16[16,128]{1,0:T(8,128)(2,1)S(1)} %shard_map.92.refs_0_), channel_id=1, source_target_pairs={{0,128},{8,136},{16,144},{24,152},{32,160},{40,168},{48,176},{56,1... | collective-permute-start | bytes 12296 | tf_op jit(solution)/shard_map/ppermute | solution.py:430
  77.9 3.6 %collective-permute-start.13 = (bf16[16,128]{1,0:T(8,128)(2,1)S(1)}, bf16[16,128]{1,0:T(8,128)(2,1)S(1)}, u32[]{:S(2)}, u32[]{:S(2)}) collective-permute-start(bf16[16,128]{1,0:T(8,128)(2,1)S(1)} %shard_map.92.refs_0_), channel_id=1, source_target_pairs={{0,192},{8,200},{16,208},{24,216},{32,224},{40,232},{48,240},{56,2... | collective-permute-start | bytes 12296 | tf_op jit(solution)/shard_map/ppermute | solution.py:430
  82.2 14.8 %all-to-all-start.3 = ((bf16[8,64,128]{2,1,0:T(8,128)(2,1)}), bf16[8,64,128]{2,1,0:T(8,128)(2,1)S(1)}, u32[]{:S(2)}, u32[]{:S(2)}) async-start(bf16[8,64,128]{2,1,0:T(8,128)(2,1)} %shard_map.94), calls=%async_computation.3 | async-start | bytes 262144 | tf_op jit(solution)/shard_map/all_to_all | solution.py:434
  89.4 12.6 %collective-permute-start.15 = (bf16[2,128,512]{2,1,0:T(8,128)(2,1)}, bf16[2,128,512]{2,1,0:T(8,128)(2,1)S(1)}, u32[]{:S(2)}, u32[]{:S(2)}) collective-permute-start(bf16[2,128,512]{2,1,0:T(8,128)(2,1)} %get-tuple-element.66), channel_id=1, source_target_pairs={{0,2},{1,3},{2,4},{3,5},{4,6},{5,7},{6,0},{7,1},{8,10},{9,11},{10,... | collective-permute-start | bytes 786440 | tf_op jit(solution)/shard_map/ppermute | solution.py:432
  91.8 13.7 %collective-permute-start.16 = (bf16[2,128,512]{2,1,0:T(8,128)(2,1)}, bf16[2,128,512]{2,1,0:T(8,128)(2,1)S(1)}, u32[]{:S(2)}, u32[]{:S(2)}) collective-permute-start(bf16[2,128,512]{2,1,0:T(8,128)(2,1)} %get-tuple-element.67), channel_id=1, source_target_pairs={{0,6},{1,7},{2,0},{3,1},{4,2},{5,3},{6,4},{7,5},{8,14},{9,15},{10,... | collective-permute-start | bytes 786440 | tf_op jit(solution)/shard_map/ppermute | solution.py:432
  95.6 11.8 %collective-permute-start.17 = (bf16[2,128,512]{2,1,0:T(8,128)(2,1)S(1)}, bf16[2,128,512]{2,1,0:T(8,128)(2,1)S(1)}, u32[]{:S(2)}, u32[]{:S(2)}) collective-permute-start(bf16[2,128,512]{2,1,0:T(8,128)(2,1)S(1)} %get-tuple-element.68), channel_id=1, source_target_pairs={{0,4},{1,5},{2,6},{3,7},{4,0},{5,1},{6,2},{7,3},{8,12},{9,13},{10,... | collective-permute-start | bytes 786440 | tf_op jit(solution)/shard_map/ppermute | solution.py:432
  97.8 9.5 %collective-permute-start.18 = (bf16[512,128]{1,0:T(8,128)(2,1)S(1)}, bf16[512,128]{1,0:T(8,128)(2,1)S(1)}, u32[]{:S(2)}, u32[]{:S(2)}) collective-permute-start(bf16[512,128]{1,0:T(8,128)(2,1)S(1)} %get-tuple-element.73.mine_ref), channel_id=1, source_target_pairs={{0,1},{1,0},{2,3},{3,2},{4,5},{5,4},{6,7},{7,6},{8,9},{9,8},{10,11... | collective-permute-start | bytes 393224 | tf_op jit(solution)/shard_map/ppermute | solution.py:449
  97.9 1.3 collective-permute-start.19

commit v5 on v4

--- a/solution.py
+++ b/solution.py
@@ -31,37 +31,39 @@
     return jax.ShapeDtypeStruct(dims, kind)
 
 
-def pack_kernel(side_hbm, rate_hbm, out_ref, side_ref, rate_ref, sems):
+def pack_kernel(side_hbm, rate_hbm, out_hbm, side_ref, rate_ref, out_ref, sems):
     blocks, _, lanes = out_ref.shape
     count = side_ref.shape[0] // 2
     per = count // blocks
-    groups = 4
-    copies = [pltpu.make_async_copy(rate_hbm, rate_ref, sems.at[groups])]
+    groups, some = count // lanes, lanes // per
+    copies = [pltpu.make_async_copy(rate_hbm, rate_ref, sems.at[2 * groups])]
     for g in range(groups):
-        rows = pl.ds(g * (2 * count // groups), 2 * count // groups)
+        rows = pl.ds(g * 2 * lanes, 2 * lanes)
         copies.append(pltpu.make_async_copy(side_hbm.at[rows], side_ref.at[rows], sems.at[g]))
     for copy in copies:
         copy.start()
     copies[0].wait()
-    for g in range(groups):
-        copies[1 + g].wait()
-        first, some = g * (blocks // groups), blocks // groups
-        for h in range(2):
-            rows = side_ref[pl.ds(2 * first * per + h, some * per, stride=2), :]
-            out_ref[first : first + some, h * per : (h + 1) * per, :] = rows.reshape(
-                some, per, lanes
-            ).astype(BF)
     rate = rate_ref[...]
     high = rate.astype(BF).astype(F32)
     middle = (rate - high).astype(BF).astype(F32)
     low = rate - high - middle
     terms = jnp.concatenate([high, middle, low, jnp.zeros_like(low)], axis=0)
-    shared = lanes // per
-    for group in range(count // lanes):
-        part = terms[:, group * lanes : (group + 1) * lanes].astype(BF)
-        out_ref[group * shared : (group + 1) * shared, 2 * per :, :] = jnp.broadcast_to(
-            part[None], (shared,) + part.shape
-        )
+    back = []
+    for g in range(groups):
+        copies[1 + g].wait()
+        here = slice(g * some, (g + 1) * some)
+        for h in range(2):
+            rows = side_ref[pl.ds(2 * g * lanes + h, lanes, stride=2), :]
+            out_ref[here, h * per : (h + 1) * per, :] = rows.reshape(some, per, lanes).astype(BF)
+        part = terms[:, g * lanes : (g + 1) * lanes].astype(BF)
+        out_ref[here, 2 * per :, :] = jnp.broadcast_to(part[None], (some,) + part.shape)
+        span = pl.ds(g * some, some)
+        back.append(
+            pltpu.make_async_copy(out_ref.at[span], out_hbm.at[span], sems.at[groups + g])
+        )
+        back[g].start()
+    for copy in back:
+        copy.wait()
 
 
 def forward_kernel(got_ref, out_ref, rate_ref, rows_ref, turn_ref):
@@ -357,13 +359,15 @@
     far = pl.BlockSpec(memory_space=pltpu.HBM)
     packed = call(
         pack_kernel,
-        shape((times, 2 * per + 8, lanes), BF),
+        pltpu.HBM((times, 2 * per + 8, lanes), BF),
         [
             pltpu.VMEM((2 * count, lanes), F32),
             pltpu.VMEM((2, count), F32),
-            pltpu.SemaphoreType.DMA((5,)),
+            pltpu.VMEM((times, 2 * per + 8, lanes), BF),
+            pltpu.SemaphoreType.DMA((9,)),
         ],
         in_specs=[far, far],
+        out_specs=far,
     )(distant(right_side.reshape(2 * count, lanes)), distant(jnp.transpose(carry_rate[0])))
     packed, tile_mask = lax.optimization_barrier((packed, tile_mask))
     held = call(
@@ -416,9 +420,9 @@
         flops=1 << 31,
         moved=12 * MIB,
     )(*[distant(p) for p in pieces], distant(held))
+    send, fixed = lax.optimization_barrier((send, fixed))
     chunk = (sums.shape[0] // 2, lanes)
     settled = call(settle_kernel, shape(chunk, BF))(*fixed)
-    send, settled = lax.optimization_barrier((send, settled))
     parts = call(add_kernel, (shape(part, BF),) * 4, vmem=8)(keep, lax.ppermute(send, "space", near))
 
     line = 8

time: 145 us -> 145 us (level)
  waiting for transfers between devices: 30.2 us -> 32.9 us
  starting transfers between devices: 47.1 us -> 45.1 us
    ppermute x3, waiting for transfers between devices: 1.29 us -> 3.06 us  [on_device(): chunks.append(lax.ppermute(settled, 'tm', pairs))]
  transfers between devices with their start and end apart: 23 -> 23, of which waited for: 12 -> 13; matrix products, arithmetic and copies ran while one was open for 0% -> 0% of each run, Pallas kernels for 6% -> 6%
where the time goes in v5:
time: 145 us
  blocking collectives  50.5 us (35%)
  starting transfers between devices  45.1 us (31%)
  waiting for transfers between devices  32.9 us (23%)
  Pallas kernels  14.5 us (10%)
    all_to_all x3, blocking collectives, turned(): return lax.all_to_all(array, 'tm', 0, 0, tiled=True)  50.5 us
    all_to_all x2, starting transfers between devices, turned(): return lax.all_to_all(array, 'tm', 0, 0, tiled=True)  16.1 us
    all_to_all x2, waiting for transfers between devices, turned(): return lax.all_to_all(array, 'tm', 0, 0, tiled=True)  9.24 us
    ppermute x3, waiting for transfers between devices, on_device(): lax.ppermute(forward_b, 'space', along(s))  9.04 us
    ppermute x3, waiting for transfers between devices, on_device(): lax.ppermute(p, 'space', along(s))  7.6 us
    ppermute x3, starting transfers between devices, on_device(): lax.ppermute(p, 'space', along(s))  7.22 us
    all_to_all x1, starting transfers between devices, on_device(): lax.all_to_all(spread, 'tm', 0, 0, axis_index_groups=inner, tiled=True)  7.21 us
    ppermute x3, starting transfers between devices, on_device(): lax.ppermute(forward_b, 'space', along(s))  5.14 us
  transfers between devices with their start and end apart: 23, of which 13 were waited for; matrix products, arithmetic and copies ran while one was open for 0% of the time, Pallas kernels for 6%

profile of v5, /device:TPU:32, one launch (start us, length us, event | category | flops | bytes accessed | tf_op | source)
XLA Modules:
  0.0 144.7 jit_solution(5429748743696489659)
XLA Ops:
  0.6 1.8 %shard_map.86 = bf16[32,40,128]{2,1,0:T(8,128)(2,1)} custom-call(f32[1024,128]{1,0:T(8,128)} %bitcast.14, f32[2,512]{1,0:T(2,128)} %bitcast.16), custom_call_target="tpu_custom_call" | custom-call | flops 1048576 | bytes 1048576 | tf_op jit(solution)/shard_map/pallas_call | solution.py:360
  2.5 11.4 %all-to-all-start = ((bf16[32,40,128]{2,1,0:T(8,128)(2,1)}), bf16[32,40,128]{2,1,0:T(8,128)(2,1)S(1)}, u32[]{:S(2)}, u32[]{:S(2)}) async-start(bf16[32,40,128]{2,1,0:T(8,128)(2,1)} %shard_map.86), calls=%async_computation | async-start | bytes 655360 | tf_op jit(solution)/shard_map/all_to_all | solution.py:354
  13.8 0.0 copy-start.2
  13.9 0.7 copy-done.2
  14.6 3.6 %shard_map.87.refs_8_ = bf16[8,2,512,512]{3,2,1,0:T(8,128)(2,1)} custom-call(s32[32,32]{1,0:T(8,128)S(1)} %copy-done.2, bf16[2,512,4096]{2,1,0:T(8,128)(2,1)} %bitcast.13), custom_call_target="tpu_custom_call" | custom-call | flops 1048576 | bytes 16777216 | tf_op jit(solution)/shard_map/pallas_call | solution.py:373
  18.2 9.2 %all-to-all-done.got_ref = bf16[32,40,128]{2,1,0:T(8,128)(2,1)S(1)} async-done(((bf16[32,40,128]{2,1,0:T(8,128)(2,1)}), bf16[32,40,128]{2,1,0:T(8,128)(2,1)S(1)}, u32[]{:S(2)}, u32[]{:S(2)}) %all-to-all-start) | async-done | bytes 327712 | tf_op jit(solution)/shard_map/all_to_all | solution.py:354
  27.4 0.4 shard_map.88
  27.8 15.9 %all_to_all.30.forward_ref.refs_0_ = bf16[32,32,128]{2,1,0:T(8,128)(2,1)S(1)} all-to-all(bf16[32,32,128]{2,1,0:T(8,128)(2,1)S(1)} %get-tuple-element.47), channel_id=1, replica_groups=mesh['tm'=32,'space'=8] {'tm'}, dimensions={0} | all-to-all | bytes 524288 | tf_op jit(solution)/shard_map/all_to_all | solution.py:354
  43.8 0.2 copy.11
  43.9 0.0 copy-start.3
  43.9 1.2 shard_map.89
  45.1 4.7 %all-to-all-start.2 = ((bf16[32,32,128]{2,1,0:T(8,128)(2,1)}), bf16[32,32,128]{2,1,0:T(8,128)(2,1)S(1)}, u32[]{:S(2)}, u32[]{:S(2)}) async-start(bf16[32,32,128]{2,1,0:T(8,128)(2,1)} %shard_map.89), calls=%async_computation.2 | async-start | bytes 524288 | tf_op jit(solution)/shard_map/all_to_all | solution.py:354
  49.8 3.1 %collective-permute-start.2 = (bf16[32,32,128]{2,1,0:T(8,128)(2,1)S(1)}, bf16[32,32,128]{2,1,0:T(8,128)(2,1)S(1)}, u32[]{:S(2)}, u32[]{:S(2)}) collective-permute-start(bf16[32,32,128]{2,1,0:T(8,128)(2,1)S(1)} %all_to_all.30.forward_ref.refs_0_), channel_id=1, source_target_pairs={{0,4},{1,5},{2,6},{3,7},{4,0},{5,1},{6,2},{7,3},{8,12},{9,13},{10,... | collective-permute-start | bytes 786440 | tf_op jit(solution)/shard_map/ppermute | solution.py:390
  53.0 1.1 collective-permute-start.1
  54.1 0.9 collective-permute-start
  55.0 0.0 collective-permute-start.3
  55.0 5.4 %collective-permute-done.2.refs_3_ = bf16[32,32,128]{2,1,0:T(8,128)(2,1)S(1)} collective-permute-done((bf16[32,32,128]{2,1,0:T(8,128)(2,1)S(1)}, bf16[32,32,128]{2,1,0:T(8,128)(2,1)S(1)}, u32[]{:S(2)}, u32[]{:S(2)}) %collective-permute-start.2) | collective-permute-done | bytes 262176 | tf_op jit(solution)/shard_map/ppermute | solution.py:390
  60.4 0.0 collective-permute-start.6
  60.4 3.7 %collective-permute-done.1.refs_2_ = bf16[32,32,128]{2,1,0:T(8,128)(2,1)S(1)} collective-permute-done((bf16[32,32,128]{2,1,0:T(8,128)(2,1)S(1)}, bf16[32,32,128]{2,1,0:T(8,128)(2,1)S(1)}, u32[]{:S(2)}, u32[]{:S(2)}) %collective-permute-start.1) | collective-permute-done | bytes 262176 | tf_op jit(solution)/shard_map/ppermute | solution.py:390
  64.0 0.0 collective-permute-start.5
  64.0 0.0 collective-permute-done.refs_1_
  64.1 0.5 collective-permute-start.4
  64.6 0.0 all-to-all-done.2.got_ref
  64.6 0.2 collective-permute-start.7
  64.8 1.2 collective-permute-done.7
  66.0 0.0 collective-permute-done.3.refs_4_
  66.0 0.0 collective-permute-done.6.refs_7_
  66.0 0.0 collective-permute-done.5.refs_6_
  66.0 0.1 collective-permute-done.4.refs_5_
  66.1 1.7 %collective-permute-start.10 = (f32[32,128]{1,0:T(8,128)S(1)}, f32[32,128]{1,0:T(8,128)S(1)}, u32[]{:S(2)}, u32[]{:S(2)}) collective-permute-start(f32[32,128]{1,0:T(8,128)S(1)} %add.3.a_ref), channel_id=1, source_target_pairs={{0,4},{1,5},{2,6},{3,7},{4,0},{5,1},{6,2},{7,3},{8,12},{9,13},{10,... | collective-permute-start | bytes 49160 | tf_op jit(solution)/shard_map/ppermute | solution.py:405
  67.8 1.5 %collective-permute-start.9 = (f32[32,128]{1,0:T(8,128)S(1)}, f32[32,128]{1,0:T(8,128)S(1)}, u32[]{:S(2)}, u32[]{:S(2)}) collective-permute-start(f32[32,128]{1,0:T(8,128)S(1)} %add.3.a_ref), channel_id=1, source_target_pairs={{0,6},{1,7},{2,0},{3,1},{4,2},{5,3},{6,4},{7,5},{8,14},{9,15},{10,... | collective-permute-start | bytes 49160 | tf_op jit(solution)/shard_map/ppermute | solution.py:405
  69.3 0.5 collective-permute-start.8
  69.8 2.9 %shard_map.91 = (bf16[4,2,128,512]{3,2,1,0:T(8,128)(2,1)S(1)}, bf16[4,2,128,512]{3,2,1,0:T(8,128)(2,1)S(1)}) custom-call(bf16[32,32,128]{2,1,0:T(8,128)(2,1)} %copy-done, bf16[32,32,128]{2,1,0:T(8,128)(2,1)} %copy-done.7, bf16[32,32,128]{2,1,0:T(8,128)(2,1)} %copy-done.6, bf16[32,32,128]{2,1,0:T(8,128)(2,1)} %copy-done.5, ...), custom_call_target="tpu_custom_call" | custom-call | flops 2147483648 | bytes 12582912 | tf_op jit(solution)/shard_map/pallas_call | solution.py:407
  72.8 0.0 collective-permute-done.10.d_ref
  72.8 0.0 collective-permute-done.9.c_ref
  72.8 1.5 %collective-permute-done.8.b_ref = f32[32,128]{1,0:T(8,128)S(1)} collective-permute-done((f32[32,128]{1,0:T(8,128)S(1)}, f32[32,128]{1,0:T(8,128)S(1)}, u32[]{:S(2)}, u32[]{:S(2)}) %collective-permute-start.8) | collective-permute-done | bytes 16416 | tf_op jit(solution)/shard_map/ppermute | solution.py:405
  74.3 0.0 collective-permute-start.14
  74.3 2.8 %collective-permute-start.13 = (bf16[16,128]{1,0:T(8,128)(2,1)S(1)}, bf16[16,128]{1,0:T(8,128)(2,1)S(1)}, u32[]{:S(2)}, u32[]{:S(2)}) collective-permute-start(bf16[16,128]{1,0:T(8,128)(2,1)S(1)} %shard_map.92.refs_0_), channel_id=1, source_target_pairs={{0,192},{8,200},{16,208},{24,216},{32,224},{40,232},{48,240},{56,2... | collective-permute-start | bytes 12296 | tf_op jit(solution)/shard_map/ppermute | solution.py:434
  77.1 0.8 collective-permute-start.12
  77.9 0.9 collective-permute-start.11
  78.8 0.0 collective-permute-done.14.got_ref
  78.8 0.9 shard_map.93
  79.7 0.0 collective-permute-done.13.refs_3_
  79.7 2.5 %collective-permute-done.12.refs_2_ = bf16[16,128]{1,0:T(8,128)(2,1)S(1)} collective-permute-done((bf16[16,128]{1,0:T(8,128)(2,1)S(1)}, bf16[16,128]{1,0:T(8,128)(2,1)S(1)}, u32[]{:S(2)}, u32[]{:S(2)}) %collective-permute-start.12) | collective-permute-done | bytes 4128 | tf_op jit(solution)/shard_map/ppermute | solution.py:434
  82.2 0.5 collective-permute-done.11.refs_1_
  82.7 0.7 shard_map.94
  83.4 7.2 %all-to-all-start.3 = ((bf16[8,64,128]{2,1,0:T(8,128)(2,1)}), bf16[8,64,128]{2,1,0:T(8,128)(2,1)S(1)}, u32[]{:S(2)}, u32[]{:S(2)}) async-start(bf16[8,64,128]{2,1,0:T(8,128)(2,1)} %shard_map.94), calls=%async_computation.3 | async-start | bytes 262144 | tf_op jit(solution)/shard_map/all_to_all | solution.py:438
  90.6 1.9 %collective-permute-start.15 = (bf16[2,128,512]{2,1,0:T(8,128)(2,1)}, bf16[2,128,512]{2,1,0:T(8,128)(2,1)S(1)}, u32[]{:S(2)}, u32[]{:S(2)}) collective-permute-start(bf16[2,128,512]{2,1,0:T(8,128)(2,1)} %get-tuple-element.72), channel_id=1, source_target_pairs={{0,2},{1,3},{2,4},{3,5},{4,6},{5,7},{6,0},{7,1},{8,10},{9,11},{10,... | collective-permute-start | bytes 786440 | tf_op jit(solution)/shard_map/ppermute | solution.py:436
  92.5 3.8 %collective-permute-start.16 = (bf16[2,128,512]{2,1,0:T(8,128)(2,1)}, bf16[2,128,512]{2,1,0:T(8,128)(2,1)S(1)}, u32[]{:S(2)}, u32[]{:S(2)}) collective-permute-start(bf16[2,128,512]{2,1,0:T(8,128)(2,1)} %get-tuple-element.73), channel_id=1, source_target_pairs={{0,6},{1,7},{2,0},{3,1},{4,2},{5,3},{6,4},{7,5},{8,14},{9,15},{10,... | collective-permute-start | bytes 786440 | tf_op jit(solution)/shard_map/ppermute | solution.py:436
  96.4 1.5 %collective-permute-start.17 = (bf16[2,128,512]{2,1,0:T(8,128)(2,1)S(1)}, bf16[2,128,512]{2,1,0:T(8,128)(2,1)S(1)}, u32[]{:S(2)}, u32[]{:S(2)}) collective-permute-start(bf16[2,128,512]{2,1,0:T(8,128)(2,1)S(1)} %get-tuple-element.74), channel_id=1, source_target_pairs={{0,4},{1,5},{2,6},{3,7},{4,0},{5,1},{6,2},{7,3},{8,12},{9,13},{10,... | collective-permute-start | bytes 786440 | tf_op jit(solution)/shard_map/ppermute | solution.py:436
  97.8 0.4 all-to-all-done.3.got_ref
  98.2 0.8 shard_map.95
  99.0 0.1 collective-permute-start.18
  99.1 0.5 collective-permute-start.19
  99.6 0.8 collective-permute-done.19.got_ref
  100.4 2.5 %collective-permute-done.15.b_ref = bf16[2,128,512]{2,1,0:T(8,128)(2,1)S(1)} collective-permute-done((bf16[2,128,512]{2,1,0:T(8,128)(2,1)}, bf16[2,128,512]{2,1,0:T(8,128)(2,1)S(1)}, u32[]{:S(2)}, u32[]{:S(2)}) %collective-permute-start.15) | collective-permute-done | bytes 262176 | tf_op jit(solution)/shard_map/ppermute | solution.py:436
  102.9 3.3 %collective-permute-done.16.c_ref = bf16[2,128,512]{2,1,0:T(8,128)(2,1)S(1)} collective-permute-done((bf16[2,128,512]{2,1,0:T(8,128)(2,1)}, bf16[2,128,512]{2,1,0:T(8,128)(2,1)S(1)}, u32[]{:S(2)}, u32[]{:S(2)}) %collective-permute-start.16) | collective-permute-done | bytes 262176 | tf_op jit(solution)/shard_map/ppermute | solution.py:436
  106.2 1.8 %collective-permute-done.17.d_ref = bf16[2,128,512]{2,1,0:T(8,128)(2,1)S(1)} collective-permute-done((bf16[2,128,512]{2,1,0:T(8,128)(2,1)S(1)}, bf16[2,128,512]{2,1,0:T(8,128)(2,1)S(1)}, u32[]{:S(2)}, u32[]{:S(2)}) %collective-permute-start.17) | collective-permute-done | bytes 262176 | tf_op jit(solution)/shard_map/ppermute | solution.py:436
  108.0 0.0 collective-permute-done.18.other_ref
  108.0 1.0 shard_map.96
  109.0 19.2 %all_to_all.31.got_ref = bf16[32,32,128]{2,1,0:T(8,128)(2,1)S(1)} all-to-all(bf16[32,32,128]{2,1,0:T(8,128)(2,1)S(1)} %get-tuple-element.83), channel_id=1, replica_groups=mesh['tm'=32,'space'=8] {'tm'}, dimensions={0} | all-to-all | bytes 524288 | tf_op jit(solution)/shard_map/all_to_all | solution.py:354
  128.2 0.3 shard_map.97
  128.5 15.3 %all_to_all.32.following_ref = bf16[32,32,128]{2,1,0:T(8,128)(2,1)S(1)} all-to-all(bf16[32,32,128]{2,1,0:T(8,128)(2,1)S(1)} %shard_map.97), channel_id=1, replica_groups=mesh['tm'=32,'space'=8] {'tm'}, dimensions={0} | all-to-all | bytes 524288 | tf_op jit(solution)/shard_map/all_to_all | solution.py:354
  143.8 0.8 shard_map.98
  (16 shorter events, 0.1 us)
Async XLA Ops:
  2.5 25.0 %all-to-all-start = ((bf16[32,40,128]{2,1,0:T(8,128)(2,1)}), bf16[32,40,128]{2,1,0:T(8,128)(2,1)S(1)}, u32[]{:S(2)}, u32[]{:S(2)}) async-start(bf16[32,40,128]{2,1,0:T(8,128)(2,1)} %shard_map.86), calls=%async_computation | async-start | bytes 655360 | tf_op jit(solution)/shard_map/all_to_all | solution.py:354
  13.8 0.7 copy-start.2
  14.6 29.2 %copy-start.4 = (bf16[1,512,2,512]{3,2,1,0:T(2,128)(2,1)S(1)}, bf16[1,512,2,512]{3,2,1,0:T(2,128)(2,1)}, u32[]{:S(2)}) copy-start(bf16[1,512,2,512]{3,2,1,0:T(2,128)(2,1)} %param.11) | copy-start | bytes 3145732
  43.8 11.2 %copy-start = (bf16[32,32,128]{2,1,0:T(8,128)(2,1)}, bf16[32,32,128]{2,1,0:T(8,128)(2,1)S(1)}, u32[]{:S(2)}) copy-start(bf16[32,32,128]{2,1,0:T(8,128)(2,1)S(1)} %all_to_all.30.forward_ref.refs_0_) | copy-start | bytes 786436
  43.9 20.6 %copy-start.3 = (f32[2,2,128]{2,1,0:T(2,128)S(1)}, f32[2,2,128]{2,1,0:T(2,128)}, u32[]{:S(2)}) copy-start(f32[2,2,128]{2,1,0:T(2,128)} %rhs_ref.1) | copy-start | bytes 6148
  45.1 53.1 %copy-start.1 = (bf16[2,512,512]{2,1,0:T(8,128)(2,1)S(1)}, bf16[2,512,512]{2,1,0:T(8,128)(2,1)}, u32[]{:S(2)}) copy-start(bf16[2,512,512]{2,1,0:T(8,128)(2,1)} %tip_ref.1) | copy-start | bytes 3145732
  45.1 19.4 %all-to-all-start.2 = ((bf16[32,32,128]{2,1,0:T(8,128)(2,1)}), bf16[32,32,128]{2,1,0:T(8,128)(2,1)S(1)}, u32[]{:S(2)}, u32[]{:S(2)}) async-start(bf16[32,32,128]{2,1,0:T(8,128)(2,1)} %shard_map.89), calls=%async_computation.2 | async-start | bytes 524288 | tf_op jit(solution)/shard_map/all_to_all | solution.py:354
  49.8 10.5 %collective-permute-start.2 = (bf16[32,32,128]{2,1,0:T(8,128)(2,1)S(1)}, bf16[32,32,128]{2,1,0:T(8,128)(2,1)S(1)}, u32[]{:S(2)}, u32[]{:S(2)}) collective-permute-start(bf16[32,32,128]{2,1,0:T(8,128)(2,1)S(1)} %all_to_all.30.forward_ref.refs_0_), channel_id=1, source_target_pairs={{0,4},{1,5},{2,6},{3,7},{4,0},{5,1},{6,2},{7,3},{8,12},{9,13},{10,... | collective-permute-start | bytes 786440 | tf_op jit(solution)/shard_map/ppermute | solution.py:390
  53.0 11.1 %collective-permute-start.1 = (bf16[32,32,128]{2,1,0:T(8,128)(2,1)S(1)}, bf16[32,32,128]{2,1,0:T(8,128)(2,1)S(1)}, u32[]{:S(2)}, u32[]{:S(2)}) collective-permute-start(bf16[32,32,128]{2,1,0:T(8,128)(2,1)S(1)} %all_to_all.30.forward_ref.refs_0_), channel_id=1, source_target_pairs={{0,6},{1,7},{2,0},{3,1},{4,2},{5,3},{6,4},{7,5},{8,14},{9,15},{10,... | collective-permute-start | bytes 786440 | tf_op jit(solution)/shard_map/ppermute | solution.py:390
  54.1 9.9 %collective-permute-start = (bf16[32,32,128]{2,1,0:T(8,128)(2,1)S(1)}, bf16[32,32,128]{2,1,0:T(8,128)(2,1)S(1)}, u32[]{:S(2)}, u32[]{:S(2)}) collective-permute-start(bf16[32,32,128]{2,1,0:T(8,128)(2,1)S(1)} %all_to_all.30.forward_ref.refs_0_), channel_id=1, source_target_pairs={{0,2},{1,3},{2,4},{3,5},{4,6},{5,7},{6,0},{7,1},{8,10},{9,11},{10,... | collective-permute-start | bytes 786440 | tf_op jit(solution)/shard_map/ppermute | solution.py:390
  55.0 11.0 %collective-permute-start.3 = (bf16[32,32,128]{2,1,0:T(8,128)(2,1)S(1)}, bf16[32,32,128]{2,1,0:T(8,128)(2,1)}, u32[]{:S(2)}, u32[]{:S(2)}) collective-permute-start(bf16[32,32,128]{2,1,0:T(8,128)(2,1)S(1)} %all_to_all.30.forward_ref.refs_0_), channel_id=1, source_target_pairs={{0,1},{1,0},{2,3},{3,2},{4,5},{5,4},{6,7},{7,6},{8,9},{9,8},{10,11... | collective-permute-start | bytes 786440 | tf_op jit(solution)/shard_map/ppermute | solution.py:402
  60.4 9.4 %copy-start.5 = (bf16[32,32,128]{2,1,0:T(8,128)(2,1)}, bf16[32,32,128]{2,1,0:T(8,128)(2,1)S(1)}, u32[]{:S(2)}) copy-start(bf16[32,32,128]{2,1,0:T(8,128)(2,1)S(1)} %collective-permute-done.2.refs_3_) | copy-start | bytes 786436
  60.4 5.6 %collective-permute-start.6 = (bf16[32,32,128]{2,1,0:T(8,128)(2,1)S(1)}, bf16[32,32,128]{2,1,0:T(8,128)(2,1)}, u32[]{:S(2)}, u32[]{:S(2)}) collective-permute-start(bf16[32,32,128]{2,1,0:T(8,128)(2,1)S(1)} %collective-permute-done.2.refs_3_), channel_id=1, source_target_pairs={{0,1},{1,0},{2,3},{3,2},{4,5},{5,4},{6,7},{7,6},{8,9},{9,8},{10,11... | collective-permute-start | bytes 786440 | tf_op jit(solution)/shard_map/ppermute | solution.py:402
  64.0 5.8 %copy-start.6 = (bf16[32,32,128]{2,1,0:T(8,128)(2,1)}, bf16[32,32,128]{2,1,0:T(8,128)(2,1)S(1)}, u32[]{:S(2)}) copy-start(bf16[32,32,128]{2,1,0:T(8,128)(2,1)S(1)} %collective-permute-done.1.refs_2_) | copy-start | bytes 786436
  64.0 2.0 %collective-permute-start.5 = (bf16[32,32,128]{2,1,0:T(8,128)(2,1)S(1)}, bf16[32,32,128]{2,1,0:T(8,128)(2,1)}, u32[]{:S(2)}, u32[]{:S(2)}) collective-permute-start(bf16[32,32,128]{2,1,0:T(8,128)(2,1)S(1)} %collective-permute-done.1.refs_2_), channel_id=1, source_target_pairs={{0,1},{1,0},{2,3},{3,2},{4,5},{5,4},{6,7},{7,6},{8,9},{9,8},{10,11... | collective-permute-start | bytes 786440 | tf_op jit(solution)/shard_map/ppermute | solution.py:402
  64.0 5.8 %copy-start.7 = (bf16[32,32,128]{2,1,0:T(8,128)(2,1)}, bf16[32,32,128]{2,1,0:T(8,128)(2,1)S(1)}, u32[]{:S(2)}) copy-start(bf16[32,32,128]{2,1,0:T(8,128)(2,1)S(1)} %collective-permute-done.refs_1_) | copy-start | bytes 786436
  64.1 2.0 %collective-permute-start.4 = (bf16[32,32,128]{2,1,0:T(8,128)(2,1)S(1)}, bf16[32,32,128]{2,1,0:T(8,128)(2,1)}, u32[]{:S(2)}, u32[]{:S(2)}) collective-permute-start(bf16[32,32,128]{2,1,0:T(8,128)(2,1)S(1)} %collective-permute-done.refs_1_), channel_id=1, source_target_pairs={{0,1},{1,0},{2,3},{3,2},{4,5},{5,4},{6,7},{7,6},{8,9},{9,8},{10,11... | collective-permute-start | bytes 786440 | tf_op jit(solution)/shard_map/ppermute | solution.py:402
  64.6 1.4 collective-permute-start.7
  66.1 6.7 %collective-permute-start.10 = (f32[32,128]{1,0:T(8,128)S(1)}, f32[32,128]{1,0:T(8,128)S(1)}, u32[]{:S(2)}, u32[]{:S(2)}) collective-permute-start(f32[32,128]{1,0:T(8,128)S(1)} %add.3.a_ref), channel_id=1, source_target_pairs={{0,4},{1,5},{2,6},{3,7},{4,0},{5,1},{6,2},{7,3},{8,12},{9,13},{10,... | collective-permute-start | bytes 49160 | tf_op jit(solution)/shard_map/ppermute | solution.py:405
  67.8 5.0 %collective-permute-start.9 = (f32[32,128]{1,0:T(8,128)S(1)}, f32[32,128]{1,0:T(8,128)S(1)}, u32[]{:S(2)}, u32[]{:S(2)}) collective-permute-start(f32[32,128]{1,0:T(8,128)S(1)} %add.3.a_ref), channel_id=1, source_target_pairs={{0,6},{1,7},{2,0},{3,1},{4,2},{5,3},{6,4},{7,5},{8,14},{9,15},{10,... | collective-permute-start | bytes 49160 | tf_op jit(solution)/shard_map/ppermute | solution.py:405
  69.3 4.9 %collective-permute-start.8 = (f32[32,128]{1,0:T(8,128)S(1)}, f32[32,128]{1,0:T(8,128)S(1)}, u32[]{:S(2)}, u32[]{:S(2)}) collective-permute-start(f32[32,128]{1,0:T(8,128)S(1)} %add.3.a_ref), channel_id=1, source_target_pairs={{0,2},{1,3},{2,4},{3,5},{4,6},{5,7},{6,0},{7,1},{8,10},{9,11},{10,... | collective-permute-start | bytes 49160 | tf_op jit(solution)/shard_map/ppermute | solution.py:405
  74.3 4.5 %collective-permute-start.14 = (bf16[4,2,128,512]{3,2,1,0:T(8,128)(2,1)S(1)}, bf16[4,2,128,512]{3,2,1,0:T(8,128)(2,1)S(1)}, u32[]{:S(2)}, u32[]{:S(2)}) collective-permute-start(bf16[4,2,128,512]{3,2,1,0:T(8,128)(2,1)S(1)} %get-tuple-element.66), channel_id=1, source_target_pairs={{0,1},{1,0},{2,3},{3,2},{4,5},{5,4},{6,7},{7,6},{8,9},{9,8},{10,11... | collective-permute-start | bytes 3145736 | tf_op jit(solution)/shard_map/ppermute | solution.py:426
  74.3 5.4 %collective-permute-start.13 = (bf16[16,128]{1,0:T(8,128)(2,1)S(1)}, bf16[16,128]{1,0:T(8,128)(2,1)S(1)}, u32[]{:S(2)}, u32[]{:S(2)}) collective-permute-start(bf16[16,128]{1,0:T(8,128)(2,1)S(1)} %shard_map.92.refs_0_), channel_id=1, source_target_pairs={{0,192},{8,200},{16,208},{24,216},{32,224},{40,232},{48,240},{56,2... | collective-permute-start | bytes 12296 | tf_op jit(solution)/shard_map/ppermute | solution.py:434
  77.1 5.1 %collective-permute-start.12 = (bf16[16,128]{1,0:T(8,128)(2,1)S(1)}, bf16[16,128]{1,0:T(8,128)(2,1)S(1)}, u32[]{:S(2)}, u32[]{:S(2)}) collective-permute-start(bf16[16,128]{1,0:T(8,128)(2,1)S(1)} %shard_map.92.refs_0_), channel_id=1, source_target_pairs={{0,128},{8,136},{16,144},{24,152},{32,160},{40,168},{48,176},{56,1... | collective-permute-start | bytes 12296 | tf_op jit(solution)/shard_map/ppermute | solution.py:434
  77.9 4.8 %collective-permute-start.11 = (bf16[16,128]{1,0:T(8,128)(2,1)S(1)}, bf16[16,128]{1,0:T(8,128)(2,1)S(1)}, u32[]{:S(2)}, u32[]{:S(2)}) collective-permute-start(bf16[16,128]{1,0:T(8,128)(2,1)S(1)} %shard_map.92.refs_0_), channel_id=1, source_target_pairs={{0,64},{8,72},{16,80},{24,88},{32,96},{40,104},{48,112},{56,120},{... | collective-permute-start | bytes 12296 | tf_op jit(solution)/shard_map/ppermute | solution.py:434
  83.4 14.8 %all-to-all-start.3 = ((bf16[8,64,128]{2,1,0:T(8,128)(2,1)}), bf16[8,64,128]{2,1,0:T(8,128)(2,1)S(1)}, u32[]{:S(2)}, u32[]{:S(2)}) async-start(bf16[8,64,128]{2,1,0:T(8,128)(2,1)} %shard_map.94), calls=%async_computation.3 | async-start | bytes 262144 | tf_op jit(solution)/shard_map/all_to_all | solution.py:438
  90.6 12.3 %collective-permute-start.15 = (bf16[2,128,512]{2,1,0:T(8,128)(2,1)}, bf16[2,128,512]{2,1,0:T(8,128)(2,1)S(1)}, u32[]{:S(2)}, u32[]{:S(2)}) collective-permute-start(bf16[2,128,512]{2,1,0:T(8,128)(2,1)} %get-tuple-element.72), channel_id=1, source_target_pairs={{0,2},{1,3},{2,4},{3,5},{4,6},{5,7},{6,0},{7,1},{8,10},{9,11},{10,... | collective-permute-start | bytes 786440 | tf_op jit(solution)/shard_map/ppermute | solution.py:436
  92.5 13.7 %collective-permute-start.16 = (bf16[2,128,512]{2,1,0:T(8,128)(2,1)}, bf16[2,128,512]{2,1,0:T(8,128)(2,1)S(1)}, u32[]{:S(2)}, u32[]{:S(2)}) collective-permute-start(bf16[2,128,512]{2,1,0:T(8,128)(2,1)} %get-tuple-element.73), channel_id=1, source_target_pairs={{0,6},{1,7},{2,0},{3,1},{4,2},{5,3},{6,4},{7,5},{8,14},{9,15},{10,... | collective-permute-start | bytes 786440 | tf_op jit(solution)/shard_map/ppermute | solution.py:436
  96.4 11.7 %collective-permute-start.17 = (bf16[2,128,512]{2,1,0:T(8,128)(2,1)S(1)}, bf16[2,128,512]{2,1,0:T(8,128)(2,1)S(1)}, u32[]{:S(2)}, u32[]{:S(2)}) collective-permute-start(bf16[2,128,512]{2,1,0:T(8,128)(2,1)S(1)} %get-tuple-element.74), channel_id=1, source_target_pairs={{0,4},{1,5},{2,6},{3,7},{4,0},{5,1},{6,2},{7,3},{8,12},{9,13},{10,... | collective-permute-start | bytes 786440 | tf_op jit(solution)/shard_map/ppermute | solution.py:436
  99.0 9.0 %collective-permute-start.18 = (bf16[512,128]{1,0:T(8,128)(2,1)S(1)}, bf16[512,128]{1,0:T(8,128)(2,1)S(1)}, u32[]{:S(2)}, u32[]{:S(2)}) collective-permute-start(bf16[512,128]{1,0:T(8,128)(2,1)S(1)} %get-tuple-element.79.mine_ref), channel_id=1, source_target_pairs={{0,1},{1,0},{2,3},{3,2},{4,5},{5,4},{6,7},{7,6},{8,9},{9,8},{10,11... | collective-permute-start | bytes 393224 | tf_op jit(solution)/shard_map/ppermute | solution.py:453
  99.1 1.3 collective-permute-start.19
